TPU v7x, 512 devices: a whole 4x8x8 slice. The times are simulated.
512 devices in a mesh: seq: 128 (over x, y_hi, z, core), tp: 4 (over y_lo).
Axes of the slice: x: 4, y: 8 (y_hi: 2, y_lo: 4; y = y_hi * 4 + y_lo), z: 8, core: 2. Of those that a mesh axis runs over, the one named last changes fastest.
Arguments:
- tokens: bfloat16 [16384, 2560], P('seq', 'tp'), may hold values from -6 to 6
- seg_ids: int32 [16384], P('seq'), may hold values from 0 to 31, never falling along the last dimension, each value on 1 to 4096 neighbouring positions
- norm_gain: bfloat16 [2560], replicated, may hold values from 0.099609375 to 1.8984375
- w_query: bfloat16 [2560, 2048], P('seq', 'tp'), may hold values from -3 to 3
- w_keyval: bfloat16 [2560, 512], P('seq'), may hold values from -1 to 1
- w_out: bfloat16 [2048, 2560], P('tp', 'seq'), may hold values from -0.125 to 0.125
Outputs:
- hidden: bfloat16 [16384, 2560], P('seq', 'tp')
- kv_cache: bfloat16 [16384, 512], P('seq')
Inputs may be any that keep to these rules, and one draw needn't show every extreme that they name: `seg_ids`: ids never fall along the stream; each of the 32 requests holds 1 to 4096 consecutive tokens, one exactly 4096.
All inputs are finite; a program needn't handle non-finite values.
Results may differ from a plain program's by a relative error of at most 0.0085.
Values may be sent and summed in bfloat16 or wider, within the bound.
No kernel may reach another device: no remote copies, remote signals or barrier semaphores. Data moves between devices by JAX's collectives and lax.ppermute only.
A program may use at most 64 MiB of HBM per device.

v0:
```python
import jax
import jax.numpy as jnp
from jax import lax
from jax.sharding import Mesh, PartitionSpec as P


HD = 256
WINDOW = 2048
SEGS = 32
GRID = (4, 2, 8, 2)
SEQ = ("x", "yh", "z", "c")


def rms_norm(values, gain):
    wide = values.astype(jnp.float32)
    scaled = wide * lax.rsqrt(jnp.mean(wide * wide, axis=-1, keepdims=True) + 1e-06)
    return (scaled * gain.astype(jnp.float32)).astype(jnp.bfloat16)


def angles(positions):
    quarter = HD // 4
    freq = 10000.0 ** (-jnp.arange(quarter, dtype=jnp.float32) / quarter)
    angle = positions[:, None] * freq
    return jnp.cos(angle), jnp.sin(angle)


def rotate(tensor, cosine, sine):
    quarter = HD // 4
    first = tensor[:, :quarter]
    second = tensor[:, quarter : 2 * quarter]
    return jnp.concatenate(
        [
            first * cosine - second * sine,
            second * cosine + first * sine,
            tensor[:, 2 * quarter :],
        ],
        axis=-1,
    )


def after(value, *others):
    return lax.optimization_barrier((value, *others))[0]


def spread(slab, axes, count):
    copies = jnp.broadcast_to(slab[None], (count, *slab.shape))
    return lax.all_to_all(copies, axes, 0, 0, tiled=True)


def natural_to_gathered(per, rows, ny):
    nat = lax.broadcasted_iota(jnp.int32, (per, per), 0)
    gat = lax.broadcasted_iota(jnp.int32, (per, per), 1)
    place, row = gat // rows, gat % rows
    source = ((place % ny) * (per // rows // ny) + place // ny) * rows + row
    return (nat == source).astype(jnp.bfloat16)


def per_device(tokens, seg_ids, norm_gain, w_query, w_keyval, w_out):
    nx, ny, nz, nc = GRID
    tok, shard = tokens.shape
    rows = w_query.shape[0]
    cols = w_query.shape[1]
    ix, iy, iz, ic = (lax.axis_index(a) for a in SEQ)
    my_block = ix * ny + iy
    my_index = (my_block * nz + iz) * nc + ic
    bf = jnp.bfloat16

    qo_own = jnp.concatenate([w_query, w_out.T], axis=0)
    qo_other = lax.ppermute(qo_own, "yh", [(0, 1), (1, 0)])
    low = jnp.where(iy == 0, qo_own, qo_other)
    high = jnp.where(iy == 0, qo_other, qo_own)
    qo_send = jnp.concatenate([low[:rows], high[:rows], low[rows:], high[rows:]], axis=0)
    qo_all = lax.all_gather(qo_send, ("x", "z", "c"), axis=0, tiled=False)
    part = ny * rows

    it = lax.axis_index("tp")
    share = 2 * HD // nx
    ids = jnp.pad(seg_ids.astype(bf)[None, :], ((0, 3), (0, 0)))
    kv_slab = jnp.concatenate([lax.dynamic_slice_in_dim(w_keyval, it * share, share, 1), ids], axis=0)
    kv_all = spread(after(kv_slab, qo_send), SEQ, nx * ny * nz * nc)

    others = [lax.ppermute(tokens, "tp", [(i, (i + k) % nx) for i in range(nx)]) for k in range(1, nx)]
    shares = [tokens, *others]
    groups = []
    for g in range(nx):
        took = (it - g) % nx
        group = shares[nx - 1]
        for k in range(nx - 1):
            group = jnp.where(took == k, shares[k], group)
        groups.append(group)
    normed = rms_norm(jnp.concatenate(groups, axis=1), norm_gain)
    perm = natural_to_gathered(shard, rows, ny)
    reordered = jnp.concatenate(
        [
            jnp.dot(normed[:, g * shard : (g + 1) * shard], perm, preferred_element_type=jnp.float32).astype(bf)
            for g in range(nx)
        ],
        axis=1,
    )
    kv_all, normed, reordered, perm = lax.optimization_barrier((kv_all, normed, reordered, perm))

    all_ids = kv_all[:, rows].astype(jnp.int32)
    labels = jnp.arange(SEGS, dtype=jnp.int32)
    starts = jnp.sum((all_ids.reshape(-1)[None, :] < labels[:, None]).astype(jnp.int32), axis=1)
    own_start = jnp.sum(jnp.where(seg_ids[:, None] == labels[None, :], starts[None, :], 0), axis=1)
    token_index = my_index * tok + jnp.arange(tok, dtype=jnp.int32)
    cosine, sine = angles((token_index - own_start).astype(jnp.float32))

    kv_raw = jnp.dot(
        normed, kv_all[:, :rows].reshape(nx * shard, share), preferred_element_type=jnp.float32
    )
    turned = rotate(kv_raw, cosine, sine)
    kv_share = jnp.where(it == 0, turned, kv_raw).astype(bf)
    kv_cache = jnp.concatenate(list(spread(kv_share, "tp", nx)), axis=1)

    block = nz * nc
    devices = nx * ny * block
    before = lax.ppermute(kv_cache, SEQ, [(i, i + block) for i in range(devices - block)])
    chips = jnp.arange(nz, dtype=jnp.int32)
    to_send = jnp.where((chips > iz)[:, None, None], kv_cache[None], before[None])
    mine = lax.all_to_all(to_send, "z", 0, 0, tiled=True)
    at_self = (chips == iz)[:, None, None] & (ic == 0)
    partner = lax.ppermute(jnp.where(at_self, kv_cache[None], mine), "c", [(0, 1), (1, 0)])
    block_of_mine = my_block - (chips >= iz).astype(jnp.int32)
    block_of_partner = my_block - jnp.where(ic == 1, chips > iz, chips >= iz).astype(jnp.int32)
    first_of_mine = ((block_of_mine * nz + chips) * nc + ic) * tok
    first_of_partner = ((block_of_partner * nz + chips) * nc + 1 - ic) * tok
    firsts = jnp.concatenate([first_of_mine, first_of_partner, my_index[None] * tok])
    key_index = (firsts[:, None] + jnp.arange(tok, dtype=jnp.int32)[None, :]).reshape(-1)
    window_kv = jnp.concatenate(
        [mine.reshape(nz * tok, 2 * HD), partner.reshape(nz * tok, 2 * HD), kv_cache], axis=0
    )

    query_raw = jnp.dot(
        reordered,
        qo_all[:, :part].reshape(nx * shard, cols),
        preferred_element_type=jnp.float32,
    )
    heads = [
        rotate(query_raw[:, h * HD : (h + 1) * HD], cosine, sine).astype(bf) for h in range(cols // HD)
    ]
    live = (key_index[None, :] <= token_index[:, None]) & (key_index[None, :] >= own_start[:, None])
    live = live & (token_index[:, None] - key_index[None, :] < WINDOW)
    all_keys = window_kv[:, :HD]
    all_values = window_kv[:, HD:]
    head_outputs = []
    for queries in heads:
        scores = lax.dot_general(
            queries, all_keys, (((1,), (1,)), ((), ())), preferred_element_type=jnp.float32
        ) * HD ** (-0.5)
        scores = jnp.where(live, scores, -1e30)
        peak = jnp.max(scores, axis=1, keepdims=True)
        powered = jnp.exp(scores - peak)
        weights = (powered / jnp.sum(powered, axis=1, keepdims=True)).astype(bf)
        head_outputs.append(
            jnp.dot(weights, all_values, preferred_element_type=jnp.float32).astype(bf)
        )
    attended = jnp.concatenate(head_outputs, axis=1)

    partial = lax.dot_general(
        attended,
        qo_all[:, part:].reshape(nx * shard, cols),
        (((1,), (1,)), ((), ())),
        preferred_element_type=jnp.float32,
    ).astype(bf)
    pieces = jnp.stack([partial[:, g * shard : (g + 1) * shard] for g in range(nx)])
    received = lax.all_to_all(pieces, "tp", 0, 0, tiled=True)
    summed = jnp.zeros((tok, shard), jnp.float32)
    for g in range(nx):
        summed = summed + lax.dot_general(
            received[g], perm, (((1,), (1,)), ((), ())), preferred_element_type=jnp.float32
        )
    hidden = (tokens.astype(jnp.float32) + summed).astype(bf)
    return (hidden, kv_cache)


def solution(mesh):
    fine = Mesh(mesh.devices.reshape(*GRID, mesh.shape["tp"]), (*SEQ, "tp"))
    in_specs = (P(SEQ, "tp"), P(SEQ), P(), P(SEQ, "tp"), P(SEQ, None), P("tp", SEQ))
    out_specs = (P(SEQ, "tp"), P(SEQ, None))
    return jax.shard_map(per_device, mesh=fine, in_specs=in_specs, out_specs=out_specs, check_vma=False)
```

profile of v0, /device:TPU:2, one launch (start us, length us, event | category | flops | bytes accessed | tf_op | source)
XLA Modules:
  0.0 194.6 jit_solution(6997838407716693688)
XLA Ops:
  7.2 0.0 copy-start
  7.2 0.0 all-gather.3.cloned.1.call-start
  7.2 3.5 %collective-permute-start.2 = (bf16[128,640]{1,0:T(8,128)(2,1)}, bf16[128,640]{1,0:T(8,128)(2,1)S(1)}, u32[]{:S(2)}, u32[]{:S(2)}) collective-permute-start(bf16[128,640]{1,0:T(8,128)(2,1)} %param.6), channel_id=1, source_target_pairs={{0,1},{1,2},{2,3},{3,0},{4,5},{5,6},{6,7},{7,4},{8,9},{9,10},{10,1... | collective-permute-start | bytes 491528 | tf_op jit(solution)/shard_map/ppermute | solution.py:82
  10.7 4.5 %collective-permute-start.1 = (bf16[128,640]{1,0:T(8,128)(2,1)}, bf16[128,640]{1,0:T(8,128)(2,1)S(1)}, u32[]{:S(2)}, u32[]{:S(2)}) collective-permute-start(bf16[128,640]{1,0:T(8,128)(2,1)} %param.6), channel_id=1, source_target_pairs={{0,2},{1,3},{2,0},{3,1},{4,6},{5,7},{6,4},{7,5},{8,10},{9,11},{10,... | collective-permute-start | bytes 491528 | tf_op jit(solution)/shard_map/ppermute | solution.py:82
  15.2 3.3 %collective-permute-start.3 = (bf16[128,640]{1,0:T(8,128)(2,1)}, bf16[128,640]{1,0:T(8,128)(2,1)S(1)}, u32[]{:S(2)}, u32[]{:S(2)}) collective-permute-start(bf16[128,640]{1,0:T(8,128)(2,1)} %param.6), channel_id=1, source_target_pairs={{0,3},{1,0},{2,1},{3,2},{4,7},{5,4},{6,5},{7,6},{8,11},{9,8},{10,9... | collective-permute-start | bytes 491528 | tf_op jit(solution)/shard_map/ppermute | solution.py:82
  18.5 0.8 pad_maximum_fusion.5
  19.3 6.1 %collective-permute-start = (bf16[40,512]{1,0:T(8,128)(2,1)S(1)}, bf16[40,512]{1,0:T(8,128)(2,1)S(1)}, u32[]{:S(2)}, u32[]{:S(2)}) collective-permute-start(bf16[40,512]{1,0:T(8,128)(2,1)S(1)} %pad_maximum_fusion.5), channel_id=1, source_target_pairs={{0,64},{64,0},{1,65},{65,1},{2,66},{66,2},{3,67},{67,3},{4,68},{68... | collective-permute-start | bytes 122888 | tf_op jit(solution)/shard_map/ppermute | solution.py:69
  25.4 3.8 %collective-permute-done = bf16[40,512]{1,0:T(8,128)(2,1)S(1)} collective-permute-done((bf16[40,512]{1,0:T(8,128)(2,1)S(1)}, bf16[40,512]{1,0:T(8,128)(2,1)S(1)}, u32[]{:S(2)}, u32[]{:S(2)}) %collective-permute-start) | collective-permute-done | bytes 40992 | tf_op jit(solution)/shard_map/ppermute | solution.py:69
  29.2 0.8 broadcast_select_fusion.3
  30.0 0.7 pad_maximum_fusion.4
  30.7 0.0 all-gather.3.cloned.1.call-update
  30.7 0.7 convert_bitcast_fusion
  31.4 0.3 fusion.86
  31.8 1.0 broadcast_in_dim.61
  32.9 18.3 %all-to-all-start = ((bf16[128,24,128]{2,1,0:T(8,128)(2,1)}), bf16[128,24,128]{2,1,0:T(8,128)(2,1)S(1)}, u32[]{:S(2)}, u32[]{:S(2)}) async-start(bf16[128,24,128]{2,1,0:T(8,128)(2,1)} %broadcast_in_dim.61), calls=%async_computation | async-start | bytes 1572864 | tf_op jit(solution)/shard_map/all_to_all | solution.py:47
  51.2 0.0 collective-permute-done.1
  51.2 0.1 select_select_fusion.4
  51.3 0.2 fusion.11
  51.5 0.2 fusion.13
  51.8 0.5 convolution_convert_fusion.1
  52.3 0.5 convolution_convert_fusion.2
  52.8 0.5 convolution_convert_fusion.3
  53.3 0.5 convolution_convert_fusion.4
  53.8 0.0 copy-start.5
  53.8 0.1 pad_maximum_fusion.1
  53.9 21.0 %all-to-all-done = bf16[128,24,128]{2,1,0:T(8,128)(2,1)S(1)} async-done(((bf16[128,24,128]{2,1,0:T(8,128)(2,1)}), bf16[128,24,128]{2,1,0:T(8,128)(2,1)S(1)}, u32[]{:S(2)}, u32[]{:S(2)}) %all-to-all-start) | async-done | bytes 786464 | tf_op jit(solution)/shard_map/all_to_all | solution.py:47
  74.8 1.0 reshape.90
  75.9 0.1 slice_convert_fusion
  76.0 0.3 convert_reduce_fusion
  76.3 0.1 select_reduce_fusion
  76.4 1.4 fusion.98
  77.8 0.3 fusion.51
  78.1 0.1 fusion.62
  78.2 14.2 %all_to_all.20 = bf16[4,128,128]{2,1,0:T(8,128)(2,1)S(1)} all-to-all(bf16[4,128,128]{2,1,0:T(8,128)(2,1)S(1)} %broadcast_in_dim.65), channel_id=1, replica_groups=mesh['x'=4,'yh'=2,'z'=8,'c'=2,'tp'=4] {'tp'}, dimensions={0} | all-to-all | bytes 262144 | tf_op jit(solution)/shard_map/all_to_all | solution.py:47
  92.5 0.0 copy-start.2
  92.5 2.1 %collective-permute-start.4 = (bf16[128,512]{1,0:T(8,128)(2,1)S(1)}, bf16[128,512]{1,0:T(8,128)(2,1)S(1)}, u32[]{:S(2)}, u32[]{:S(2)}) collective-permute-start(bf16[128,512]{1,0:T(8,128)(2,1)S(1)} %pad_maximum_fusion.3), channel_id=1, source_target_pairs={{0,64},{4,68},{8,72},{12,76},{16,80},{20,84},{24,88},{28,92},{32,9... | collective-permute-start | bytes 393224 | tf_op jit(solution)/shard_map/ppermute | solution.py:118
  94.6 10.3 %collective-permute-done.4 = bf16[128,512]{1,0:T(8,128)(2,1)S(1)} collective-permute-done((bf16[128,512]{1,0:T(8,128)(2,1)S(1)}, bf16[128,512]{1,0:T(8,128)(2,1)S(1)}, u32[]{:S(2)}, u32[]{:S(2)}) %collective-permute-start.4) | collective-permute-done | bytes 131104 | tf_op jit(solution)/shard_map/ppermute | solution.py:118
  104.9 1.1 broadcast_select_fusion.1
  106.1 3.6 %all-to-all-start.2 = ((bf16[8,128,512]{2,1,0:T(8,128)(2,1)}), bf16[8,128,512]{2,1,0:T(8,128)(2,1)S(1)}, u32[]{:S(2)}, u32[]{:S(2)}) async-start(bf16[8,128,512]{2,1,0:T(8,128)(2,1)} %broadcast_select_fusion.1), calls=%async_computation.2 | async-start | bytes 2097152 | tf_op jit(solution)/shard_map/all_to_all | solution.py:121
  109.7 33.9 %all-to-all-done.2 = bf16[8,128,512]{2,1,0:T(8,128)(2,1)S(1)} async-done(((bf16[8,128,512]{2,1,0:T(8,128)(2,1)}), bf16[8,128,512]{2,1,0:T(8,128)(2,1)S(1)}, u32[]{:S(2)}, u32[]{:S(2)}) %all-to-all-start.2) | async-done | bytes 1048608 | tf_op jit(solution)/shard_map/all_to_all | solution.py:121
  143.5 1.1 broadcast_select_fusion
  144.7 2.1 %collective-permute-start.5 = (bf16[8,128,512]{2,1,0:T(8,128)(2,1)}, bf16[8,128,512]{2,1,0:T(8,128)(2,1)}, u32[]{:S(2)}, u32[]{:S(2)}) collective-permute-start(bf16[8,128,512]{2,1,0:T(8,128)(2,1)} %broadcast_select_fusion), channel_id=1, source_target_pairs={{0,4},{4,0},{1,5},{5,1},{2,6},{6,2},{3,7},{7,3},{8,12},{12,8},{9,1... | collective-permute-start | bytes 3145736 | tf_op jit(solution)/shard_map/ppermute | solution.py:123
  146.8 0.1 pad_add_fusion
  146.9 0.1 add_bitcast_fusion
  147.0 2.6 %collective-permute-done.5 = bf16[8,128,512]{2,1,0:T(8,128)(2,1)} collective-permute-done((bf16[8,128,512]{2,1,0:T(8,128)(2,1)}, bf16[8,128,512]{2,1,0:T(8,128)(2,1)}, u32[]{:S(2)}, u32[]{:S(2)}) %collective-permute-start.5) | collective-permute-done | bytes 1048608 | tf_op jit(solution)/shard_map/ppermute | solution.py:123
  149.6 7.1 %maximum_maximum_fusion = bf16[2176,512]{1,0:T(8,128)(2,1)} fusion(bf16[128,128]{1,0:T(8,128)(2,1)S(1)} %get-tuple-element.29, bf16[128,128]{1,0:T(8,128)(2,1)S(1)} %get-tuple-element.30, bf16[128,128]{1,0:T(8,128)(2,1)S(1)} %get-tuple-element.31, bf16[128,128]{1,0:T(8,128)(2,1)S(1)} %get-tuple-element.28, bf16[1024,512]{1,0:T(8,128)(2,1)} %bitcast.12, ...), kind=kLoop, calls=%fused_computation.13 | loop fusion | flops 13369344 | bytes 4456448 | tf_op jit(solution)/shard_map/concatenate | solution.py:130
  156.7 2.9 %fusion.91 = (bf16[64,40,512]{2,1,0:T(8,128)(2,1)S(1)}, bf16[64,40,512]{2,1,0:T(8,128)(2,1)S(1)}) fusion(bf16[64,80,512]{2,1,0:T(8,128)(2,1)} %bitcast.53), kind=kLoop, calls=%fused_computation.167 | loop fusion | bytes 10485760 | tf_op jit(solution)/shard_map/slice | solution.py:136
  159.6 0.5 fusion.95
  160.1 0.3 fusion.48
  160.4 0.7 copy-done.1
  161.2 0.7 fusion.96
  161.9 0.3 fusion.18
  162.2 0.4 convolution_convert_fusion.5
  162.6 0.7 fusion.97
  163.3 0.3 fusion.17
  163.7 0.4 convolution_convert_fusion.6
  164.1 1.0 convolution_convert_fusion
  165.0 0.1 slice_bitcast_fusion.11
  165.1 0.1 pad_maximum_fusion.2
  165.2 20.4 %all_to_all.21 = bf16[4,128,640]{2,1,0:T(8,128)(2,1)S(1)} all-to-all(bf16[4,128,640]{2,1,0:T(8,128)(2,1)S(1)} %pad_maximum_fusion.2), channel_id=1, replica_groups=mesh['x'=4,'yh'=2,'z'=8,'c'=2,'tp'=4] {'tp'}, dimensions={0} | all-to-all | bytes 1310720 | tf_op jit(solution)/shard_map/all_to_all | solution.py:167
  185.6 0.4 fusion.27
  186.0 0.4 convolution_add_fusion.2
  186.4 0.4 convolution_add_fusion.1
  186.7 1.0 fusion.15
  (30 shorter events, 0.2 us)
Async XLA Ops:
  7.2 18.2 %copy-start = (bf16[20,512]{1,0:T(8,128)(2,1)S(1)}, bf16[20,512]{1,0:T(8,128)(2,1)}, u32[]{:S(2)}) copy-start(bf16[20,512]{1,0:T(8,128)(2,1)} %param.10) | copy-start | bytes 61444
  7.2 24.6 %copy-start.4 = (bf16[2560]{0:T(1024)(128)(2,1)S(1)}, bf16[2560]{0:T(1024)(128)(2,1)}, u32[]{:S(2)}) copy-start(bf16[2560]{0:T(1024)(128)(2,1)} %param.8) | copy-start | bytes 15364
  7.2 149.5 %all-gather.3.cloned.1.call-start = ((), (), s32[]{:S(2)}) async-start(), calls=%async_computation.4 | async-start | bytes 5324800 | tf_op jit(solution)/shard_map/all_gather | solution.py:73
  7.2 43.9 %collective-permute-start.2 = (bf16[128,640]{1,0:T(8,128)(2,1)}, bf16[128,640]{1,0:T(8,128)(2,1)S(1)}, u32[]{:S(2)}, u32[]{:S(2)}) collective-permute-start(bf16[128,640]{1,0:T(8,128)(2,1)} %param.6), channel_id=1, source_target_pairs={{0,1},{1,2},{2,3},{3,0},{4,5},{5,6},{6,7},{7,4},{8,9},{9,10},{10,1... | collective-permute-start | bytes 491528 | tf_op jit(solution)/shard_map/ppermute | solution.py:82
  10.7 40.4 %collective-permute-start.1 = (bf16[128,640]{1,0:T(8,128)(2,1)}, bf16[128,640]{1,0:T(8,128)(2,1)S(1)}, u32[]{:S(2)}, u32[]{:S(2)}) collective-permute-start(bf16[128,640]{1,0:T(8,128)(2,1)} %param.6), channel_id=1, source_target_pairs={{0,2},{1,3},{2,0},{3,1},{4,6},{5,7},{6,4},{7,5},{8,10},{9,11},{10,... | collective-permute-start | bytes 491528 | tf_op jit(solution)/shard_map/ppermute | solution.py:82
  15.2 35.9 %collective-permute-start.3 = (bf16[128,640]{1,0:T(8,128)(2,1)}, bf16[128,640]{1,0:T(8,128)(2,1)S(1)}, u32[]{:S(2)}, u32[]{:S(2)}) collective-permute-start(bf16[128,640]{1,0:T(8,128)(2,1)} %param.6), channel_id=1, source_target_pairs={{0,3},{1,0},{2,1},{3,2},{4,7},{5,4},{6,5},{7,6},{8,11},{9,8},{10,9... | collective-permute-start | bytes 491528 | tf_op jit(solution)/shard_map/ppermute | solution.py:82
  19.3 10.0 %collective-permute-start = (bf16[40,512]{1,0:T(8,128)(2,1)S(1)}, bf16[40,512]{1,0:T(8,128)(2,1)S(1)}, u32[]{:S(2)}, u32[]{:S(2)}) collective-permute-start(bf16[40,512]{1,0:T(8,128)(2,1)S(1)} %pad_maximum_fusion.5), channel_id=1, source_target_pairs={{0,64},{64,0},{1,65},{65,1},{2,66},{66,2},{3,67},{67,3},{4,68},{68... | collective-permute-start | bytes 122888 | tf_op jit(solution)/shard_map/ppermute | solution.py:69
  31.4 19.8 %copy-start.3 = (bf16[128,640]{1,0:T(8,128)(2,1)S(1)}, bf16[128,640]{1,0:T(8,128)(2,1)}, u32[]{:S(2)}) copy-start(bf16[128,640]{1,0:T(8,128)(2,1)} %param.6) | copy-start | bytes 491524
  32.9 42.0 %all-to-all-start = ((bf16[128,24,128]{2,1,0:T(8,128)(2,1)}), bf16[128,24,128]{2,1,0:T(8,128)(2,1)S(1)}, u32[]{:S(2)}, u32[]{:S(2)}) async-start(bf16[128,24,128]{2,1,0:T(8,128)(2,1)} %broadcast_in_dim.61), calls=%async_computation | async-start | bytes 1572864 | tf_op jit(solution)/shard_map/all_to_all | solution.py:47
  53.8 22.5 %copy-start.5 = (s32[128]{0:T(128)S(1)}, s32[128]{0:T(128)}, u32[]{:S(2)}) copy-start(s32[128]{0:T(128)} %param.7) | copy-start | bytes 1540
  92.5 51.1 %copy-start.2 = (bf16[128,512]{1,0:T(8,128)(2,1)}, bf16[128,512]{1,0:T(8,128)(2,1)S(1)}, u32[]{:S(2)}) copy-start(bf16[128,512]{1,0:T(8,128)(2,1)S(1)} %pad_maximum_fusion.3) | copy-start | bytes 393220
  92.5 12.5 %collective-permute-start.4 = (bf16[128,512]{1,0:T(8,128)(2,1)S(1)}, bf16[128,512]{1,0:T(8,128)(2,1)S(1)}, u32[]{:S(2)}, u32[]{:S(2)}) collective-permute-start(bf16[128,512]{1,0:T(8,128)(2,1)S(1)} %pad_maximum_fusion.3), channel_id=1, source_target_pairs={{0,64},{4,68},{8,72},{12,76},{16,80},{20,84},{24,88},{28,92},{32,9... | collective-permute-start | bytes 393224 | tf_op jit(solution)/shard_map/ppermute | solution.py:118
  106.1 37.5 %all-to-all-start.2 = ((bf16[8,128,512]{2,1,0:T(8,128)(2,1)}), bf16[8,128,512]{2,1,0:T(8,128)(2,1)S(1)}, u32[]{:S(2)}, u32[]{:S(2)}) async-start(bf16[8,128,512]{2,1,0:T(8,128)(2,1)} %broadcast_select_fusion.1), calls=%async_computation.2 | async-start | bytes 2097152 | tf_op jit(solution)/shard_map/all_to_all | solution.py:121
  144.7 4.9 %collective-permute-start.5 = (bf16[8,128,512]{2,1,0:T(8,128)(2,1)}, bf16[8,128,512]{2,1,0:T(8,128)(2,1)}, u32[]{:S(2)}, u32[]{:S(2)}) collective-permute-start(bf16[8,128,512]{2,1,0:T(8,128)(2,1)} %broadcast_select_fusion), channel_id=1, source_target_pairs={{0,4},{4,0},{1,5},{5,1},{2,6},{6,2},{3,7},{7,3},{8,12},{12,8},{9,1... | collective-permute-start | bytes 3145736 | tf_op jit(solution)/shard_map/ppermute | solution.py:123
  159.6 1.6 copy-start.1
Sparse Core Ops, SparseCore 0:
  30.9 106.9 all-gather.2
where the time goes:
time: 195 us
  waiting for transfers between devices  71.6 us (37%)
  starting transfers between devices  43.3 us (22%)
  blocking collectives  34.6 us (18%)
  other arithmetic  15.4 us (8%)
  between operations  14.6 us (7%)
  matrix products  9.22 us (5%)
  local copies, waits for them, and re-layouts  5.83 us (3%)
    all_to_all x1, waiting for transfers between devices, per_device(): mine = lax.all_to_all(to_send, 'z', 0, 0, tiled=True)  33.9 us
    all_to_all x1, waiting for transfers between devices, spread(): return lax.all_to_all(copies, axes, 0, 0, tiled=True)  21 us
    all_to_all x1, blocking collectives, per_device(): received = lax.all_to_all(pieces, 'tp', 0, 0, tiled=True)  20.4 us
    all_to_all x1, starting transfers between devices, spread(): return lax.all_to_all(copies, axes, 0, 0, tiled=True)  18.3 us
    all_to_all x1, blocking collectives, spread(): return lax.all_to_all(copies, axes, 0, 0, tiled=True)  14.2 us
    ppermute x3, starting transfers between devices, per_device(): lax.ppermute(tokens, 'tp', [(i, (i + k) % nx) for i in range(nx)])  11.2 us
    ppermute x1, waiting for transfers between devices, per_device(): lax.ppermute(kv_cache, SEQ, [(i, i + block) for i in range(devices - bloc...  10.3 us
    concatenate x1, other arithmetic, per_device(): jnp.concatenate([mine.reshape(nz * tok, 2 * HD), partner.reshape(nz * tok...  7.11 us
  transfers between devices with their start and end apart: 9, of which 5 were waited for; matrix products, arithmetic and copies ran while one was open for 10% of the time, Pallas kernels for 0%

commit v1 on v0

v1 whole, which is shorter than its diff:
```python
import jax
import jax.numpy as jnp
from jax import lax
from jax.experimental import pallas as pl
from jax.experimental.pallas import tpu as pltpu
from jax.sharding import Mesh, PartitionSpec as P


HD = 256
WINDOW = 2048
SEGS = 32
GRID = (4, 2, 8, 2)
SEQ = ("x", "yh", "z", "c")


def rms_norm(values, gain):
    wide = values.astype(jnp.float32)
    scaled = wide * lax.rsqrt(jnp.mean(wide * wide, axis=-1, keepdims=True) + 1e-06)
    return (scaled * gain.astype(jnp.float32)).astype(jnp.bfloat16)


def angles(positions):
    quarter = HD // 4
    freq = 10000.0 ** (-jnp.arange(quarter, dtype=jnp.float32) / quarter)
    angle = positions[:, None] * freq
    cosine, sine = jnp.cos(angle), jnp.sin(angle)
    return jnp.concatenate([cosine, cosine], axis=1), jnp.concatenate([-sine, sine], axis=1)


def after(value, *others):
    return lax.optimization_barrier((value, *others))[0]


def spread(slab, axes, count):
    copies = jnp.broadcast_to(slab[None], (count, *slab.shape))
    return lax.all_to_all(copies, axes, 0, 0, tiled=True)


def natural_to_gathered(per, rows, ny, nz):
    nat = lax.broadcasted_iota(jnp.int32, (per, per), 0)
    gat = lax.broadcasted_iota(jnp.int32, (per, per), 1)
    half = per // 2
    core, rest = gat // half, gat % half
    place, row = rest // rows, rest % rows
    source = (((place % ny) * nz + place // ny) * 2 + core) * rows + row
    return (nat == source).astype(jnp.bfloat16)


def queries_kernel(normed_ref, cosine_ref, sine_ref, qo_ref, out_ref, weights_ref, sem):
    groups, part, cols = weights_ref.shape
    copy = pltpu.make_async_copy(qo_ref.at[:, pl.ds(0, part), :], weights_ref, sem)
    copy.start()
    copy.wait()
    raw = jnp.dot(normed_ref[0], weights_ref[0], preferred_element_type=jnp.float32)
    for g in range(1, groups):
        raw = raw + jnp.dot(normed_ref[g], weights_ref[g], preferred_element_type=jnp.float32)
    half = HD // 2
    for h in range(cols // HD):
        lo = raw[:, h * HD : h * HD + half]
        turned = lo * cosine_ref[...] + pltpu.roll(lo, half // 2, 1) * sine_ref[...]
        out_ref[:, h * HD : h * HD + half] = turned.astype(out_ref.dtype)
        out_ref[:, h * HD + half : (h + 1) * HD] = raw[:, h * HD + half : (h + 1) * HD].astype(
            out_ref.dtype
        )


def attend_kernel(
    queries_ref, mine_ref, partner_ref, keys_at_ref, token_ref, start_ref, qo_ref, out_ref, weights_ref, sem
):
    groups, part, cols = weights_ref.shape
    copy = pltpu.make_async_copy(qo_ref.at[:, pl.ds(part, part), :], weights_ref, sem)
    copy.start()
    flat = lambda ref, t: ref[t].reshape(ref.shape[1] * ref.shape[2], ref.shape[3])
    whole = lambda t: jnp.concatenate([flat(mine_ref, t), flat(partner_ref, t)], axis=0)
    keys = jnp.concatenate([whole(0), whole(1)], axis=1)
    values = jnp.concatenate([whole(2), whole(3)], axis=1)
    at = keys_at_ref[...]
    token = token_ref[...]
    live = (at <= token) & (at >= start_ref[...]) & (token - at < WINDOW)
    heads = []
    for h in range(cols // HD):
        scores = lax.dot_general(
            queries_ref[:, h * HD : (h + 1) * HD],
            keys,
            (((1,), (1,)), ((), ())),
            preferred_element_type=jnp.float32,
        ) * HD ** (-0.5)
        scores = jnp.where(live, scores, -1e30)
        powered = jnp.exp(scores - jnp.max(scores, axis=1, keepdims=True))
        weights = (powered / jnp.sum(powered, axis=1, keepdims=True)).astype(jnp.bfloat16)
        heads.append(
            jnp.dot(weights, values, preferred_element_type=jnp.float32).astype(jnp.bfloat16)
        )
    attended = jnp.concatenate(heads, axis=1)
    copy.wait()
    for g in range(groups // 2):
        rows = jnp.concatenate([weights_ref[2 * g], weights_ref[2 * g + 1]], axis=0)
        out_ref[g] = lax.dot_general(
            attended, rows, (((1,), (1,)), ((), ())), preferred_element_type=jnp.float32
        ).astype(out_ref.dtype)


def per_device(tokens, seg_ids, norm_gain, w_query, w_keyval, w_out):
    nx, ny, nz, nc = GRID
    tok, shard = tokens.shape
    rows = w_query.shape[0]
    cols = w_query.shape[1]
    ix, iy, iz, ic = (lax.axis_index(a) for a in SEQ)
    it = lax.axis_index("tp")
    my_block = ix * ny + iy
    my_index = (my_block * nz + iz) * nc + ic
    bf = jnp.bfloat16
    both = [(0, 1), (1, 0)]

    share = 2 * HD // nx
    ids = jnp.pad(seg_ids.astype(bf)[None, :], ((0, 3), (0, 0)))
    kv_own = jnp.concatenate([lax.dynamic_slice_in_dim(w_keyval, it * share, share, 1), ids], axis=0)
    own = jnp.concatenate([w_query, w_out.T, jnp.pad(kv_own, ((0, 0), (0, cols - share)))], axis=0)
    other = lax.ppermute(own, "yh", both)
    low = jnp.where(iy == 0, own, other)
    high = jnp.where(iy == 0, other, own)

    others = [lax.ppermute(tokens, "tp", [(i, (i + k) % nx) for i in range(nx)]) for k in range(1, nx)]

    w_at, id_at = slice(2 * rows, 3 * rows), slice(3 * rows, 3 * rows + 1)
    kv_pair = jnp.concatenate([low[w_at], high[w_at], low[id_at], high[id_at]], axis=0)[:, :share]
    kv_pair = jnp.pad(kv_pair, ((0, -kv_pair.shape[0] % 8), (0, 0)))
    kv_core = spread(kv_pair, ("x", "z"), nx * nz)
    kv_twin = lax.ppermute(kv_core, "c", both)

    qo_pair = jnp.concatenate([low[:rows], high[:rows], low[rows : 2 * rows], high[rows : 2 * rows]], axis=0)
    qo_near = spread(after(qo_pair, kv_core), "z", nz)
    part = nz * ny * rows
    qo_send = jnp.concatenate(
        [
            qo_near[:, : ny * rows].reshape(part, cols),
            qo_near[:, ny * rows :].reshape(part, cols),
        ],
        axis=0,
    )
    qo_all = lax.all_gather(qo_send, ("x", "c"), axis=0, tiled=False)

    shares = [tokens, *others]
    groups = []
    for g in range(nx):
        took = (it - g) % nx
        group = shares[nx - 1]
        for k in range(nx - 1):
            group = jnp.where(took == k, shares[k], group)
        groups.append(group)
    normed = rms_norm(jnp.concatenate(groups, axis=1), norm_gain)
    perm = natural_to_gathered(shard, rows, ny, nz)
    reordered = jnp.concatenate(
        [
            jnp.dot(normed[:, g * shard : (g + 1) * shard], perm, preferred_element_type=jnp.float32).astype(bf)
            for g in range(nx)
        ],
        axis=1,
    )
    blocks = jnp.stack([reordered[:, i * part : (i + 1) * part] for i in range(nx * nc)])
    kv_core, reordered, blocks, perm = lax.optimization_barrier((kv_core, reordered, blocks, perm))

    kv_zero = jnp.where(ic == 0, kv_core, kv_twin)
    kv_one = jnp.where(ic == 0, kv_twin, kv_core)
    all_ids = jnp.concatenate(
        [kv[:, ny * rows : ny * rows + ny] for kv in (kv_core, kv_twin)], axis=0
    ).astype(jnp.int32)
    labels = jnp.arange(SEGS, dtype=jnp.int32)
    starts = jnp.sum((all_ids.reshape(-1)[None, :] < labels[:, None]).astype(jnp.int32), axis=1)
    own_start = jnp.sum(jnp.where(seg_ids[:, None] == labels[None, :], starts[None, :], 0), axis=1)
    token_index = my_index * tok + jnp.arange(tok, dtype=jnp.int32)
    cosine, sine = angles((token_index - own_start).astype(jnp.float32))

    kv_rows = jnp.stack(
        [
            kv[:, : ny * rows].reshape(nx, part, share)
            for kv in (kv_zero, kv_one)
        ],
        axis=1,
    ).reshape(nx * nc * part, share)
    kv_raw = jnp.dot(reordered, kv_rows, preferred_element_type=jnp.float32)
    quarter = HD // 4
    swapped = jnp.concatenate([kv_raw[:, quarter:], kv_raw[:, :quarter]], axis=1)
    kv_share = jnp.where(it == 0, kv_raw * cosine + swapped * sine, kv_raw).astype(bf)

    block = nz * nc
    devices = nx * ny * block
    before = lax.ppermute(kv_share, SEQ, [(i, i + block) for i in range(devices - block)])
    chips = jnp.arange(nz, dtype=jnp.int32)
    to_send = jnp.where((chips > iz)[:, None, None], kv_share[None], before[None])
    near = lax.all_to_all(after(to_send, qo_send), "z", 0, 0, tiled=True)
    mine = spread(jnp.concatenate([near, kv_share[None]], axis=0), "tp", nx)
    kv_cache = jnp.concatenate([mine[t, nz] for t in range(nx)], axis=1)
    at_self = (chips == iz)[None, :, None, None] & (ic == 0)
    partner = lax.ppermute(jnp.where(at_self, mine[:, nz:], mine[:, :nz]), "c", both)
    block_of_mine = my_block - (chips >= iz).astype(jnp.int32)
    block_of_partner = my_block - jnp.where(ic == 1, chips > iz, chips >= iz).astype(jnp.int32)
    first_of_mine = ((block_of_mine * nz + chips) * nc + ic) * tok
    first_of_partner = ((block_of_partner * nz + chips) * nc + 1 - ic) * tok
    firsts = jnp.concatenate([first_of_mine, my_index[None] * tok, first_of_partner])
    keys_at = (firsts[:, None] + jnp.arange(tok, dtype=jnp.int32)[None, :]).reshape(1, -1)

    vmem = pl.BlockSpec(memory_space=pltpu.VMEM)
    hbm = pl.BlockSpec(memory_space=pl.ANY)
    scratch = [pltpu.VMEM((nx * nc, part, cols), bf), pltpu.SemaphoreType.DMA]
    queries = pl.pallas_call(
        queries_kernel,
        out_shape=jax.ShapeDtypeStruct((tok, cols), bf),
        in_specs=[vmem, vmem, vmem, hbm],
        out_specs=vmem,
        scratch_shapes=scratch,
        name="queries",
    )(blocks, cosine, sine, qo_all)
    partial = pl.pallas_call(
        attend_kernel,
        out_shape=jax.ShapeDtypeStruct((nx, tok, shard), bf),
        in_specs=[vmem] * 6 + [hbm],
        out_specs=vmem,
        scratch_shapes=scratch,
        name="attend",
    )(queries, mine, partner, keys_at, token_index[:, None], own_start[:, None], qo_all)

    received = lax.all_to_all(partial, "tp", 0, 0, tiled=True)
    summed = jnp.zeros((tok, shard), jnp.float32)
    for g in range(nx):
        summed = summed + lax.dot_general(
            received[g], perm, (((1,), (1,)), ((), ())), preferred_element_type=jnp.float32
        )
    hidden = (tokens.astype(jnp.float32) + summed).astype(bf)
    return (hidden, kv_cache)


def solution(mesh):
    fine = Mesh(mesh.devices.reshape(*GRID, mesh.shape["tp"]), (*SEQ, "tp"))
    in_specs = (P(SEQ, "tp"), P(SEQ), P(), P(SEQ, "tp"), P(SEQ, None), P("tp", SEQ))
    out_specs = (P(SEQ, "tp"), P(SEQ, None))
    return jax.shard_map(per_device, mesh=fine, in_specs=in_specs, out_specs=out_specs, check_vma=False)
```

time: 195 us -> 199 us (1.021)
  blocking collectives: 34.6 us -> 13.5 us
  starting transfers between devices: 43.3 us -> 59.2 us
  Pallas kernels: 0 us -> 10.3 us
  waiting for transfers between devices: 71.6 us -> 78 us
  other arithmetic: 15.4 us -> 9.42 us
  matrix products: 9.22 us -> 5.46 us
    all_to_all x1 -> x3, waiting for transfers between devices: 21 us -> 51.7 us  [spread(): return lax.all_to_all(copies, axes, 0, 0, tiled=True)]
    all_to_all x2 -> x1, blocking collectives: 34.6 us -> 13.5 us  [per_device(): near = lax.all_to_all(after(to_send, qo_send), 'z', 0, 0, tiled=True)]
    all_to_all x1, waiting for transfers between devices: 33.9 us -> 16.7 us  [per_device(): received = lax.all_to_all(partial, 'tp', 0, 0, tiled=True)]
    pallas_call x0 -> x2, Pallas kernels: none -> 10.3 us  [the longest x1 5.94 us: per_device(): pl.pallas_call(attend_kernel, out_shape=jax.ShapeDtypeStruct((nx, tok, sh...]
    all_to_all x1 -> x3, starting transfers between devices: 18.3 us -> 27.5 us  [spread(): return lax.all_to_all(copies, axes, 0, 0, tiled=True)]
    ppermute x3 -> x4, waiting for transfers between devices: 16.8 us -> 9.56 us  [the longest x1 4.85 us: per_device(): lax.ppermute(kv_share, SEQ, [(i, i + block) for i in range(devices - bloc...]
    concatenate x5 -> x8, other arithmetic: 8.64 us -> 2.61 us  [the longest x1 0.97 us: per_device(): jnp.concatenate([qo_near[:, :ny * rows].reshape(part, cols), qo_near[:, n...]
    ppermute x3 -> x4, starting transfers between devices: 10.2 us -> 15.8 us  [the longest x1 6.08 us: per_device(): lax.ppermute(kv_share, SEQ, [(i, i + block) for i in range(devices - bloc...]
  transfers between devices with their start and end apart: 9 -> 12, of which waited for: 5 -> 7; matrix products, arithmetic and copies ran while one was open for 10% -> 8% of each run, Pallas kernels for 0% -> 2%
where the time goes in v1:
time: 199 us; the launch traced here: 198 us
  waiting for transfers between devices  78 us (39%)
  starting transfers between devices  59.2 us (30%)
  between operations  14.6 us (7%)
  blocking collectives  13.5 us (7%)
  Pallas kernels  10.3 us (5%)
  other arithmetic  9.42 us (5%)
  local copies, waits for them, and re-layouts  7.31 us (4%)
  matrix products  5.46 us (3%)
    all_to_all x3, waiting for transfers between devices, spread(): return lax.all_to_all(copies, axes, 0, 0, tiled=True)  51.7 us
    all_to_all x3, starting transfers between devices, spread(): return lax.all_to_all(copies, axes, 0, 0, tiled=True)  27.5 us
    all_to_all x1, waiting for transfers between devices, per_device(): received = lax.all_to_all(partial, 'tp', 0, 0, tiled=True)  16.7 us
    all_to_all x1, blocking collectives, per_device(): near = lax.all_to_all(after(to_send, qo_send), 'z', 0, 0, tiled=True)  13.5 us
    ppermute x3, starting transfers between devices, per_device(): lax.ppermute(tokens, 'tp', [(i, (i + k) % nx) for i in range(nx)])  12.3 us
    ppermute x1, starting transfers between devices, per_device(): lax.ppermute(kv_share, SEQ, [(i, i + block) for i in range(devices - bloc...  6.08 us
    pallas_call x1, Pallas kernels, per_device(): pl.pallas_call(attend_kernel, out_shape=jax.ShapeDtypeStruct((nx, tok, sh...  5.94 us
    ppermute x1, starting transfers between devices, per_device(): other = lax.ppermute(own, 'yh', both)  5.94 us
  transfers between devices with their start and end apart: 12, of which 7 were waited for; matrix products, arithmetic and copies ran while one was open for 8% of the time, Pallas kernels for 2%

profile of v1, /device:TPU:2, one launch (start us, length us, event | category | flops | bytes accessed | tf_op | source)
XLA Modules:
  0.0 197.8 jit_solution(11325835170313260941)
XLA Ops:
  7.2 4.6 %collective-permute-start.1 = (bf16[128,640]{1,0:T(8,128)(2,1)}, bf16[128,640]{1,0:T(8,128)(2,1)S(1)}, u32[]{:S(2)}, u32[]{:S(2)}) collective-permute-start(bf16[128,640]{1,0:T(8,128)(2,1)} %param.6), channel_id=1, source_target_pairs={{0,2},{1,3},{2,0},{3,1},{4,6},{5,7},{6,4},{7,5},{8,10},{9,11},{10,... | collective-permute-start | bytes 491528 | tf_op jit(solution)/shard_map/ppermute | solution.py:123
  11.8 3.5 %collective-permute-start.2 = (bf16[128,640]{1,0:T(8,128)(2,1)}, bf16[128,640]{1,0:T(8,128)(2,1)S(1)}, u32[]{:S(2)}, u32[]{:S(2)}) collective-permute-start(bf16[128,640]{1,0:T(8,128)(2,1)} %param.6), channel_id=1, source_target_pairs={{0,1},{1,2},{2,3},{3,0},{4,5},{5,6},{6,7},{7,4},{8,9},{9,10},{10,1... | collective-permute-start | bytes 491528 | tf_op jit(solution)/shard_map/ppermute | solution.py:123
  15.3 4.2 %collective-permute-start.3 = (bf16[128,640]{1,0:T(8,128)(2,1)}, bf16[128,640]{1,0:T(8,128)(2,1)S(1)}, u32[]{:S(2)}, u32[]{:S(2)}) collective-permute-start(bf16[128,640]{1,0:T(8,128)(2,1)} %param.6), channel_id=1, source_target_pairs={{0,3},{1,0},{2,1},{3,2},{4,7},{5,4},{6,5},{7,6},{8,11},{9,8},{10,9... | collective-permute-start | bytes 491528 | tf_op jit(solution)/shard_map/ppermute | solution.py:123
  19.5 0.7 convert_bitcast_fusion
  20.2 0.8 fusion.37
  20.9 5.9 %collective-permute-start = (bf16[64,512]{1,0:T(8,128)(2,1)S(1)}, bf16[64,512]{1,0:T(8,128)(2,1)S(1)}, u32[]{:S(2)}, u32[]{:S(2)}) collective-permute-start(bf16[64,512]{1,0:T(8,128)(2,1)S(1)} %fusion.37), channel_id=1, source_target_pairs={{0,64},{64,0},{1,65},{65,1},{2,66},{66,2},{3,67},{67,3},{4,68},{68... | collective-permute-start | bytes 196616 | tf_op jit(solution)/shard_map/ppermute | solution.py:119
  27.0 0.7 convert_element_type.71
  27.7 0.3 fusion.64
  28.0 3.2 %collective-permute-done = bf16[64,512]{1,0:T(8,128)(2,1)S(1)} collective-permute-done((bf16[64,512]{1,0:T(8,128)(2,1)S(1)}, bf16[64,512]{1,0:T(8,128)(2,1)S(1)}, u32[]{:S(2)}, u32[]{:S(2)}) %collective-permute-start) | collective-permute-done | bytes 65568 | tf_op jit(solution)/shard_map/ppermute | solution.py:119
  31.3 0.8 broadcast_select_fusion.4
  32.1 0.8 broadcast_in_dim.65
  32.9 13.5 %all-to-all-start = ((bf16[32,48,128]{2,1,0:T(8,128)(2,1)}), bf16[32,48,128]{2,1,0:T(8,128)(2,1)S(1)}, u32[]{:S(2)}, u32[]{:S(2)}) async-start(bf16[32,48,128]{2,1,0:T(8,128)(2,1)} %broadcast_in_dim.65), calls=%async_computation | async-start | bytes 786432 | tf_op jit(solution)/shard_map/all_to_all | solution.py:36
  46.5 0.1 select_select_fusion.3
  46.6 0.2 fusion.18
  46.8 0.2 fusion.20
  47.1 0.5 convolution_convert_fusion.3
  47.6 0.3 copy-done.5
  47.9 9.7 %all-to-all-done = bf16[32,48,128]{2,1,0:T(8,128)(2,1)S(1)} async-done(((bf16[32,48,128]{2,1,0:T(8,128)(2,1)}), bf16[32,48,128]{2,1,0:T(8,128)(2,1)S(1)}, u32[]{:S(2)}, u32[]{:S(2)}) %all-to-all-start) | async-done | bytes 393248 | tf_op jit(solution)/shard_map/all_to_all | solution.py:36
  57.6 0.9 broadcast_in_dim.68
  58.5 3.9 %all-to-all-start.1 = ((bf16[8,80,512]{2,1,0:T(8,128)(2,1)}), bf16[8,80,512]{2,1,0:T(8,128)(2,1)S(1)}, u32[]{:S(2)}, u32[]{:S(2)}) async-start(bf16[8,80,512]{2,1,0:T(8,128)(2,1)} %broadcast_in_dim.68), calls=%async_computation.1 | async-start | bytes 1310720 | tf_op jit(solution)/shard_map/all_to_all | solution.py:36
  62.5 0.1 fusion.35
  62.6 1.4 convolution_convert_fusion.2
  64.0 15.5 %all-to-all-done.1 = bf16[8,80,512]{2,1,0:T(8,128)(2,1)S(1)} async-done(((bf16[8,80,512]{2,1,0:T(8,128)(2,1)}), bf16[8,80,512]{2,1,0:T(8,128)(2,1)S(1)}, u32[]{:S(2)}, u32[]{:S(2)}) %all-to-all-start.1) | async-done | bytes 655392 | tf_op jit(solution)/shard_map/all_to_all | solution.py:36
  79.6 1.0 pad_maximum_fusion.2
  80.6 0.1 fusion.33
  80.7 0.2 copy-done.6
  80.9 0.5 convolution_convert_fusion.1
  81.4 0.1 fusion.31
  81.6 0.5 convolution_convert_fusion
  82.1 1.9 collective-permute-start.4
  84.1 0.1 fusion.29.normed_ref
  84.3 1.5 collective-permute-done.4
  85.8 0.3 convert_reduce_fusion
  86.2 0.1 select_reduce_fusion
  86.3 0.1 pad_maximum_fusion.3
  86.4 0.3 fusion.73
  86.7 0.1 fusion.72
  86.8 0.3 fusion.45
  87.1 0.8 fusion.40
  87.9 6.1 %collective-permute-start.5 = (bf16[128,128]{1,0:T(8,128)(2,1)S(1)}, bf16[128,128]{1,0:T(8,128)(2,1)S(1)}, u32[]{:S(2)}, u32[]{:S(2)}) collective-permute-start(bf16[128,128]{1,0:T(8,128)(2,1)S(1)} %get-tuple-element.14), channel_id=1, source_target_pairs={{0,64},{4,68},{8,72},{12,76},{16,80},{20,84},{24,88},{28,92},{32,9... | collective-permute-start | bytes 98312 | tf_op jit(solution)/shard_map/ppermute | solution.py:188
  94.0 4.9 %collective-permute-done.5 = bf16[128,128]{1,0:T(8,128)(2,1)S(1)} collective-permute-done((bf16[128,128]{1,0:T(8,128)(2,1)S(1)}, bf16[128,128]{1,0:T(8,128)(2,1)S(1)}, u32[]{:S(2)}, u32[]{:S(2)}) %collective-permute-start.5) | collective-permute-done | bytes 32800 | tf_op jit(solution)/shard_map/ppermute | solution.py:188
  98.8 0.1 broadcast_select_fusion.2
  98.9 13.5 %all_to_all.25 = bf16[8,128,128]{2,1,0:T(8,128)(2,1)S(1)} all-to-all(bf16[8,128,128]{2,1,0:T(8,128)(2,1)S(1)} %broadcast_select_fusion.2), channel_id=1, replica_groups=mesh['x'=4,'yh'=2,'z'=8,'c'=2,'tp'=4] {'z'}, dimensions={0} | all-to-all | bytes 524288 | tf_op jit(solution)/shard_map/all_to_all | solution.py:191
  112.4 1.3 broadcast_in_dim.104
  113.7 10.1 %all-to-all-start.3 = ((bf16[4,9,128,128]{3,2,1,0:T(8,128)(2,1)}), bf16[4,9,128,128]{3,2,1,0:T(8,128)(2,1)S(1)}, u32[]{:S(2)}, u32[]{:S(2)}) async-start(bf16[4,9,128,128]{3,2,1,0:T(8,128)(2,1)} %broadcast_in_dim.104), calls=%async_computation.3 | async-start | bytes 2359296 | tf_op jit(solution)/shard_map/all_to_all | solution.py:36
  123.9 26.6 %all-to-all-done.3.mine_ref = bf16[4,9,128,128]{3,2,1,0:T(8,128)(2,1)S(1)} async-done(((bf16[4,9,128,128]{3,2,1,0:T(8,128)(2,1)}), bf16[4,9,128,128]{3,2,1,0:T(8,128)(2,1)S(1)}, u32[]{:S(2)}, u32[]{:S(2)}) %all-to-all-start.3) | async-done | bytes 1179680 | tf_op jit(solution)/shard_map/all_to_all | solution.py:36
  150.5 1.2 slice_select_fusion
  151.7 1.9 collective-permute-start.6
  153.7 0.1 pad_add_fusion
  153.8 0.1 add_bitcast_fusion
  153.8 0.6 copy.26
  154.4 0.6 iota_add_fusion.token_ref
  155.1 0.7 copy.22.start_ref
  155.8 4.4 %queries.1.queries_ref = bf16[128,512]{1,0:T(8,128)(2,1)} custom-call(bf16[8,128,320]{2,1,0:T(8,128)(2,1)} %copy-done.3, f32[128,128]{1,0:T(8,128)} %get-tuple-element.36.cosine_ref, f32[128,128]{1,0:T(8,128)} %get-tuple-element.15.sine_ref, bf16[8,640,512]{2,1,0:T(8,128)(2,1)} %bitcast.80), custom_call_target="tpu_custom_call" | custom-call | tf_op jit(solution)/shard_map/queries/pallas_call | solution.py:206
  160.2 0.9 copy-done.2
  161.1 5.9 %attend.1 = bf16[4,128,640]{2,1,0:T(8,128)(2,1)} custom-call(bf16[128,512]{1,0:T(8,128)(2,1)} %queries.1.queries_ref, bf16[4,9,128,128]{3,2,1,0:T(8,128)(2,1)} %copy-done.1, bf16[4,8,128,128]{3,2,1,0:T(8,128)(2,1)} %copy-done.2, s32[1,2176]{1,0:T(1,128)} %bitcast.91, s32[128,1]{1,0:T(8,128)} %iota_add_fusion.token_ref, s32[128,1]{1,0:T(8,128)} %copy.22.start_ref, ...), custom_call_target="tpu_custom_call" | custom-call | tf_op jit(solution)/shard_map/attend/pallas_call | solution.py:214
  167.1 3.5 %all-to-all-start.4 = ((bf16[4,128,640]{2,1,0:T(8,128)(2,1)}), bf16[4,128,640]{2,1,0:T(8,128)(2,1)S(1)}, u32[]{:S(2)}, u32[]{:S(2)}) async-start(bf16[4,128,640]{2,1,0:T(8,128)(2,1)} %attend.1), calls=%async_computation.4 | async-start | bytes 1310720 | tf_op jit(solution)/shard_map/all_to_all | solution.py:223
  170.6 0.8 slice_bitcast_fusion.20
  171.4 0.7 pad_maximum_fusion.5
  172.1 16.7 %all-to-all-done.4 = bf16[4,128,640]{2,1,0:T(8,128)(2,1)S(1)} async-done(((bf16[4,128,640]{2,1,0:T(8,128)(2,1)}), bf16[4,128,640]{2,1,0:T(8,128)(2,1)S(1)}, u32[]{:S(2)}, u32[]{:S(2)}) %all-to-all-start.4) | async-done | bytes 655392 | tf_op jit(solution)/shard_map/all_to_all | solution.py:223
  188.8 0.4 fusion.23
  189.2 0.4 convolution_add_fusion.2
  189.5 0.4 convolution_add_fusion.1
  189.9 1.0 fusion.22
  (50 shorter events, 0.6 us)
Async XLA Ops:
  7.2 13.0 %copy-start = (bf16[20,512]{1,0:T(8,128)(2,1)S(1)}, bf16[20,512]{1,0:T(8,128)(2,1)}, u32[]{:S(2)}) copy-start(bf16[20,512]{1,0:T(8,128)(2,1)} %param.10) | copy-start | bytes 61444
  7.2 39.3 %copy-start.4 = (bf16[128,640]{1,0:T(8,128)(2,1)S(1)}, bf16[128,640]{1,0:T(8,128)(2,1)}, u32[]{:S(2)}) copy-start(bf16[128,640]{1,0:T(8,128)(2,1)} %param.6) | copy-start | bytes 491524
  7.2 39.3 %collective-permute-start.1 = (bf16[128,640]{1,0:T(8,128)(2,1)}, bf16[128,640]{1,0:T(8,128)(2,1)S(1)}, u32[]{:S(2)}, u32[]{:S(2)}) collective-permute-start(bf16[128,640]{1,0:T(8,128)(2,1)} %param.6), channel_id=1, source_target_pairs={{0,2},{1,3},{2,0},{3,1},{4,6},{5,7},{6,4},{7,5},{8,10},{9,11},{10,... | collective-permute-start | bytes 491528 | tf_op jit(solution)/shard_map/ppermute | solution.py:123
  11.8 34.6 %collective-permute-start.2 = (bf16[128,640]{1,0:T(8,128)(2,1)}, bf16[128,640]{1,0:T(8,128)(2,1)S(1)}, u32[]{:S(2)}, u32[]{:S(2)}) collective-permute-start(bf16[128,640]{1,0:T(8,128)(2,1)} %param.6), channel_id=1, source_target_pairs={{0,1},{1,2},{2,3},{3,0},{4,5},{5,6},{6,7},{7,4},{8,9},{9,10},{10,1... | collective-permute-start | bytes 491528 | tf_op jit(solution)/shard_map/ppermute | solution.py:123
  15.3 31.2 %collective-permute-start.3 = (bf16[128,640]{1,0:T(8,128)(2,1)}, bf16[128,640]{1,0:T(8,128)(2,1)S(1)}, u32[]{:S(2)}, u32[]{:S(2)}) collective-permute-start(bf16[128,640]{1,0:T(8,128)(2,1)} %param.6), channel_id=1, source_target_pairs={{0,3},{1,0},{2,1},{3,2},{4,7},{5,4},{6,5},{7,6},{8,11},{9,8},{10,9... | collective-permute-start | bytes 491528 | tf_op jit(solution)/shard_map/ppermute | solution.py:123
  20.9 10.3 %collective-permute-start = (bf16[64,512]{1,0:T(8,128)(2,1)S(1)}, bf16[64,512]{1,0:T(8,128)(2,1)S(1)}, u32[]{:S(2)}, u32[]{:S(2)}) collective-permute-start(bf16[64,512]{1,0:T(8,128)(2,1)S(1)} %fusion.37), channel_id=1, source_target_pairs={{0,64},{64,0},{1,65},{65,1},{2,66},{66,2},{3,67},{67,3},{4,68},{68... | collective-permute-start | bytes 196616 | tf_op jit(solution)/shard_map/ppermute | solution.py:119
  32.9 24.7 %all-to-all-start = ((bf16[32,48,128]{2,1,0:T(8,128)(2,1)}), bf16[32,48,128]{2,1,0:T(8,128)(2,1)S(1)}, u32[]{:S(2)}, u32[]{:S(2)}) async-start(bf16[32,48,128]{2,1,0:T(8,128)(2,1)} %broadcast_in_dim.65), calls=%async_computation | async-start | bytes 786432 | tf_op jit(solution)/shard_map/all_to_all | solution.py:36
  47.1 0.8 copy-start.5
  58.5 21.0 %all-to-all-start.1 = ((bf16[8,80,512]{2,1,0:T(8,128)(2,1)}), bf16[8,80,512]{2,1,0:T(8,128)(2,1)S(1)}, u32[]{:S(2)}, u32[]{:S(2)}) async-start(bf16[8,80,512]{2,1,0:T(8,128)(2,1)} %broadcast_in_dim.68), calls=%async_computation.1 | async-start | bytes 1310720 | tf_op jit(solution)/shard_map/all_to_all | solution.py:36
  62.4 93.4 %all-gather.3.cloned.1.call-start = ((), (), s32[]{:S(2)}) async-start(), calls=%async_computation.5 | async-start | bytes 5898240 | tf_op jit(solution)/shard_map/all_gather | solution.py:141
  79.6 1.3 copy-start.6
  82.1 4.1 %copy-start.7 = (s32[128]{0:T(128)S(1)}, s32[128]{0:T(128)}, u32[]{:S(2)}) copy-start(s32[128]{0:T(128)} %param.7) | copy-start | bytes 1540
  82.1 3.6 %collective-permute-start.4 = (bf16[32,48,128]{2,1,0:T(8,128)(2,1)S(1)}, bf16[32,48,128]{2,1,0:T(8,128)(2,1)S(1)}, u32[]{:S(2)}, u32[]{:S(2)}) collective-permute-start(bf16[32,48,128]{2,1,0:T(8,128)(2,1)S(1)} %all-to-all-done), channel_id=1, source_target_pairs={{0,4},{4,0},{1,5},{5,1},{2,6},{6,2},{3,7},{7,3},{8,12},{12,8},{9,1... | collective-permute-start | bytes 1179656 | tf_op jit(solution)/shard_map/ppermute | solution.py:129
  84.2 2.2 %copy-start.3 = (bf16[8,128,320]{2,1,0:T(8,128)(2,1)}, bf16[8,128,320]{2,1,0:T(8,128)(2,1)S(1)}, u32[]{:S(2)}) copy-start(bf16[8,128,320]{2,1,0:T(8,128)(2,1)S(1)} %fusion.29.normed_ref) | copy-start | bytes 1966084
  87.9 11.0 %collective-permute-start.5 = (bf16[128,128]{1,0:T(8,128)(2,1)S(1)}, bf16[128,128]{1,0:T(8,128)(2,1)S(1)}, u32[]{:S(2)}, u32[]{:S(2)}) collective-permute-start(bf16[128,128]{1,0:T(8,128)(2,1)S(1)} %get-tuple-element.14), channel_id=1, source_target_pairs={{0,64},{4,68},{8,72},{12,76},{16,80},{20,84},{24,88},{28,92},{32,9... | collective-permute-start | bytes 98312 | tf_op jit(solution)/shard_map/ppermute | solution.py:188
  113.7 36.7 %all-to-all-start.3 = ((bf16[4,9,128,128]{3,2,1,0:T(8,128)(2,1)}), bf16[4,9,128,128]{3,2,1,0:T(8,128)(2,1)S(1)}, u32[]{:S(2)}, u32[]{:S(2)}) async-start(bf16[4,9,128,128]{3,2,1,0:T(8,128)(2,1)} %broadcast_in_dim.104), calls=%async_computation.3 | async-start | bytes 2359296 | tf_op jit(solution)/shard_map/all_to_all | solution.py:36
  150.5 9.7 %copy-start.1 = (bf16[4,9,128,128]{3,2,1,0:T(8,128)(2,1)}, bf16[4,9,128,128]{3,2,1,0:T(8,128)(2,1)S(1)}, u32[]{:S(2)}) copy-start(bf16[4,9,128,128]{3,2,1,0:T(8,128)(2,1)S(1)} %all-to-all-done.3.mine_ref) | copy-start | bytes 3538948
  151.7 8.4 %collective-permute-start.6 = (bf16[4,8,128,128]{3,2,1,0:T(8,128)(2,1)}, bf16[4,8,128,128]{3,2,1,0:T(8,128)(2,1)S(1)}, u32[]{:S(2)}, u32[]{:S(2)}) collective-permute-start(bf16[4,8,128,128]{3,2,1,0:T(8,128)(2,1)} %slice_select_fusion), channel_id=1, source_target_pairs={{0,4},{4,0},{1,5},{5,1},{2,6},{6,2},{3,7},{7,3},{8,12},{12,8},{9,1... | collective-permute-start | bytes 3145736 | tf_op jit(solution)/shard_map/ppermute | solution.py:195
  160.2 1.0 copy-start.2
  167.1 21.7 %all-to-all-start.4 = ((bf16[4,128,640]{2,1,0:T(8,128)(2,1)}), bf16[4,128,640]{2,1,0:T(8,128)(2,1)S(1)}, u32[]{:S(2)}, u32[]{:S(2)}) async-start(bf16[4,128,640]{2,1,0:T(8,128)(2,1)} %attend.1), calls=%async_computation.4 | async-start | bytes 1310720 | tf_op jit(solution)/shard_map/all_to_all | solution.py:223
Sparse Core Ops, SparseCore 0:
  80.7 39.8 all-gather.2

commit v2 on v1

--- a/solution.py
+++ b/solution.py
@@ -34,6 +34,18 @@
 def spread(slab, axes, count):
     copies = jnp.broadcast_to(slab[None], (count, *slab.shape))
     return lax.all_to_all(copies, axes, 0, 0, tiled=True)
+
+
+def in_order(shares, here):
+    count = len(shares)
+    ordered = []
+    for g in range(count):
+        came = (here - g) % count
+        share = shares[count - 1]
+        for k in range(count - 1):
+            share = jnp.where(came == k, shares[k], share)
+        ordered.append(share)
+    return ordered
 
 
 def natural_to_gathered(per, rows, ny, nz):
@@ -54,6 +66,7 @@
     raw = jnp.dot(normed_ref[0], weights_ref[0], preferred_element_type=jnp.float32)
     for g in range(1, groups):
         raw = raw + jnp.dot(normed_ref[g], weights_ref[g], preferred_element_type=jnp.float32)
+    raw = raw * HD ** (-0.5)
     half = HD // 2
     for h in range(cols // HD):
         lo = raw[:, h * HD : h * HD + half]
@@ -65,18 +78,20 @@
 
 
 def attend_kernel(
-    queries_ref, mine_ref, partner_ref, keys_at_ref, token_ref, start_ref, qo_ref, out_ref, weights_ref, sem
+    queries_ref, mine_ref, partner_ref, own_ref, keys_at_ref, token_ref, first_ref, qo_ref, out_ref, weights_ref, sem
 ):
     groups, part, cols = weights_ref.shape
     copy = pltpu.make_async_copy(qo_ref.at[:, pl.ds(part, part), :], weights_ref, sem)
     copy.start()
-    flat = lambda ref, t: ref[t].reshape(ref.shape[1] * ref.shape[2], ref.shape[3])
-    whole = lambda t: jnp.concatenate([flat(mine_ref, t), flat(partner_ref, t)], axis=0)
+
+    def whole(t):
+        far = [ref[:, t].reshape(ref.shape[0] * ref.shape[2], ref.shape[3]) for ref in (mine_ref, partner_ref)]
+        return jnp.concatenate([*far, own_ref[t]], axis=0)
+
     keys = jnp.concatenate([whole(0), whole(1)], axis=1)
     values = jnp.concatenate([whole(2), whole(3)], axis=1)
     at = keys_at_ref[...]
-    token = token_ref[...]
-    live = (at <= token) & (at >= start_ref[...]) & (token - at < WINDOW)
+    live = (at <= token_ref[...]) & (at >= first_ref[...])
     heads = []
     for h in range(cols // HD):
         scores = lax.dot_general(
@@ -84,10 +99,10 @@
             keys,
             (((1,), (1,)), ((), ())),
             preferred_element_type=jnp.float32,
-        ) * HD ** (-0.5)
+        )
         scores = jnp.where(live, scores, -1e30)
         powered = jnp.exp(scores - jnp.max(scores, axis=1, keepdims=True))
-        weights = (powered / jnp.sum(powered, axis=1, keepdims=True)).astype(jnp.bfloat16)
+        weights = (powered * (1.0 / jnp.sum(powered, axis=1, keepdims=True))).astype(jnp.bfloat16)
         heads.append(
             jnp.dot(weights, values, preferred_element_type=jnp.float32).astype(jnp.bfloat16)
         )
@@ -129,25 +144,21 @@
     kv_twin = lax.ppermute(kv_core, "c", both)
 
     qo_pair = jnp.concatenate([low[:rows], high[:rows], low[rows : 2 * rows], high[rows : 2 * rows]], axis=0)
-    qo_near = spread(after(qo_pair, kv_core), "z", nz)
+    least = (1 << 20) // (2 * nz * cols)
+    qo_pair = jnp.pad(qo_pair, ((0, max(0, least - qo_pair.shape[0])), (0, 0)))
+    qo_near = lax.all_gather(qo_pair, "z", axis=0, tiled=False)
     part = nz * ny * rows
     qo_send = jnp.concatenate(
         [
             qo_near[:, : ny * rows].reshape(part, cols),
-            qo_near[:, ny * rows :].reshape(part, cols),
+            qo_near[:, ny * rows : 2 * ny * rows].reshape(part, cols),
         ],
         axis=0,
     )
     qo_all = lax.all_gather(qo_send, ("x", "c"), axis=0, tiled=False)
-
-    shares = [tokens, *others]
-    groups = []
-    for g in range(nx):
-        took = (it - g) % nx
-        group = shares[nx - 1]
-        for k in range(nx - 1):
-            group = jnp.where(took == k, shares[k], group)
-        groups.append(group)
+    kv_twin = after(kv_twin, qo_send)
+
+    groups = in_order([tokens, *others], it)
     normed = rms_norm(jnp.concatenate(groups, axis=1), norm_gain)
     perm = natural_to_gathered(shard, rows, ny, nz)
     reordered = jnp.concatenate(
@@ -188,16 +199,18 @@
     before = lax.ppermute(kv_share, SEQ, [(i, i + block) for i in range(devices - block)])
     chips = jnp.arange(nz, dtype=jnp.int32)
     to_send = jnp.where((chips > iz)[:, None, None], kv_share[None], before[None])
-    near = lax.all_to_all(after(to_send, qo_send), "z", 0, 0, tiled=True)
-    mine = spread(jnp.concatenate([near, kv_share[None]], axis=0), "tp", nx)
-    kv_cache = jnp.concatenate([mine[t, nz] for t in range(nx)], axis=1)
-    at_self = (chips == iz)[None, :, None, None] & (ic == 0)
-    partner = lax.ppermute(jnp.where(at_self, mine[:, nz:], mine[:, :nz]), "c", both)
+    to_send = jnp.broadcast_to(to_send[:, None], (nz, nx, tok, share)).reshape(nz * nx, tok, share)
+    mine = lax.all_to_all(to_send, ("z", "tp"), 0, 0, tiled=True).reshape(nz, nx, tok, share)
+    rest = [lax.ppermute(kv_share, "tp", [(i, (i + k) % nx) for i in range(nx)]) for k in range(1, nx)]
+    own_kv = jnp.stack(in_order([kv_share, *rest], it))
+    kv_cache = jnp.concatenate(list(own_kv), axis=1)
+    at_self = (chips == iz)[:, None, None, None] & (ic == 0)
+    partner = lax.ppermute(jnp.where(at_self, own_kv[None], mine), "c", both)
     block_of_mine = my_block - (chips >= iz).astype(jnp.int32)
     block_of_partner = my_block - jnp.where(ic == 1, chips > iz, chips >= iz).astype(jnp.int32)
     first_of_mine = ((block_of_mine * nz + chips) * nc + ic) * tok
     first_of_partner = ((block_of_partner * nz + chips) * nc + 1 - ic) * tok
-    firsts = jnp.concatenate([first_of_mine, my_index[None] * tok, first_of_partner])
+    firsts = jnp.concatenate([first_of_mine, first_of_partner, my_index[None] * tok])
     keys_at = (firsts[:, None] + jnp.arange(tok, dtype=jnp.int32)[None, :]).reshape(1, -1)
 
     vmem = pl.BlockSpec(memory_space=pltpu.VMEM)
@@ -211,14 +224,15 @@
         scratch_shapes=scratch,
         name="queries",
     )(blocks, cosine, sine, qo_all)
+    reach_back = jnp.maximum(own_start, token_index - (WINDOW - 1))
     partial = pl.pallas_call(
         attend_kernel,
         out_shape=jax.ShapeDtypeStruct((nx, tok, shard), bf),
-        in_specs=[vmem] * 6 + [hbm],
+        in_specs=[vmem] * 7 + [hbm],
         out_specs=vmem,
         scratch_shapes=scratch,
         name="attend",
-    )(queries, mine, partner, keys_at, token_index[:, None], own_start[:, None], qo_all)
+    )(queries, mine, partner, own_kv, keys_at, token_index[:, None], reach_back[:, None], qo_all)
 
     received = lax.all_to_all(partial, "tp", 0, 0, tiled=True)
     summed = jnp.zeros((tok, shard), jnp.float32)

time: 199 us -> 197 us (0.990)
  the two profiles are of different devices: /device:TPU:2 before, /device:TPU:66 now
where the time goes in v2:
time: 197 us; the launch traced here: 196 us
  waiting for transfers between devices  84.6 us (43%)
  starting transfers between devices  65.6 us (33%)
  between operations  14.7 us (7%)
  other arithmetic  10.8 us (5%)
  Pallas kernels  10.2 us (5%)
  local copies, waits for them, and re-layouts  5.49 us (3%)
  matrix products  4.55 us (2%)
    all_gather x1, waiting for transfers between devices, per_device(): qo_near = lax.all_gather(qo_pair, 'z', axis=0, tiled=False)  41.9 us
    all_to_all x1, waiting for transfers between devices, per_device(): received = lax.all_to_all(partial, 'tp', 0, 0, tiled=True)  17.5 us
    ppermute x3, waiting for transfers between devices, per_device(): lax.ppermute(kv_share, 'tp', [(i, (i + k) % nx) for i in range(nx)])  14.7 us
    all_to_all x1, starting transfers between devices, spread(): return lax.all_to_all(copies, axes, 0, 0, tiled=True)  12.6 us
    ppermute x3, starting transfers between devices, per_device(): lax.ppermute(tokens, 'tp', [(i, (i + k) % nx) for i in range(nx)])  12.1 us
    ppermute x3, starting transfers between devices, per_device(): lax.ppermute(kv_share, 'tp', [(i, (i + k) % nx) for i in range(nx)])  11.9 us
    all_to_all x1, starting transfers between devices, per_device(): lax.all_to_all(to_send, ('z', 'tp'), 0, 0, tiled=True)  8.19 us
    ppermute x1, starting transfers between devices, per_device(): lax.ppermute(kv_share, SEQ, [(i, i + block) for i in range(devices - bloc...  7.36 us
  transfers between devices with their start and end apart: 15, of which 7 were waited for; matrix products, arithmetic and copies ran while one was open for 9% of the time, Pallas kernels for 2%

profile of v2, /device:TPU:66, one launch (start us, length us, event | category | flops | bytes accessed | tf_op | source)
XLA Modules:
  0.0 195.9 jit_solution(8342507251897237)
XLA Ops:
  7.2 4.5 %collective-permute-start.1 = (bf16[128,640]{1,0:T(8,128)(2,1)}, bf16[128,640]{1,0:T(8,128)(2,1)S(1)}, u32[]{:S(2)}, u32[]{:S(2)}) collective-permute-start(bf16[128,640]{1,0:T(8,128)(2,1)} %param.6), channel_id=1, source_target_pairs={{0,2},{1,3},{2,0},{3,1},{4,6},{5,7},{6,4},{7,5},{8,10},{9,11},{10,... | collective-permute-start | bytes 491528 | tf_op jit(solution)/shard_map/ppermute | solution.py:138
  11.7 3.5 %collective-permute-start.2 = (bf16[128,640]{1,0:T(8,128)(2,1)}, bf16[128,640]{1,0:T(8,128)(2,1)S(1)}, u32[]{:S(2)}, u32[]{:S(2)}) collective-permute-start(bf16[128,640]{1,0:T(8,128)(2,1)} %param.6), channel_id=1, source_target_pairs={{0,1},{1,2},{2,3},{3,0},{4,5},{5,6},{6,7},{7,4},{8,9},{9,10},{10,1... | collective-permute-start | bytes 491528 | tf_op jit(solution)/shard_map/ppermute | solution.py:138
  15.2 4.2 %collective-permute-start.3 = (bf16[128,640]{1,0:T(8,128)(2,1)}, bf16[128,640]{1,0:T(8,128)(2,1)S(1)}, u32[]{:S(2)}, u32[]{:S(2)}) collective-permute-start(bf16[128,640]{1,0:T(8,128)(2,1)} %param.6), channel_id=1, source_target_pairs={{0,3},{1,0},{2,1},{3,2},{4,7},{5,4},{6,5},{7,6},{8,11},{9,8},{10,9... | collective-permute-start | bytes 491528 | tf_op jit(solution)/shard_map/ppermute | solution.py:138
  19.4 0.7 convert_bitcast_fusion
  20.0 0.8 fusion.44
  20.8 6.1 %collective-permute-start = (bf16[64,512]{1,0:T(8,128)(2,1)S(1)}, bf16[64,512]{1,0:T(8,128)(2,1)S(1)}, u32[]{:S(2)}, u32[]{:S(2)}) collective-permute-start(bf16[64,512]{1,0:T(8,128)(2,1)S(1)} %fusion.44), channel_id=1, source_target_pairs={{0,64},{64,0},{1,65},{65,1},{2,66},{66,2},{3,67},{67,3},{4,68},{68... | collective-permute-start | bytes 196616 | tf_op jit(solution)/shard_map/ppermute | solution.py:134
  27.0 0.7 convert_element_type.73
  27.7 0.3 fusion.71
  28.1 3.2 %collective-permute-done = bf16[64,512]{1,0:T(8,128)(2,1)S(1)} collective-permute-done((bf16[64,512]{1,0:T(8,128)(2,1)S(1)}, bf16[64,512]{1,0:T(8,128)(2,1)S(1)}, u32[]{:S(2)}, u32[]{:S(2)}) %collective-permute-start) | collective-permute-done | bytes 65568 | tf_op jit(solution)/shard_map/ppermute | solution.py:134
  31.3 0.8 broadcast_select_fusion.5
  32.1 0.8 broadcast_in_dim.53
  33.0 12.6 %all-to-all-start = ((bf16[32,48,128]{2,1,0:T(8,128)(2,1)}), bf16[32,48,128]{2,1,0:T(8,128)(2,1)S(1)}, u32[]{:S(2)}, u32[]{:S(2)}) async-start(bf16[32,48,128]{2,1,0:T(8,128)(2,1)} %broadcast_in_dim.53), calls=%async_computation | async-start | bytes 786432 | tf_op jit(solution)/shard_map/all_to_all | solution.py:36
  45.6 0.7 fusion.34
  46.4 0.1 select_select_fusion.3
  46.5 0.2 fusion.18
  46.7 0.2 fusion.20
  46.9 0.5 convolution_convert_fusion.2
  47.5 0.5 convolution_convert_fusion.3
  48.0 41.9 %all-gather.5.cloned.1.call-done = bf16[1024,512]{1,0:T(8,128)(2,1)} async-done(((bf16[128,512]{1,0:T(8,128)(2,1)}), bf16[1024,512]{1,0:T(8,128)(2,1)}) %all-gather.5.cloned.1.call-update) | async-done | bytes 1048592 | tf_op jit(solution)/shard_map/all_gather | solution.py:149
  89.9 1.1 fusion.76
  91.0 1.0 pad_maximum_fusion.2
  92.0 0.1 fusion.42
  92.2 0.1 fusion.40
  92.3 0.5 convolution_convert_fusion.1
  92.8 0.1 fusion.38
  92.9 0.5 convolution_convert_fusion
  93.5 1.9 collective-permute-start.4
  95.4 0.1 fusion.36.normed_ref
  95.6 1.5 collective-permute-done.4
  97.2 0.3 convert_reduce_fusion
  97.5 0.1 select_reduce_fusion
  97.7 0.1 pad_maximum_fusion.3
  97.8 0.3 fusion.80
  98.1 0.1 fusion.77
  98.2 0.3 fusion.52
  98.5 0.8 fusion.47
  99.3 7.4 %collective-permute-start.5 = (bf16[128,128]{1,0:T(8,128)(2,1)S(1)}, bf16[128,128]{1,0:T(8,128)(2,1)S(1)}, u32[]{:S(2)}, u32[]{:S(2)}) collective-permute-start(bf16[128,128]{1,0:T(8,128)(2,1)S(1)} %get-tuple-element.12), channel_id=1, source_target_pairs={{0,64},{4,68},{8,72},{12,76},{16,80},{20,84},{24,88},{28,92},{32,9... | collective-permute-start | bytes 98312 | tf_op jit(solution)/shard_map/ppermute | solution.py:199
  106.7 3.3 %collective-permute-done.5 = bf16[128,128]{1,0:T(8,128)(2,1)S(1)} collective-permute-done((bf16[128,128]{1,0:T(8,128)(2,1)S(1)}, bf16[128,128]{1,0:T(8,128)(2,1)S(1)}, u32[]{:S(2)}, u32[]{:S(2)}) %collective-permute-start.5) | collective-permute-done | bytes 32800 | tf_op jit(solution)/shard_map/ppermute | solution.py:199
  109.9 0.1 broadcast_select_fusion.3
  110.0 1.2 broadcast_in_dim.92
  111.2 8.2 %all-to-all-start.1 = ((bf16[32,128,128]{2,1,0:T(8,128)(2,1)}), bf16[32,128,128]{2,1,0:T(8,128)(2,1)S(1)}, u32[]{:S(2)}, u32[]{:S(2)}) async-start(bf16[32,128,128]{2,1,0:T(8,128)(2,1)} %bitcast.18), calls=%async_computation.1 | async-start | bytes 2097152 | tf_op jit(solution)/shard_map/all_to_all | solution.py:203
  119.4 4.3 %collective-permute-start.6 = (bf16[128,128]{1,0:T(8,128)(2,1)S(1)}, bf16[128,128]{1,0:T(8,128)(2,1)S(1)}, u32[]{:S(2)}, u32[]{:S(2)}) collective-permute-start(bf16[128,128]{1,0:T(8,128)(2,1)S(1)} %get-tuple-element.12), channel_id=1, source_target_pairs={{0,2},{1,3},{2,0},{3,1},{4,6},{5,7},{6,4},{7,5},{8,10},{9,11},{10,... | collective-permute-start | bytes 98312 | tf_op jit(solution)/shard_map/ppermute | solution.py:204
  123.7 3.4 %collective-permute-start.7 = (bf16[128,128]{1,0:T(8,128)(2,1)S(1)}, bf16[128,128]{1,0:T(8,128)(2,1)S(1)}, u32[]{:S(2)}, u32[]{:S(2)}) collective-permute-start(bf16[128,128]{1,0:T(8,128)(2,1)S(1)} %get-tuple-element.12), channel_id=1, source_target_pairs={{0,1},{1,2},{2,3},{3,0},{4,5},{5,6},{6,7},{7,4},{8,9},{9,10},{10,1... | collective-permute-start | bytes 98312 | tf_op jit(solution)/shard_map/ppermute | solution.py:204
  127.1 4.3 %collective-permute-start.8 = (bf16[128,128]{1,0:T(8,128)(2,1)S(1)}, bf16[128,128]{1,0:T(8,128)(2,1)S(1)}, u32[]{:S(2)}, u32[]{:S(2)}) collective-permute-start(bf16[128,128]{1,0:T(8,128)(2,1)S(1)} %get-tuple-element.12), channel_id=1, source_target_pairs={{0,3},{1,0},{2,1},{3,2},{4,7},{5,4},{6,5},{7,6},{8,11},{9,8},{10,9... | collective-permute-start | bytes 98312 | tf_op jit(solution)/shard_map/ppermute | solution.py:204
  131.4 14.7 %collective-permute-done.6 = bf16[128,128]{1,0:T(8,128)(2,1)S(1)} collective-permute-done((bf16[128,128]{1,0:T(8,128)(2,1)S(1)}, bf16[128,128]{1,0:T(8,128)(2,1)S(1)}, u32[]{:S(2)}, u32[]{:S(2)}) %collective-permute-start.6) | collective-permute-done | bytes 32800 | tf_op jit(solution)/shard_map/ppermute | solution.py:204
  146.2 2.4 %all-to-all-done.1 = bf16[32,128,128]{2,1,0:T(8,128)(2,1)S(1)} async-done(((bf16[32,128,128]{2,1,0:T(8,128)(2,1)}), bf16[32,128,128]{2,1,0:T(8,128)(2,1)S(1)}, u32[]{:S(2)}, u32[]{:S(2)}) %all-to-all-start.1) | async-done | bytes 1048608 | tf_op jit(solution)/shard_map/all_to_all | solution.py:203
  148.6 1.3 broadcast_select_fusion
  149.9 1.9 collective-permute-start.9
  151.8 0.1 pad_add_fusion
  151.9 0.1 add_bitcast_fusion
  152.0 0.6 copy.33
  152.6 0.6 iota_add_fusion.token_ref
  153.3 0.1 copy.28
  153.4 0.6 add_maximum_fusion.first_ref
  154.0 4.4 %queries.1.queries_ref = bf16[128,512]{1,0:T(8,128)(2,1)} custom-call(bf16[8,128,320]{2,1,0:T(8,128)(2,1)} %copy-done.4, f32[128,128]{1,0:T(8,128)} %get-tuple-element.28.cosine_ref, f32[128,128]{1,0:T(8,128)} %get-tuple-element.13.sine_ref, bf16[8,640,512]{2,1,0:T(8,128)(2,1)} %bitcast.76), custom_call_target="tpu_custom_call" | custom-call | tf_op jit(solution)/shard_map/queries/pallas_call | solution.py:219
  158.4 1.0 copy-done.3
  159.4 5.8 %attend.1 = bf16[4,128,640]{2,1,0:T(8,128)(2,1)} custom-call(bf16[128,512]{1,0:T(8,128)(2,1)} %queries.1.queries_ref, bf16[8,4,128,128]{3,2,1,0:T(8,128)(2,1)} %bitcast.79, bf16[8,4,128,128]{3,2,1,0:T(8,128)(2,1)} %copy-done.3, bf16[4,128,128]{2,1,0:T(8,128)(2,1)} %copy-done.2, s32[1,2176]{1,0:T(1,128)} %bitcast.93, s32[128,1]{1,0:T(8,128)} %iota_add_fusion.token_ref, ...), custom_call_target="tpu_custom_call" | custom-call | tf_op jit(solution)/shard_map/attend/pallas_call | solution.py:228
  165.2 3.5 %all-to-all-start.2 = ((bf16[4,128,640]{2,1,0:T(8,128)(2,1)}), bf16[4,128,640]{2,1,0:T(8,128)(2,1)S(1)}, u32[]{:S(2)}, u32[]{:S(2)}) async-start(bf16[4,128,640]{2,1,0:T(8,128)(2,1)} %attend.1), calls=%async_computation.2 | async-start | bytes 1310720 | tf_op jit(solution)/shard_map/all_to_all | solution.py:237
  168.7 0.7 pad_maximum_fusion.5
  169.3 17.5 %all-to-all-done.2 = bf16[4,128,640]{2,1,0:T(8,128)(2,1)S(1)} async-done(((bf16[4,128,640]{2,1,0:T(8,128)(2,1)}), bf16[4,128,640]{2,1,0:T(8,128)(2,1)S(1)}, u32[]{:S(2)}, u32[]{:S(2)}) %all-to-all-start.2) | async-done | bytes 655392 | tf_op jit(solution)/shard_map/all_to_all | solution.py:237
  186.9 0.4 fusion.27
  187.2 0.4 convolution_add_fusion.2
  187.6 0.4 convolution_add_fusion.1
  188.0 1.0 fusion.22
  (53 shorter events, 0.6 us)
Async XLA Ops:
  7.2 12.9 %copy-start = (bf16[20,512]{1,0:T(8,128)(2,1)S(1)}, bf16[20,512]{1,0:T(8,128)(2,1)}, u32[]{:S(2)}) copy-start(bf16[20,512]{1,0:T(8,128)(2,1)} %param.10) | copy-start | bytes 61444
  7.2 39.1 %collective-permute-start.1 = (bf16[128,640]{1,0:T(8,128)(2,1)}, bf16[128,640]{1,0:T(8,128)(2,1)S(1)}, u32[]{:S(2)}, u32[]{:S(2)}) collective-permute-start(bf16[128,640]{1,0:T(8,128)(2,1)} %param.6), channel_id=1, source_target_pairs={{0,2},{1,3},{2,0},{3,1},{4,6},{5,7},{6,4},{7,5},{8,10},{9,11},{10,... | collective-permute-start | bytes 491528 | tf_op jit(solution)/shard_map/ppermute | solution.py:138
  11.7 34.6 %collective-permute-start.2 = (bf16[128,640]{1,0:T(8,128)(2,1)}, bf16[128,640]{1,0:T(8,128)(2,1)S(1)}, u32[]{:S(2)}, u32[]{:S(2)}) collective-permute-start(bf16[128,640]{1,0:T(8,128)(2,1)} %param.6), channel_id=1, source_target_pairs={{0,1},{1,2},{2,3},{3,0},{4,5},{5,6},{6,7},{7,4},{8,9},{9,10},{10,1... | collective-permute-start | bytes 491528 | tf_op jit(solution)/shard_map/ppermute | solution.py:138
  15.2 31.2 %collective-permute-start.3 = (bf16[128,640]{1,0:T(8,128)(2,1)}, bf16[128,640]{1,0:T(8,128)(2,1)S(1)}, u32[]{:S(2)}, u32[]{:S(2)}) collective-permute-start(bf16[128,640]{1,0:T(8,128)(2,1)} %param.6), channel_id=1, source_target_pairs={{0,3},{1,0},{2,1},{3,2},{4,7},{5,4},{6,5},{7,6},{8,11},{9,8},{10,9... | collective-permute-start | bytes 491528 | tf_op jit(solution)/shard_map/ppermute | solution.py:138
  20.8 25.5 %copy-start.5 = (bf16[128,640]{1,0:T(8,128)(2,1)S(1)}, bf16[128,640]{1,0:T(8,128)(2,1)}, u32[]{:S(2)}) copy-start(bf16[128,640]{1,0:T(8,128)(2,1)} %param.6) | copy-start | bytes 491524
  20.8 10.5 %collective-permute-start = (bf16[64,512]{1,0:T(8,128)(2,1)S(1)}, bf16[64,512]{1,0:T(8,128)(2,1)S(1)}, u32[]{:S(2)}, u32[]{:S(2)}) collective-permute-start(bf16[64,512]{1,0:T(8,128)(2,1)S(1)} %fusion.44), channel_id=1, source_target_pairs={{0,64},{64,0},{1,65},{65,1},{2,66},{66,2},{3,67},{67,3},{4,68},{68... | collective-permute-start | bytes 196616 | tf_op jit(solution)/shard_map/ppermute | solution.py:134
  33.0 60.6 %all-to-all-start = ((bf16[32,48,128]{2,1,0:T(8,128)(2,1)}), bf16[32,48,128]{2,1,0:T(8,128)(2,1)S(1)}, u32[]{:S(2)}, u32[]{:S(2)}) async-start(bf16[32,48,128]{2,1,0:T(8,128)(2,1)} %broadcast_in_dim.53), calls=%async_computation | async-start | bytes 786432 | tf_op jit(solution)/shard_map/all_to_all | solution.py:36
  45.5 44.4 %all-gather.5.cloned.1.call-start = ((), (), s32[]{:S(2)}) async-start(), calls=%async_computation.3 | async-start | bytes 1179648 | tf_op jit(solution)/shard_map/all_gather | solution.py:149
  46.3 107.7 %all-gather.7.cloned.1.call-start = ((), (), s32[]{:S(2)}) async-start(), calls=%async_computation.4 | async-start | bytes 5898240 | tf_op jit(solution)/shard_map/all_gather | solution.py:158
  93.5 4.1 %copy-start.6 = (s32[128]{0:T(128)S(1)}, s32[128]{0:T(128)}, u32[]{:S(2)}) copy-start(s32[128]{0:T(128)} %param.7) | copy-start | bytes 1540
  93.5 3.6 %collective-permute-start.4 = (bf16[32,48,128]{2,1,0:T(8,128)(2,1)S(1)}, bf16[32,48,128]{2,1,0:T(8,128)(2,1)S(1)}, u32[]{:S(2)}, u32[]{:S(2)}) collective-permute-start(bf16[32,48,128]{2,1,0:T(8,128)(2,1)S(1)} %all-to-all-done), channel_id=1, source_target_pairs={{0,4},{4,0},{1,5},{5,1},{2,6},{6,2},{3,7},{7,3},{8,12},{12,8},{9,1... | collective-permute-start | bytes 1179656 | tf_op jit(solution)/shard_map/ppermute | solution.py:144
  95.5 2.2 %copy-start.4 = (bf16[8,128,320]{2,1,0:T(8,128)(2,1)}, bf16[8,128,320]{2,1,0:T(8,128)(2,1)S(1)}, u32[]{:S(2)}) copy-start(bf16[8,128,320]{2,1,0:T(8,128)(2,1)S(1)} %fusion.36.normed_ref) | copy-start | bytes 1966084
  99.3 10.6 %collective-permute-start.5 = (bf16[128,128]{1,0:T(8,128)(2,1)S(1)}, bf16[128,128]{1,0:T(8,128)(2,1)S(1)}, u32[]{:S(2)}, u32[]{:S(2)}) collective-permute-start(bf16[128,128]{1,0:T(8,128)(2,1)S(1)} %get-tuple-element.12), channel_id=1, source_target_pairs={{0,64},{4,68},{8,72},{12,76},{16,80},{20,84},{24,88},{28,92},{32,9... | collective-permute-start | bytes 98312 | tf_op jit(solution)/shard_map/ppermute | solution.py:199
  111.2 37.4 %all-to-all-start.1 = ((bf16[32,128,128]{2,1,0:T(8,128)(2,1)}), bf16[32,128,128]{2,1,0:T(8,128)(2,1)S(1)}, u32[]{:S(2)}, u32[]{:S(2)}) async-start(bf16[32,128,128]{2,1,0:T(8,128)(2,1)} %bitcast.18), calls=%async_computation.1 | async-start | bytes 2097152 | tf_op jit(solution)/shard_map/all_to_all | solution.py:203
  119.4 26.7 %collective-permute-start.6 = (bf16[128,128]{1,0:T(8,128)(2,1)S(1)}, bf16[128,128]{1,0:T(8,128)(2,1)S(1)}, u32[]{:S(2)}, u32[]{:S(2)}) collective-permute-start(bf16[128,128]{1,0:T(8,128)(2,1)S(1)} %get-tuple-element.12), channel_id=1, source_target_pairs={{0,2},{1,3},{2,0},{3,1},{4,6},{5,7},{6,4},{7,5},{8,10},{9,11},{10,... | collective-permute-start | bytes 98312 | tf_op jit(solution)/shard_map/ppermute | solution.py:204
  123.7 22.4 %collective-permute-start.7 = (bf16[128,128]{1,0:T(8,128)(2,1)S(1)}, bf16[128,128]{1,0:T(8,128)(2,1)S(1)}, u32[]{:S(2)}, u32[]{:S(2)}) collective-permute-start(bf16[128,128]{1,0:T(8,128)(2,1)S(1)} %get-tuple-element.12), channel_id=1, source_target_pairs={{0,1},{1,2},{2,3},{3,0},{4,5},{5,6},{6,7},{7,4},{8,9},{9,10},{10,1... | collective-permute-start | bytes 98312 | tf_op jit(solution)/shard_map/ppermute | solution.py:204
  127.1 19.0 %collective-permute-start.8 = (bf16[128,128]{1,0:T(8,128)(2,1)S(1)}, bf16[128,128]{1,0:T(8,128)(2,1)S(1)}, u32[]{:S(2)}, u32[]{:S(2)}) collective-permute-start(bf16[128,128]{1,0:T(8,128)(2,1)S(1)} %get-tuple-element.12), channel_id=1, source_target_pairs={{0,3},{1,0},{2,1},{3,2},{4,7},{5,4},{6,5},{7,6},{8,11},{9,8},{10,9... | collective-permute-start | bytes 98312 | tf_op jit(solution)/shard_map/ppermute | solution.py:204
  146.2 12.2 %copy-start.2 = (bf16[4,128,128]{2,1,0:T(8,128)(2,1)}, bf16[4,128,128]{2,1,0:T(8,128)(2,1)S(1)}, u32[]{:S(2)}) copy-start(bf16[4,128,128]{2,1,0:T(8,128)(2,1)S(1)} %pad_maximum_fusion.4.own_ref) | copy-start | bytes 393220
  148.6 9.8 %copy-start.1 = (bf16[32,128,128]{2,1,0:T(8,128)(2,1)}, bf16[32,128,128]{2,1,0:T(8,128)(2,1)S(1)}, u32[]{:S(2)}) copy-start(bf16[32,128,128]{2,1,0:T(8,128)(2,1)S(1)} %all-to-all-done.1) | copy-start | bytes 3145732
  149.9 8.5 %collective-permute-start.9 = (bf16[8,4,128,128]{3,2,1,0:T(8,128)(2,1)}, bf16[8,4,128,128]{3,2,1,0:T(8,128)(2,1)S(1)}, u32[]{:S(2)}, u32[]{:S(2)}) collective-permute-start(bf16[8,4,128,128]{3,2,1,0:T(8,128)(2,1)} %broadcast_select_fusion), channel_id=1, source_target_pairs={{0,4},{4,0},{1,5},{5,1},{2,6},{6,2},{3,7},{7,3},{8,12},{12,8},{9,1... | collective-permute-start | bytes 3145736 | tf_op jit(solution)/shard_map/ppermute | solution.py:208
  158.4 1.0 copy-start.3
  165.2 21.7 %all-to-all-start.2 = ((bf16[4,128,640]{2,1,0:T(8,128)(2,1)}), bf16[4,128,640]{2,1,0:T(8,128)(2,1)S(1)}, u32[]{:S(2)}, u32[]{:S(2)}) async-start(bf16[4,128,640]{2,1,0:T(8,128)(2,1)} %attend.1), calls=%async_computation.2 | async-start | bytes 1310720 | tf_op jit(solution)/shard_map/all_to_all | solution.py:237
Sparse Core Ops, SparseCore 0:
  49.0 40.8 all-gather.4
  92.1 39.6 all-gather.6

commit v3 on v2

--- a/solution.py
+++ b/solution.py
@@ -129,67 +129,34 @@
 
     share = 2 * HD // nx
     ids = jnp.pad(seg_ids.astype(bf)[None, :], ((0, 3), (0, 0)))
-    kv_own = jnp.concatenate([lax.dynamic_slice_in_dim(w_keyval, it * share, share, 1), ids], axis=0)
-    own = jnp.concatenate([w_query, w_out.T, jnp.pad(kv_own, ((0, 0), (0, cols - share)))], axis=0)
-    other = lax.ppermute(own, "yh", both)
-    low = jnp.where(iy == 0, own, other)
-    high = jnp.where(iy == 0, other, own)
+    kv_slab = jnp.concatenate([lax.dynamic_slice_in_dim(w_keyval, it * share, share, 1), ids], axis=0)
+    kv_core = spread(kv_slab, ("x", "yh", "z"), nx * ny * nz)
+    kv_twin = lax.ppermute(kv_core, "c", both)
 
     others = [lax.ppermute(tokens, "tp", [(i, (i + k) % nx) for i in range(nx)]) for k in range(1, nx)]
 
-    w_at, id_at = slice(2 * rows, 3 * rows), slice(3 * rows, 3 * rows + 1)
-    kv_pair = jnp.concatenate([low[w_at], high[w_at], low[id_at], high[id_at]], axis=0)[:, :share]
-    kv_pair = jnp.pad(kv_pair, ((0, -kv_pair.shape[0] % 8), (0, 0)))
-    kv_core = spread(kv_pair, ("x", "z"), nx * nz)
-    kv_twin = lax.ppermute(kv_core, "c", both)
-
-    qo_pair = jnp.concatenate([low[:rows], high[:rows], low[rows : 2 * rows], high[rows : 2 * rows]], axis=0)
+    qo_own = jnp.concatenate([w_query, w_out.T], axis=0)
+    qo_other = lax.ppermute(qo_own, "yh", both)
+    low = jnp.where(iy == 0, qo_own, qo_other)
+    high = jnp.where(iy == 0, qo_other, qo_own)
+    qo_pair = jnp.concatenate([low[:rows], high[:rows], low[rows:], high[rows:]], axis=0)
     least = (1 << 20) // (2 * nz * cols)
     qo_pair = jnp.pad(qo_pair, ((0, max(0, least - qo_pair.shape[0])), (0, 0)))
     qo_near = lax.all_gather(qo_pair, "z", axis=0, tiled=False)
-    part = nz * ny * rows
-    qo_send = jnp.concatenate(
-        [
-            qo_near[:, : ny * rows].reshape(part, cols),
-            qo_near[:, ny * rows : 2 * ny * rows].reshape(part, cols),
-        ],
-        axis=0,
-    )
-    qo_all = lax.all_gather(qo_send, ("x", "c"), axis=0, tiled=False)
-    kv_twin = after(kv_twin, qo_send)
-
     groups = in_order([tokens, *others], it)
     normed = rms_norm(jnp.concatenate(groups, axis=1), norm_gain)
-    perm = natural_to_gathered(shard, rows, ny, nz)
-    reordered = jnp.concatenate(
-        [
-            jnp.dot(normed[:, g * shard : (g + 1) * shard], perm, preferred_element_type=jnp.float32).astype(bf)
-            for g in range(nx)
-        ],
-        axis=1,
-    )
-    blocks = jnp.stack([reordered[:, i * part : (i + 1) * part] for i in range(nx * nc)])
-    kv_core, reordered, blocks, perm = lax.optimization_barrier((kv_core, reordered, blocks, perm))
 
     kv_zero = jnp.where(ic == 0, kv_core, kv_twin)
     kv_one = jnp.where(ic == 0, kv_twin, kv_core)
-    all_ids = jnp.concatenate(
-        [kv[:, ny * rows : ny * rows + ny] for kv in (kv_core, kv_twin)], axis=0
-    ).astype(jnp.int32)
+    all_ids = jnp.concatenate([kv_core[:, rows], kv_twin[:, rows]], axis=0).astype(jnp.int32)
     labels = jnp.arange(SEGS, dtype=jnp.int32)
     starts = jnp.sum((all_ids.reshape(-1)[None, :] < labels[:, None]).astype(jnp.int32), axis=1)
     own_start = jnp.sum(jnp.where(seg_ids[:, None] == labels[None, :], starts[None, :], 0), axis=1)
     token_index = my_index * tok + jnp.arange(tok, dtype=jnp.int32)
     cosine, sine = angles((token_index - own_start).astype(jnp.float32))
 
-    kv_rows = jnp.stack(
-        [
-            kv[:, : ny * rows].reshape(nx, part, share)
-            for kv in (kv_zero, kv_one)
-        ],
-        axis=1,
-    ).reshape(nx * nc * part, share)
-    kv_raw = jnp.dot(reordered, kv_rows, preferred_element_type=jnp.float32)
+    kv_rows = jnp.stack([kv_zero[:, :rows], kv_one[:, :rows]], axis=1).reshape(nx * shard, share)
+    kv_raw = jnp.dot(normed, kv_rows, preferred_element_type=jnp.float32)
     quarter = HD // 4
     swapped = jnp.concatenate([kv_raw[:, quarter:], kv_raw[:, :quarter]], axis=1)
     kv_share = jnp.where(it == 0, kv_raw * cosine + swapped * sine, kv_raw).astype(bf)
@@ -206,6 +173,23 @@
     kv_cache = jnp.concatenate(list(own_kv), axis=1)
     at_self = (chips == iz)[:, None, None, None] & (ic == 0)
     partner = lax.ppermute(jnp.where(at_self, own_kv[None], mine), "c", both)
+    part = nz * ny * rows
+    qo_near = after(qo_near, to_send)
+    qo_send = jnp.concatenate(
+        [
+            qo_near[:, : ny * rows].reshape(part, cols),
+            qo_near[:, ny * rows : 2 * ny * rows].reshape(part, cols),
+        ],
+        axis=0,
+    )
+    qo_all = lax.all_gather(qo_send, ("x", "c"), axis=0, tiled=False)
+    perm = natural_to_gathered(shard, rows, ny, nz)
+    normed = after(normed, to_send)
+    blocks = []
+    for g in range(nx):
+        turned = jnp.dot(normed[:, g * shard : (g + 1) * shard], perm, preferred_element_type=jnp.float32)
+        blocks += [turned[:, :part].astype(bf), turned[:, part:].astype(bf)]
+    blocks = jnp.stack(blocks)
     block_of_mine = my_block - (chips >= iz).astype(jnp.int32)
     block_of_partner = my_block - jnp.where(ic == 1, chips > iz, chips >= iz).astype(jnp.int32)
     first_of_mine = ((block_of_mine * nz + chips) * nc + ic) * tok

time: 197 us -> 186 us (0.944)
  the two profiles are of different devices: /device:TPU:66 before, /device:TPU:1 now
where the time goes in v3:
time: 186 us; the launch traced here: 185 us
  starting transfers between devices  70.9 us (38%)
  waiting for transfers between devices  64.7 us (35%)
  between operations  14.6 us (8%)
  local copies, waits for them, and re-layouts  10.2 us (5%)
  Pallas kernels  10.2 us (5%)
  other arithmetic  9.72 us (5%)
  matrix products  5.04 us (3%)
    all_gather x1, waiting for transfers between devices, per_device(): qo_near = lax.all_gather(qo_pair, 'z', axis=0, tiled=False)  21.2 us
    all_to_all x1, waiting for transfers between devices, per_device(): lax.all_to_all(to_send, ('z', 'tp'), 0, 0, tiled=True)  20.5 us
    all_to_all x1, starting transfers between devices, spread(): return lax.all_to_all(copies, axes, 0, 0, tiled=True)  17 us
    all_to_all x1, waiting for transfers between devices, per_device(): received = lax.all_to_all(partial, 'tp', 0, 0, tiled=True)  16.4 us
    ppermute x3, starting transfers between devices, per_device(): lax.ppermute(tokens, 'tp', [(i, (i + k) % nx) for i in range(nx)])  12.2 us
    ppermute x3, starting transfers between devices, per_device(): lax.ppermute(kv_share, 'tp', [(i, (i + k) % nx) for i in range(nx)])  11.1 us
    ppermute x1, starting transfers between devices, per_device(): kv_twin = lax.ppermute(kv_core, 'c', both)  7.33 us
    ppermute x1, starting transfers between devices, per_device(): qo_other = lax.ppermute(qo_own, 'yh', both)  6.83 us
  transfers between devices with their start and end apart: 15, of which 7 were waited for; matrix products, arithmetic and copies ran while one was open for 10% of the time, Pallas kernels for 2%

profile of v3, /device:TPU:1, one launch (start us, length us, event | category | flops | bytes accessed | tf_op | source)
XLA Modules:
  0.0 185.3 jit_solution(4815798946058266198)
XLA Ops:
  7.2 5.2 %collective-permute-start = (bf16[128,640]{1,0:T(8,128)(2,1)}, bf16[128,640]{1,0:T(8,128)(2,1)S(1)}, u32[]{:S(2)}, u32[]{:S(2)}) collective-permute-start(bf16[128,640]{1,0:T(8,128)(2,1)} %param.6), channel_id=1, source_target_pairs={{0,2},{1,3},{2,0},{3,1},{4,6},{5,7},{6,4},{7,5},{8,10},{9,11},{10,... | collective-permute-start | bytes 491528 | tf_op jit(solution)/shard_map/ppermute | solution.py:136
  12.4 3.2 %collective-permute-start.1 = (bf16[128,640]{1,0:T(8,128)(2,1)}, bf16[128,640]{1,0:T(8,128)(2,1)S(1)}, u32[]{:S(2)}, u32[]{:S(2)}) collective-permute-start(bf16[128,640]{1,0:T(8,128)(2,1)} %param.6), channel_id=1, source_target_pairs={{0,1},{1,2},{2,3},{3,0},{4,5},{5,6},{6,7},{7,4},{8,9},{9,10},{10,1... | collective-permute-start | bytes 491528 | tf_op jit(solution)/shard_map/ppermute | solution.py:136
  15.6 3.9 %collective-permute-start.2 = (bf16[128,640]{1,0:T(8,128)(2,1)}, bf16[128,640]{1,0:T(8,128)(2,1)S(1)}, u32[]{:S(2)}, u32[]{:S(2)}) collective-permute-start(bf16[128,640]{1,0:T(8,128)(2,1)} %param.6), channel_id=1, source_target_pairs={{0,3},{1,0},{2,1},{3,2},{4,7},{5,4},{6,5},{7,6},{8,11},{9,8},{10,9... | collective-permute-start | bytes 491528 | tf_op jit(solution)/shard_map/ppermute | solution.py:136
  19.5 0.7 convert_bitcast_fusion
  20.1 0.8 broadcast_in_dim.60
  20.9 17.0 %all-to-all-start = ((bf16[64,24,128]{2,1,0:T(8,128)(2,1)}), bf16[64,24,128]{2,1,0:T(8,128)(2,1)S(1)}, u32[]{:S(2)}, u32[]{:S(2)}) async-start(bf16[64,24,128]{2,1,0:T(8,128)(2,1)} %broadcast_in_dim.60), calls=%async_computation | async-start | bytes 786432 | tf_op jit(solution)/shard_map/all_to_all | solution.py:36
  38.0 0.8 pad_maximum_fusion.7
  38.7 6.8 %collective-permute-start.5 = (bf16[40,512]{1,0:T(8,128)(2,1)S(1)}, bf16[40,512]{1,0:T(8,128)(2,1)S(1)}, u32[]{:S(2)}, u32[]{:S(2)}) collective-permute-start(bf16[40,512]{1,0:T(8,128)(2,1)S(1)} %pad_maximum_fusion.7), channel_id=1, source_target_pairs={{0,64},{64,0},{1,65},{65,1},{2,66},{66,2},{3,67},{67,3},{4,68},{68... | collective-permute-start | bytes 122888 | tf_op jit(solution)/shard_map/ppermute | solution.py:139
  45.7 0.7 convert_element_type.62
  46.4 3.6 %collective-permute-done.5 = bf16[40,512]{1,0:T(8,128)(2,1)S(1)} collective-permute-done((bf16[40,512]{1,0:T(8,128)(2,1)S(1)}, bf16[40,512]{1,0:T(8,128)(2,1)S(1)}, u32[]{:S(2)}, u32[]{:S(2)}) %collective-permute-start.5) | collective-permute-done | bytes 40992 | tf_op jit(solution)/shard_map/ppermute | solution.py:139
  50.0 0.8 broadcast_select_fusion.3
  50.8 0.7 fusion.34
  51.6 0.1 select_select_fusion.3
  51.7 0.2 fusion.18
  51.9 0.8 all-to-all-done
  52.8 7.3 %collective-permute-start.3 = (bf16[64,24,128]{2,0,1:T(8,128)(2,1)S(1)}, bf16[64,24,128]{2,0,1:T(8,128)(2,1)S(1)}, u32[]{:S(2)}, u32[]{:S(2)}) collective-permute-start(bf16[64,24,128]{2,0,1:T(8,128)(2,1)S(1)} %copy.43), channel_id=1, source_target_pairs={{0,4},{4,0},{1,5},{5,1},{2,6},{6,2},{3,7},{7,3},{8,12},{12,8},{9,1... | collective-permute-start | bytes 1179656 | tf_op jit(solution)/shard_map/ppermute | solution.py:134
  60.1 0.2 fusion.20
  60.4 1.1 collective-permute-done.3
  61.6 0.4 copy.45
  62.0 0.1 reshape.108
  62.2 0.3 convert_reduce_fusion
  62.5 0.1 select_reduce_fusion
  62.6 0.3 fusion.75
  63.0 0.3 fusion.47
  63.3 0.8 fusion.45
  64.0 3.0 %collective-permute-start.4 = (bf16[128,128]{1,0:T(8,128)(2,1)S(1)}, bf16[128,128]{1,0:T(8,128)(2,1)S(1)}, u32[]{:S(2)}, u32[]{:S(2)}) collective-permute-start(bf16[128,128]{1,0:T(8,128)(2,1)S(1)} %get-tuple-element.6), channel_id=1, source_target_pairs={{0,64},{4,68},{8,72},{12,76},{16,80},{20,84},{24,88},{28,92},{32,9... | collective-permute-start | bytes 98312 | tf_op jit(solution)/shard_map/ppermute | solution.py:166
  67.0 1.0 collective-permute-done.4
  68.0 0.1 broadcast_select_fusion.1
  68.1 21.2 %all-gather.5.cloned.1.call-done = bf16[1024,512]{1,0:T(8,128)(2,1)} async-done(((bf16[128,512]{1,0:T(8,128)(2,1)}), bf16[1024,512]{1,0:T(8,128)(2,1)}) %all-gather.5.cloned.1.call-update) | async-done | bytes 1048592 | tf_op jit(solution)/shard_map/all_gather | solution.py:145
  89.4 1.2 broadcast_in_dim.92
  90.6 0.1 copy-done.4
  90.8 1.0 pad_maximum_fusion.2
  91.9 0.6 copy.57
  92.6 4.0 %collective-permute-start.6 = (bf16[128,128]{1,0:T(8,128)(2,1)S(1)}, bf16[128,128]{1,0:T(8,128)(2,1)S(1)}, u32[]{:S(2)}, u32[]{:S(2)}) collective-permute-start(bf16[128,128]{1,0:T(8,128)(2,1)S(1)} %get-tuple-element.6), channel_id=1, source_target_pairs={{0,2},{1,3},{2,0},{3,1},{4,6},{5,7},{6,4},{7,5},{8,10},{9,11},{10,... | collective-permute-start | bytes 98312 | tf_op jit(solution)/shard_map/ppermute | solution.py:171
  96.6 3.1 %collective-permute-start.7 = (bf16[128,128]{1,0:T(8,128)(2,1)S(1)}, bf16[128,128]{1,0:T(8,128)(2,1)S(1)}, u32[]{:S(2)}, u32[]{:S(2)}) collective-permute-start(bf16[128,128]{1,0:T(8,128)(2,1)S(1)} %get-tuple-element.6), channel_id=1, source_target_pairs={{0,1},{1,2},{2,3},{3,0},{4,5},{5,6},{6,7},{7,4},{8,9},{9,10},{10,1... | collective-permute-start | bytes 98312 | tf_op jit(solution)/shard_map/ppermute | solution.py:171
  99.8 4.0 %collective-permute-start.8 = (bf16[128,128]{1,0:T(8,128)(2,1)S(1)}, bf16[128,128]{1,0:T(8,128)(2,1)S(1)}, u32[]{:S(2)}, u32[]{:S(2)}) collective-permute-start(bf16[128,128]{1,0:T(8,128)(2,1)S(1)} %get-tuple-element.6), channel_id=1, source_target_pairs={{0,3},{1,0},{2,1},{3,2},{4,7},{5,4},{6,5},{7,6},{8,11},{9,8},{10,9... | collective-permute-start | bytes 98312 | tf_op jit(solution)/shard_map/ppermute | solution.py:171
  103.7 0.1 copy.52
  103.9 0.7 add_maximum_fusion
  104.5 4.7 %all-to-all-start.1 = ((bf16[32,128,128]{2,1,0:T(8,128)(2,1)}), bf16[32,128,128]{2,1,0:T(8,128)(2,1)S(1)}, u32[]{:S(2)}, u32[]{:S(2)}) async-start(bf16[32,128,128]{2,1,0:T(8,128)(2,1)} %bitcast.6), calls=%async_computation.1 | async-start | bytes 2097152 | tf_op jit(solution)/shard_map/all_to_all | solution.py:170
  109.3 0.5 convolution_convert_fusion.3
  109.9 0.5 convolution_convert_fusion.2
  110.4 0.6 fusion.42
  111.1 0.7 fusion.41
  111.8 0.7 fusion.40
  112.5 0.7 fusion.39
  113.2 0.5 convolution_convert_fusion.1
  113.8 0.7 fusion.38
  114.4 0.8 fusion.37
  115.2 20.5 %all-to-all-done.1 = bf16[32,128,128]{2,1,0:T(8,128)(2,1)S(1)} async-done(((bf16[32,128,128]{2,1,0:T(8,128)(2,1)}), bf16[32,128,128]{2,1,0:T(8,128)(2,1)S(1)}, u32[]{:S(2)}, u32[]{:S(2)}) %all-to-all-start.1) | async-done | bytes 1048608 | tf_op jit(solution)/shard_map/all_to_all | solution.py:170
  135.7 1.3 broadcast_select_fusion
  137.0 4.6 %collective-permute-start.9 = (bf16[8,4,128,128]{3,2,1,0:T(8,128)(2,1)}, bf16[8,4,128,128]{3,2,1,0:T(8,128)(2,1)S(1)}, u32[]{:S(2)}, u32[]{:S(2)}) collective-permute-start(bf16[8,4,128,128]{3,2,1,0:T(8,128)(2,1)} %broadcast_select_fusion), channel_id=1, source_target_pairs={{0,4},{4,0},{1,5},{5,1},{2,6},{6,2},{3,7},{7,3},{8,12},{12,8},{9,1... | collective-permute-start | bytes 3145736 | tf_op jit(solution)/shard_map/ppermute | solution.py:175
  141.6 0.5 convolution_convert_fusion
  142.2 0.6 fusion.36
  142.8 0.8 fusion.35.normed_ref
  143.6 4.4 %queries.1.queries_ref = bf16[128,512]{1,0:T(8,128)(2,1)} custom-call(bf16[8,128,320]{2,1,0:T(8,128)(2,1)} %fusion.35.normed_ref, f32[128,128]{1,0:T(8,128)} %get-tuple-element.22.cosine_ref, f32[128,128]{1,0:T(8,128)} %get-tuple-element.7.sine_ref, bf16[8,640,512]{2,1,0:T(8,128)(2,1)} %bitcast.80), custom_call_target="tpu_custom_call" | custom-call | tf_op jit(solution)/shard_map/queries/pallas_call | solution.py:203
  148.0 1.0 copy-done.3
  148.9 5.8 %attend.1 = bf16[4,128,640]{2,1,0:T(8,128)(2,1)} custom-call(bf16[128,512]{1,0:T(8,128)(2,1)} %queries.1.queries_ref, bf16[8,4,128,128]{3,2,1,0:T(8,128)(2,1)} %bitcast.83, bf16[8,4,128,128]{3,2,1,0:T(8,128)(2,1)} %copy-done.3, bf16[4,128,128]{2,1,0:T(8,128)(2,1)} %copy-done.2, s32[1,2176]{1,0:T(1,128)} %bitcast.93, s32[128,1]{1,0:T(8,128)} %get-tuple-element.33.token_ref, ...), custom_call_target="tpu_custom_call" | custom-call | tf_op jit(solution)/shard_map/attend/pallas_call | solution.py:212
  154.7 4.0 %all-to-all-start.2 = ((bf16[4,128,640]{2,1,0:T(8,128)(2,1)}), bf16[4,128,640]{2,1,0:T(8,128)(2,1)S(1)}, u32[]{:S(2)}, u32[]{:S(2)}) async-start(bf16[4,128,640]{2,1,0:T(8,128)(2,1)} %attend.1), calls=%async_computation.2 | async-start | bytes 1310720 | tf_op jit(solution)/shard_map/all_to_all | solution.py:221
  158.8 0.7 pad_maximum_fusion.4
  159.4 16.4 %all-to-all-done.2 = bf16[4,128,640]{2,1,0:T(8,128)(2,1)S(1)} async-done(((bf16[4,128,640]{2,1,0:T(8,128)(2,1)}), bf16[4,128,640]{2,1,0:T(8,128)(2,1)S(1)}, u32[]{:S(2)}, u32[]{:S(2)}) %all-to-all-start.2) | async-done | bytes 655392 | tf_op jit(solution)/shard_map/all_to_all | solution.py:221
  175.9 0.5 fusion.27
  176.3 0.5 convolution_add_fusion.2
  176.8 0.5 convolution_add_fusion.1
  177.3 1.2 fusion.22
  (48 shorter events, 0.7 us)
Async XLA Ops:
  7.2 13.0 %copy-start = (bf16[20,512]{1,0:T(8,128)(2,1)S(1)}, bf16[20,512]{1,0:T(8,128)(2,1)}, u32[]{:S(2)}) copy-start(bf16[20,512]{1,0:T(8,128)(2,1)} %param.10) | copy-start | bytes 61444
  7.2 44.4 %copy-start.5 = (bf16[128,640]{1,0:T(8,128)(2,1)S(1)}, bf16[128,640]{1,0:T(8,128)(2,1)}, u32[]{:S(2)}) copy-start(bf16[128,640]{1,0:T(8,128)(2,1)} %param.6) | copy-start | bytes 491524
  7.2 44.3 %collective-permute-start = (bf16[128,640]{1,0:T(8,128)(2,1)}, bf16[128,640]{1,0:T(8,128)(2,1)S(1)}, u32[]{:S(2)}, u32[]{:S(2)}) collective-permute-start(bf16[128,640]{1,0:T(8,128)(2,1)} %param.6), channel_id=1, source_target_pairs={{0,2},{1,3},{2,0},{3,1},{4,6},{5,7},{6,4},{7,5},{8,10},{9,11},{10,... | collective-permute-start | bytes 491528 | tf_op jit(solution)/shard_map/ppermute | solution.py:136
  12.4 39.2 %collective-permute-start.1 = (bf16[128,640]{1,0:T(8,128)(2,1)}, bf16[128,640]{1,0:T(8,128)(2,1)S(1)}, u32[]{:S(2)}, u32[]{:S(2)}) collective-permute-start(bf16[128,640]{1,0:T(8,128)(2,1)} %param.6), channel_id=1, source_target_pairs={{0,1},{1,2},{2,3},{3,0},{4,5},{5,6},{6,7},{7,4},{8,9},{9,10},{10,1... | collective-permute-start | bytes 491528 | tf_op jit(solution)/shard_map/ppermute | solution.py:136
  15.6 36.0 %collective-permute-start.2 = (bf16[128,640]{1,0:T(8,128)(2,1)}, bf16[128,640]{1,0:T(8,128)(2,1)S(1)}, u32[]{:S(2)}, u32[]{:S(2)}) collective-permute-start(bf16[128,640]{1,0:T(8,128)(2,1)} %param.6), channel_id=1, source_target_pairs={{0,3},{1,0},{2,1},{3,2},{4,7},{5,4},{6,5},{7,6},{8,11},{9,8},{10,9... | collective-permute-start | bytes 491528 | tf_op jit(solution)/shard_map/ppermute | solution.py:136
  20.9 31.8 %all-to-all-start = ((bf16[64,24,128]{2,1,0:T(8,128)(2,1)}), bf16[64,24,128]{2,1,0:T(8,128)(2,1)S(1)}, u32[]{:S(2)}, u32[]{:S(2)}) async-start(bf16[64,24,128]{2,1,0:T(8,128)(2,1)} %broadcast_in_dim.60), calls=%async_computation | async-start | bytes 786432 | tf_op jit(solution)/shard_map/all_to_all | solution.py:36
  37.9 51.4 %all-gather.5.cloned.1.call-start = ((), (), s32[]{:S(2)}) async-start(), calls=%async_computation.3 | async-start | bytes 1179648 | tf_op jit(solution)/shard_map/all_gather | solution.py:145
  38.7 11.2 %collective-permute-start.5 = (bf16[40,512]{1,0:T(8,128)(2,1)S(1)}, bf16[40,512]{1,0:T(8,128)(2,1)S(1)}, u32[]{:S(2)}, u32[]{:S(2)}) collective-permute-start(bf16[40,512]{1,0:T(8,128)(2,1)S(1)} %pad_maximum_fusion.7), channel_id=1, source_target_pairs={{0,64},{64,0},{1,65},{65,1},{2,66},{66,2},{3,67},{67,3},{4,68},{68... | collective-permute-start | bytes 122888 | tf_op jit(solution)/shard_map/ppermute | solution.py:139
  51.5 92.1 %all-gather.7.cloned.1.call-start = ((), (), s32[]{:S(2)}) async-start(), calls=%async_computation.4 | async-start | bytes 5898240 | tf_op jit(solution)/shard_map/all_gather | solution.py:185
  52.8 8.7 %collective-permute-start.3 = (bf16[64,24,128]{2,0,1:T(8,128)(2,1)S(1)}, bf16[64,24,128]{2,0,1:T(8,128)(2,1)S(1)}, u32[]{:S(2)}, u32[]{:S(2)}) collective-permute-start(bf16[64,24,128]{2,0,1:T(8,128)(2,1)S(1)} %copy.43), channel_id=1, source_target_pairs={{0,4},{4,0},{1,5},{5,1},{2,6},{6,2},{3,7},{7,3},{8,12},{12,8},{9,1... | collective-permute-start | bytes 1179656 | tf_op jit(solution)/shard_map/ppermute | solution.py:134
  61.6 0.9 copy-start.6
  64.0 4.0 %collective-permute-start.4 = (bf16[128,128]{1,0:T(8,128)(2,1)S(1)}, bf16[128,128]{1,0:T(8,128)(2,1)S(1)}, u32[]{:S(2)}, u32[]{:S(2)}) collective-permute-start(bf16[128,128]{1,0:T(8,128)(2,1)S(1)} %get-tuple-element.6), channel_id=1, source_target_pairs={{0,64},{4,68},{8,72},{12,76},{16,80},{20,84},{24,88},{28,92},{32,9... | collective-permute-start | bytes 98312 | tf_op jit(solution)/shard_map/ppermute | solution.py:166
  89.3 1.4 copy-start.4
  92.6 16.7 %collective-permute-start.6 = (bf16[128,128]{1,0:T(8,128)(2,1)S(1)}, bf16[128,128]{1,0:T(8,128)(2,1)S(1)}, u32[]{:S(2)}, u32[]{:S(2)}) collective-permute-start(bf16[128,128]{1,0:T(8,128)(2,1)S(1)} %get-tuple-element.6), channel_id=1, source_target_pairs={{0,2},{1,3},{2,0},{3,1},{4,6},{5,7},{6,4},{7,5},{8,10},{9,11},{10,... | collective-permute-start | bytes 98312 | tf_op jit(solution)/shard_map/ppermute | solution.py:171
  96.6 12.6 %collective-permute-start.7 = (bf16[128,128]{1,0:T(8,128)(2,1)S(1)}, bf16[128,128]{1,0:T(8,128)(2,1)S(1)}, u32[]{:S(2)}, u32[]{:S(2)}) collective-permute-start(bf16[128,128]{1,0:T(8,128)(2,1)S(1)} %get-tuple-element.6), channel_id=1, source_target_pairs={{0,1},{1,2},{2,3},{3,0},{4,5},{5,6},{6,7},{7,4},{8,9},{9,10},{10,1... | collective-permute-start | bytes 98312 | tf_op jit(solution)/shard_map/ppermute | solution.py:171
  99.8 9.5 %collective-permute-start.8 = (bf16[128,128]{1,0:T(8,128)(2,1)S(1)}, bf16[128,128]{1,0:T(8,128)(2,1)S(1)}, u32[]{:S(2)}, u32[]{:S(2)}) collective-permute-start(bf16[128,128]{1,0:T(8,128)(2,1)S(1)} %get-tuple-element.6), channel_id=1, source_target_pairs={{0,3},{1,0},{2,1},{3,2},{4,7},{5,4},{6,5},{7,6},{8,11},{9,8},{10,9... | collective-permute-start | bytes 98312 | tf_op jit(solution)/shard_map/ppermute | solution.py:171
  104.5 31.2 %all-to-all-start.1 = ((bf16[32,128,128]{2,1,0:T(8,128)(2,1)}), bf16[32,128,128]{2,1,0:T(8,128)(2,1)S(1)}, u32[]{:S(2)}, u32[]{:S(2)}) async-start(bf16[32,128,128]{2,1,0:T(8,128)(2,1)} %bitcast.6), calls=%async_computation.1 | async-start | bytes 2097152 | tf_op jit(solution)/shard_map/all_to_all | solution.py:170
  111.1 24.6 %copy-start.2 = (bf16[4,128,128]{2,1,0:T(8,128)(2,1)}, bf16[4,128,128]{2,1,0:T(8,128)(2,1)S(1)}, u32[]{:S(2)}) copy-start(bf16[4,128,128]{2,1,0:T(8,128)(2,1)S(1)} %pad_maximum_fusion.3.own_ref) | copy-start | bytes 393220
  135.7 6.5 %copy-start.1 = (bf16[32,128,128]{2,1,0:T(8,128)(2,1)}, bf16[32,128,128]{2,1,0:T(8,128)(2,1)S(1)}, u32[]{:S(2)}) copy-start(bf16[32,128,128]{2,1,0:T(8,128)(2,1)S(1)} %all-to-all-done.1) | copy-start | bytes 3145732
  137.0 11.0 %collective-permute-start.9 = (bf16[8,4,128,128]{3,2,1,0:T(8,128)(2,1)}, bf16[8,4,128,128]{3,2,1,0:T(8,128)(2,1)S(1)}, u32[]{:S(2)}, u32[]{:S(2)}) collective-permute-start(bf16[8,4,128,128]{3,2,1,0:T(8,128)(2,1)} %broadcast_select_fusion), channel_id=1, source_target_pairs={{0,4},{4,0},{1,5},{5,1},{2,6},{6,2},{3,7},{7,3},{8,12},{12,8},{9,1... | collective-permute-start | bytes 3145736 | tf_op jit(solution)/shard_map/ppermute | solution.py:175
  148.0 1.0 copy-start.3
  154.7 21.1 %all-to-all-start.2 = ((bf16[4,128,640]{2,1,0:T(8,128)(2,1)}), bf16[4,128,640]{2,1,0:T(8,128)(2,1)S(1)}, u32[]{:S(2)}, u32[]{:S(2)}) async-start(bf16[4,128,640]{2,1,0:T(8,128)(2,1)} %attend.1), calls=%async_computation.2 | async-start | bytes 1310720 | tf_op jit(solution)/shard_map/all_to_all | solution.py:221
Sparse Core Ops, SparseCore 0:
  51.6 37.6 all-gather.4
  91.9 44.8 all-gather.6

commit v4 on v3

--- a/solution.py
+++ b/solution.py
@@ -48,27 +48,36 @@
     return ordered
 
 
-def natural_to_gathered(per, rows, ny, nz):
+def natural_to_gathered(per, rows):
     nat = lax.broadcasted_iota(jnp.int32, (per, per), 0)
     gat = lax.broadcasted_iota(jnp.int32, (per, per), 1)
     half = per // 2
     core, rest = gat // half, gat % half
     place, row = rest // rows, rest % rows
-    source = (((place % ny) * nz + place // ny) * 2 + core) * rows + row
+    source = (place * 2 + core) * rows + row
     return (nat == source).astype(jnp.bfloat16)
 
 
-def queries_kernel(normed_ref, cosine_ref, sine_ref, qo_ref, out_ref, weights_ref, sem):
-    groups, part, cols = weights_ref.shape
-    copy = pltpu.make_async_copy(qo_ref.at[:, pl.ds(0, part), :], weights_ref, sem)
-    copy.start()
-    copy.wait()
-    raw = jnp.dot(normed_ref[0], weights_ref[0], preferred_element_type=jnp.float32)
-    for g in range(1, groups):
-        raw = raw + jnp.dot(normed_ref[g], weights_ref[g], preferred_element_type=jnp.float32)
-    raw = raw * HD ** (-0.5)
+def fetch(qo_ref, at, weights_ref, sems):
+    groups = qo_ref.shape[0]
+    part = qo_ref.shape[1] // 2
+    copies = [
+        pltpu.make_async_copy(
+            qo_ref.at[g, pl.ds(at * part, part), :], weights_ref.at[pl.ds(g * part, part), :], sems.at[g]
+        )
+        for g in range(groups)
+    ]
+    for copy in copies:
+        copy.start()
+    return copies
+
+
+def queries_kernel(normed_ref, cosine_ref, sine_ref, qo_ref, out_ref, weights_ref, sems):
+    for copy in fetch(qo_ref, 0, weights_ref, sems):
+        copy.wait()
+    raw = jnp.dot(normed_ref[...], weights_ref[...], preferred_element_type=jnp.float32) * HD ** (-0.5)
     half = HD // 2
-    for h in range(cols // HD):
+    for h in range(raw.shape[1] // HD):
         lo = raw[:, h * HD : h * HD + half]
         turned = lo * cosine_ref[...] + pltpu.roll(lo, half // 2, 1) * sine_ref[...]
         out_ref[:, h * HD : h * HD + half] = turned.astype(out_ref.dtype)
@@ -78,12 +87,8 @@
 
 
 def attend_kernel(
-    queries_ref, mine_ref, partner_ref, own_ref, keys_at_ref, token_ref, first_ref, qo_ref, out_ref, weights_ref, sem
+    queries_ref, mine_ref, partner_ref, own_ref, keys_at_ref, token_ref, first_ref, out_ref
 ):
-    groups, part, cols = weights_ref.shape
-    copy = pltpu.make_async_copy(qo_ref.at[:, pl.ds(part, part), :], weights_ref, sem)
-    copy.start()
-
     def whole(t):
         far = [ref[:, t].reshape(ref.shape[0] * ref.shape[2], ref.shape[3]) for ref in (mine_ref, partner_ref)]
         return jnp.concatenate([*far, own_ref[t]], axis=0)
@@ -92,8 +97,7 @@
     values = jnp.concatenate([whole(2), whole(3)], axis=1)
     at = keys_at_ref[...]
     live = (at <= token_ref[...]) & (at >= first_ref[...])
-    heads = []
-    for h in range(cols // HD):
+    for h in range(out_ref.shape[1] // HD):
         scores = lax.dot_general(
             queries_ref[:, h * HD : (h + 1) * HD],
             keys,
@@ -103,16 +107,28 @@
         scores = jnp.where(live, scores, -1e30)
         powered = jnp.exp(scores - jnp.max(scores, axis=1, keepdims=True))
         weights = (powered * (1.0 / jnp.sum(powered, axis=1, keepdims=True))).astype(jnp.bfloat16)
-        heads.append(
-            jnp.dot(weights, values, preferred_element_type=jnp.float32).astype(jnp.bfloat16)
-        )
-    attended = jnp.concatenate(heads, axis=1)
-    copy.wait()
-    for g in range(groups // 2):
-        rows = jnp.concatenate([weights_ref[2 * g], weights_ref[2 * g + 1]], axis=0)
-        out_ref[g] = lax.dot_general(
-            attended, rows, (((1,), (1,)), ((), ())), preferred_element_type=jnp.float32
+        out_ref[:, h * HD : (h + 1) * HD] = jnp.dot(
+            weights, values, preferred_element_type=jnp.float32
         ).astype(out_ref.dtype)
+
+
+def finish_kernel(every_ref, perm_ref, tokens_ref, qo_ref, out_ref, weights_ref, sems):
+    copies = fetch(qo_ref, 1, weights_ref, sems)
+    shard = out_ref.shape[1]
+    cols = qo_ref.shape[2]
+    turn = lambda a, b: lax.dot_general(a, b, (((1,), (1,)), ((), ())), preferred_element_type=jnp.float32)
+    for copy in copies:
+        copy.wait()
+    summed = jnp.zeros(out_ref.shape, jnp.float32)
+    for b in range(weights_ref.shape[0] // shard):
+        summed = summed + turn(every_ref[:, b * cols : (b + 1) * cols], weights_ref[b * shard : (b + 1) * shard, :])
+    first = summed.astype(jnp.bfloat16)
+    rest = summed - first.astype(jnp.float32)
+    second = rest.astype(jnp.bfloat16)
+    third = (rest - second.astype(jnp.float32)).astype(jnp.bfloat16)
+    perm = perm_ref[...]
+    natural = turn(first, perm) + (turn(second, perm) + turn(third, perm))
+    out_ref[...] = (tokens_ref[...].astype(jnp.float32) + natural).astype(out_ref.dtype)
 
 
 def per_device(tokens, seg_ids, norm_gain, w_query, w_keyval, w_out):
@@ -135,14 +151,11 @@
 
     others = [lax.ppermute(tokens, "tp", [(i, (i + k) % nx) for i in range(nx)]) for k in range(1, nx)]
 
-    qo_own = jnp.concatenate([w_query, w_out.T], axis=0)
-    qo_other = lax.ppermute(qo_own, "yh", both)
-    low = jnp.where(iy == 0, qo_own, qo_other)
-    high = jnp.where(iy == 0, qo_other, qo_own)
-    qo_pair = jnp.concatenate([low[:rows], high[:rows], low[rows:], high[rows:]], axis=0)
-    least = (1 << 20) // (2 * nz * cols)
-    qo_pair = jnp.pad(qo_pair, ((0, max(0, least - qo_pair.shape[0])), (0, 0)))
-    qo_near = lax.all_gather(qo_pair, "z", axis=0, tiled=False)
+    diagonal = [(a * nx + b, b * nx + a) for a in range(nx) for b in range(nx)]
+    o_rows = lax.ppermute(w_out.T, ("x", "tp"), diagonal)
+    qo_slab = jnp.concatenate([w_query, o_rows], axis=0)
+    qo_near = spread(after(qo_slab, kv_core), ("yh", "z"), ny * nz)
+
     groups = in_order([tokens, *others], it)
     normed = rms_norm(jnp.concatenate(groups, axis=1), norm_gain)
 
@@ -174,22 +187,17 @@
     at_self = (chips == iz)[:, None, None, None] & (ic == 0)
     partner = lax.ppermute(jnp.where(at_self, own_kv[None], mine), "c", both)
     part = nz * ny * rows
-    qo_near = after(qo_near, to_send)
-    qo_send = jnp.concatenate(
+    qo_send = jnp.concatenate([qo_near[:, :rows].reshape(part, cols), qo_near[:, rows:].reshape(part, cols)], axis=0)
+    qo_all = lax.all_gather(qo_send, ("x", "c"), axis=0, tiled=False)
+    perm = natural_to_gathered(shard, rows)
+    normed = after(normed, to_send)
+    reordered = jnp.concatenate(
         [
-            qo_near[:, : ny * rows].reshape(part, cols),
-            qo_near[:, ny * rows : 2 * ny * rows].reshape(part, cols),
+            jnp.dot(normed[:, g * shard : (g + 1) * shard], perm, preferred_element_type=jnp.float32).astype(bf)
+            for g in range(nx)
         ],
-        axis=0,
+        axis=1,
     )
-    qo_all = lax.all_gather(qo_send, ("x", "c"), axis=0, tiled=False)
-    perm = natural_to_gathered(shard, rows, ny, nz)
-    normed = after(normed, to_send)
-    blocks = []
-    for g in range(nx):
-        turned = jnp.dot(normed[:, g * shard : (g + 1) * shard], perm, preferred_element_type=jnp.float32)
-        blocks += [turned[:, :part].astype(bf), turned[:, part:].astype(bf)]
-    blocks = jnp.stack(blocks)
     block_of_mine = my_block - (chips >= iz).astype(jnp.int32)
     block_of_partner = my_block - jnp.where(ic == 1, chips > iz, chips >= iz).astype(jnp.int32)
     first_of_mine = ((block_of_mine * nz + chips) * nc + ic) * tok
@@ -199,7 +207,7 @@
 
     vmem = pl.BlockSpec(memory_space=pltpu.VMEM)
     hbm = pl.BlockSpec(memory_space=pl.ANY)
-    scratch = [pltpu.VMEM((nx * nc, part, cols), bf), pltpu.SemaphoreType.DMA]
+    scratch = [pltpu.VMEM((nx * nc * part, cols), bf), pltpu.SemaphoreType.DMA((nx * nc,))]
     queries = pl.pallas_call(
         queries_kernel,
         out_shape=jax.ShapeDtypeStruct((tok, cols), bf),
@@ -207,24 +215,25 @@
         out_specs=vmem,
         scratch_shapes=scratch,
         name="queries",
-    )(blocks, cosine, sine, qo_all)
+    )(reordered, cosine, sine, qo_all)
     reach_back = jnp.maximum(own_start, token_index - (WINDOW - 1))
-    partial = pl.pallas_call(
+    attended = pl.pallas_call(
         attend_kernel,
-        out_shape=jax.ShapeDtypeStruct((nx, tok, shard), bf),
-        in_specs=[vmem] * 7 + [hbm],
+        out_shape=jax.ShapeDtypeStruct((tok, cols), bf),
+        in_specs=[vmem] * 7,
+        out_specs=vmem,
+        name="attend",
+    )(queries, mine, partner, own_kv, keys_at, token_index[:, None], reach_back[:, None])
+
+    every = lax.all_gather(attended, "tp", axis=1, tiled=True)
+    hidden = pl.pallas_call(
+        finish_kernel,
+        out_shape=jax.ShapeDtypeStruct((tok, shard), bf),
+        in_specs=[vmem, vmem, vmem, hbm],
         out_specs=vmem,
         scratch_shapes=scratch,
-        name="attend",
-    )(queries, mine, partner, own_kv, keys_at, token_index[:, None], reach_back[:, None], qo_all)
-
-    received = lax.all_to_all(partial, "tp", 0, 0, tiled=True)
-    summed = jnp.zeros((tok, shard), jnp.float32)
-    for g in range(nx):
-        summed = summed + lax.dot_general(
-            received[g], perm, (((1,), (1,)), ((), ())), preferred_element_type=jnp.float32
-        )
-    hidden = (tokens.astype(jnp.float32) + summed).astype(bf)
+        name="finish",
+    )(every, perm, tokens, qo_all)
     return (hidden, kv_cache)
 
 

time: 186 us -> 190 us (1.022)
  the two profiles are of different devices: /device:TPU:1 before, /device:TPU:6 now
where the time goes in v4:
time: 190 us; the launch traced here: 189 us
  starting transfers between devices  63.2 us (33%)
  blocking collectives  41.2 us (22%)
  waiting for transfers between devices  40.8 us (21%)
  Pallas kernels  14.6 us (8%)
  between operations  14.5 us (8%)
  other arithmetic  8.36 us (4%)
  local copies, waits for them, and re-layouts  3.8 us (2%)
  matrix products  2.35 us (1%)
    all_to_all x1, blocking collectives, spread(): return lax.all_to_all(copies, axes, 0, 0, tiled=True)  23.7 us
    all_to_all x1, starting transfers between devices, spread(): return lax.all_to_all(copies, axes, 0, 0, tiled=True)  19.3 us
    all_gather x1, blocking collectives, per_device(): every = lax.all_gather(attended, 'tp', axis=1, tiled=True)  17.5 us
    ppermute x3, starting transfers between devices, per_device(): lax.ppermute(tokens, 'tp', [(i, (i + k) % nx) for i in range(nx)])  16.4 us
    ppermute x3, waiting for transfers between devices, per_device(): lax.ppermute(kv_share, 'tp', [(i, (i + k) % nx) for i in range(nx)])  12.4 us
    ppermute x3, starting transfers between devices, per_device(): lax.ppermute(kv_share, 'tp', [(i, (i + k) % nx) for i in range(nx)])  12.2 us
    ppermute x1, waiting for transfers between devices, per_device(): lax.ppermute(kv_share, SEQ, [(i, i + block) for i in range(devices - bloc...  7.9 us
    ppermute x1, waiting for transfers between devices, per_device(): o_rows = lax.ppermute(w_out.T, ('x', 'tp'), diagonal)  7.46 us
  transfers between devices with their start and end apart: 13, of which 7 were waited for; matrix products, arithmetic and copies ran while one was open for 6% of the time, Pallas kernels for 2%

profile of v4, /device:TPU:6, one launch (start us, length us, event | category | flops | bytes accessed | tf_op | source)
XLA Modules:
  0.0 188.9 jit_solution(15109094726776106433)
XLA Ops:
  7.2 0.0 copy-start
  7.2 0.7 convert_bitcast_fusion
  7.8 0.1 copy-done
  7.9 0.8 broadcast_in_dim.56
  8.7 19.3 %all-to-all-start = ((bf16[64,24,128]{2,1,0:T(8,128)(2,1)}), bf16[64,24,128]{2,1,0:T(8,128)(2,1)S(1)}, u32[]{:S(2)}, u32[]{:S(2)}) async-start(bf16[64,24,128]{2,1,0:T(8,128)(2,1)} %broadcast_in_dim.56), calls=%async_computation | async-start | bytes 786432 | tf_op jit(solution)/shard_map/all_to_all | solution.py:36
  28.0 0.0 all-gather.3.cloned.1.call-start
  28.1 2.5 %collective-permute-start.5 = (bf16[20,512]{1,0:T(8,128)(2,1)}, bf16[20,512]{1,0:T(8,128)(2,1)S(1)}, u32[]{:S(2)}, u32[]{:S(2)}) collective-permute-start(bf16[20,512]{1,0:T(8,128)(2,1)} %bitcast.43), channel_id=1, source_target_pairs={{0,0},{1,128},{2,256},{3,384},{128,1},{129,129},{130,257},{131,385... | collective-permute-start | bytes 61448 | tf_op jit(solution)/shard_map/ppermute | solution.py:155
  30.6 7.5 %collective-permute-done.5 = bf16[20,512]{1,0:T(8,128)(2,1)S(1)} collective-permute-done((bf16[20,512]{1,0:T(8,128)(2,1)}, bf16[20,512]{1,0:T(8,128)(2,1)S(1)}, u32[]{:S(2)}, u32[]{:S(2)}) %collective-permute-start.5) | collective-permute-done | bytes 20512 | tf_op jit(solution)/shard_map/ppermute | solution.py:155
  38.0 0.7 pad_maximum_fusion.8
  38.8 6.3 %all-to-all-done = bf16[64,24,128]{2,1,0:T(8,128)(2,1)S(1)} async-done(((bf16[64,24,128]{2,1,0:T(8,128)(2,1)}), bf16[64,24,128]{2,1,0:T(8,128)(2,1)S(1)}, u32[]{:S(2)}, u32[]{:S(2)}) %all-to-all-start) | async-done | bytes 393248 | tf_op jit(solution)/shard_map/all_to_all | solution.py:36
  45.1 23.7 %all_to_all.15 = bf16[16,40,512]{2,1,0:T(8,128)(2,1)S(1)} all-to-all(bf16[16,40,512]{2,1,0:T(8,128)(2,1)S(1)} %broadcast_in_dim.68), channel_id=1, replica_groups=mesh['x'=4,'yh'=2,'z'=8,'c'=2,'tp'=4] {'yh','z'}, dimensions={0} | all-to-all | bytes 1310720 | tf_op jit(solution)/shard_map/all_to_all | solution.py:36
  68.8 0.1 fusion.44
  68.9 0.0 copy-start.3
  69.0 0.1 reshape.112
  69.0 0.1 reshape.111
  69.1 0.9 pad_maximum_fusion.3
  70.0 0.0 all-gather.3.cloned.1.call-update
  70.1 8.8 %collective-permute-start = (bf16[128,640]{1,0:T(8,128)(2,1)S(1)}, bf16[128,640]{1,0:T(8,128)(2,1)S(1)}, u32[]{:S(2)}, u32[]{:S(2)}) collective-permute-start(bf16[128,640]{1,0:T(8,128)(2,1)S(1)} %copy-done.3), channel_id=1, source_target_pairs={{0,2},{1,3},{2,0},{3,1},{4,6},{5,7},{6,4},{7,5},{8,10},{9,11},{10,... | collective-permute-start | bytes 491528 | tf_op jit(solution)/shard_map/ppermute | solution.py:152
  78.9 1.9 %collective-permute-start.1 = (bf16[128,640]{1,0:T(8,128)(2,1)S(1)}, bf16[128,640]{1,0:T(8,128)(2,1)S(1)}, u32[]{:S(2)}, u32[]{:S(2)}) collective-permute-start(bf16[128,640]{1,0:T(8,128)(2,1)S(1)} %copy-done.3), channel_id=1, source_target_pairs={{0,1},{1,2},{2,3},{3,0},{4,5},{5,6},{6,7},{7,4},{8,9},{9,10},{10,1... | collective-permute-start | bytes 491528 | tf_op jit(solution)/shard_map/ppermute | solution.py:152
  80.8 5.7 %collective-permute-start.2 = (bf16[128,640]{1,0:T(8,128)(2,1)S(1)}, bf16[128,640]{1,0:T(8,128)(2,1)S(1)}, u32[]{:S(2)}, u32[]{:S(2)}) collective-permute-start(bf16[128,640]{1,0:T(8,128)(2,1)S(1)} %copy-done.3), channel_id=1, source_target_pairs={{0,3},{1,0},{2,1},{3,2},{4,7},{5,4},{6,5},{7,6},{8,11},{9,8},{10,9... | collective-permute-start | bytes 491528 | tf_op jit(solution)/shard_map/ppermute | solution.py:152
  86.6 0.1 pad_add_fusion
  86.7 0.1 add_bitcast_fusion
  86.9 3.8 %collective-permute-done = bf16[128,640]{1,0:T(8,128)(2,1)S(1)} collective-permute-done((bf16[128,640]{1,0:T(8,128)(2,1)S(1)}, bf16[128,640]{1,0:T(8,128)(2,1)S(1)}, u32[]{:S(2)}, u32[]{:S(2)}) %collective-permute-start) | collective-permute-done | bytes 163872 | tf_op jit(solution)/shard_map/ppermute | solution.py:152
  90.7 1.3 collective-permute-done.2
  92.0 0.1 select_select_fusion.3
  92.1 0.2 fusion.12
  92.4 0.1 copy.43
  92.5 1.9 %collective-permute-start.3 = (bf16[64,24,128]{2,0,1:T(8,128)(2,1)S(1)}, bf16[64,24,128]{2,0,1:T(8,128)(2,1)S(1)}, u32[]{:S(2)}, u32[]{:S(2)}) collective-permute-start(bf16[64,24,128]{2,0,1:T(8,128)(2,1)S(1)} %copy.43), channel_id=1, source_target_pairs={{0,4},{4,0},{1,5},{5,1},{2,6},{6,2},{3,7},{7,3},{8,12},{12,8},{9,1... | collective-permute-start | bytes 1179656 | tf_op jit(solution)/shard_map/ppermute | solution.py:150
  94.4 0.2 fusion.14
  94.6 1.5 collective-permute-done.3
  96.2 0.1 pad_maximum_fusion.1
  96.3 0.4 copy.45
  96.7 0.1 reshape.109
  96.9 0.3 convert_reduce_fusion
  97.2 0.1 select_reduce_fusion
  97.3 0.3 fusion.46
  97.7 0.3 fusion.23
  98.0 0.8 fusion.21
  98.8 2.7 %collective-permute-start.4 = (bf16[128,128]{1,0:T(8,128)(2,1)S(1)}, bf16[128,128]{1,0:T(8,128)(2,1)S(1)}, u32[]{:S(2)}, u32[]{:S(2)}) collective-permute-start(bf16[128,128]{1,0:T(8,128)(2,1)S(1)} %get-tuple-element.6), channel_id=1, source_target_pairs={{0,64},{4,68},{8,72},{12,76},{16,80},{20,84},{24,88},{28,92},{32,9... | collective-permute-start | bytes 98312 | tf_op jit(solution)/shard_map/ppermute | solution.py:179
  101.5 7.9 %collective-permute-done.4 = bf16[128,128]{1,0:T(8,128)(2,1)S(1)} collective-permute-done((bf16[128,128]{1,0:T(8,128)(2,1)S(1)}, bf16[128,128]{1,0:T(8,128)(2,1)S(1)}, u32[]{:S(2)}, u32[]{:S(2)}) %collective-permute-start.4) | collective-permute-done | bytes 32800 | tf_op jit(solution)/shard_map/ppermute | solution.py:179
  109.4 0.1 broadcast_select_fusion.1
  109.4 1.2 broadcast_in_dim.67
  110.7 6.2 %all-to-all-start.2 = ((bf16[32,128,128]{2,1,0:T(8,128)(2,1)}), bf16[32,128,128]{2,1,0:T(8,128)(2,1)S(1)}, u32[]{:S(2)}, u32[]{:S(2)}) async-start(bf16[32,128,128]{2,1,0:T(8,128)(2,1)} %bitcast.6), calls=%async_computation.2 | async-start | bytes 2097152 | tf_op jit(solution)/shard_map/all_to_all | solution.py:183
  116.9 0.6 copy.57
  117.5 1.1 fusion.39.perm_ref
  118.6 4.6 %collective-permute-start.6 = (bf16[128,128]{1,0:T(8,128)(2,1)S(1)}, bf16[128,128]{1,0:T(8,128)(2,1)S(1)}, u32[]{:S(2)}, u32[]{:S(2)}) collective-permute-start(bf16[128,128]{1,0:T(8,128)(2,1)S(1)} %get-tuple-element.6), channel_id=1, source_target_pairs={{0,2},{1,3},{2,0},{3,1},{4,6},{5,7},{6,4},{7,5},{8,10},{9,11},{10,... | collective-permute-start | bytes 98312 | tf_op jit(solution)/shard_map/ppermute | solution.py:184
  123.2 3.4 %collective-permute-start.7 = (bf16[128,128]{1,0:T(8,128)(2,1)S(1)}, bf16[128,128]{1,0:T(8,128)(2,1)S(1)}, u32[]{:S(2)}, u32[]{:S(2)}) collective-permute-start(bf16[128,128]{1,0:T(8,128)(2,1)S(1)} %get-tuple-element.6), channel_id=1, source_target_pairs={{0,1},{1,2},{2,3},{3,0},{4,5},{5,6},{6,7},{7,4},{8,9},{9,10},{10,1... | collective-permute-start | bytes 98312 | tf_op jit(solution)/shard_map/ppermute | solution.py:184
  126.6 4.3 %collective-permute-start.8 = (bf16[128,128]{1,0:T(8,128)(2,1)S(1)}, bf16[128,128]{1,0:T(8,128)(2,1)S(1)}, u32[]{:S(2)}, u32[]{:S(2)}) collective-permute-start(bf16[128,128]{1,0:T(8,128)(2,1)S(1)} %get-tuple-element.6), channel_id=1, source_target_pairs={{0,3},{1,0},{2,1},{3,2},{4,7},{5,4},{6,5},{7,6},{8,11},{9,8},{10,9... | collective-permute-start | bytes 98312 | tf_op jit(solution)/shard_map/ppermute | solution.py:184
  130.8 0.1 copy.52
  130.9 0.7 add_maximum_fusion
  131.6 12.4 %collective-permute-done.6 = bf16[128,128]{1,0:T(8,128)(2,1)S(1)} collective-permute-done((bf16[128,128]{1,0:T(8,128)(2,1)S(1)}, bf16[128,128]{1,0:T(8,128)(2,1)S(1)}, u32[]{:S(2)}, u32[]{:S(2)}) %collective-permute-start.6) | collective-permute-done | bytes 32800 | tf_op jit(solution)/shard_map/ppermute | solution.py:184
  144.1 0.5 convolution_convert_fusion
  144.6 0.5 convolution_convert_fusion.1
  145.1 0.0 all-to-all-done.2
  145.1 0.1 broadcast_select_fusion
  145.3 1.9 %collective-permute-start.9 = (bf16[8,4,128,128]{3,2,1,0:T(8,128)(2,1)S(1)}, bf16[8,4,128,128]{3,2,1,0:T(8,128)(2,1)}, u32[]{:S(2)}, u32[]{:S(2)}) collective-permute-start(bf16[8,4,128,128]{3,2,1,0:T(8,128)(2,1)S(1)} %broadcast_select_fusion), channel_id=1, source_target_pairs={{0,4},{4,0},{1,5},{5,1},{2,6},{6,2},{3,7},{7,3},{8,12},{12,8},{9,1... | collective-permute-start | bytes 3145736 | tf_op jit(solution)/shard_map/ppermute | solution.py:188
  147.2 0.5 convolution_convert_fusion.2
  147.7 0.7 pad_maximum_fusion.5
  148.4 0.5 convolution_convert_fusion.3
  148.9 0.9 pad_maximum_fusion.2.normed_ref
  149.8 4.1 %queries.1.queries_ref = bf16[128,512]{1,0:T(8,128)(2,1)} custom-call(bf16[128,2560]{1,0:T(8,128)(2,1)} %pad_maximum_fusion.2.normed_ref, f32[128,128]{1,0:T(8,128)} %get-tuple-element.20.cosine_ref, f32[128,128]{1,0:T(8,128)} %get-tuple-element.7.sine_ref, bf16[8,640,512]{2,1,0:T(8,128)(2,1)} %bitcast.33), custom_call_target="tpu_custom_call" | custom-call | tf_op jit(solution)/shard_map/queries/pallas_call | solution.py:211
  153.9 4.6 %attend.1 = bf16[128,512]{1,0:T(8,128)(2,1)} custom-call(bf16[128,512]{1,0:T(8,128)(2,1)} %queries.1.queries_ref, bf16[8,4,128,128]{3,2,1,0:T(8,128)(2,1)} %bitcast.36, bf16[8,4,128,128]{3,2,1,0:T(8,128)(2,1)} %collective-permute-done.9.partner_ref, bf16[4,128,128]{2,1,0:T(8,128)(2,1)} %copy-done.2, s32[1,2176]{1,0:T(1,128)} %bitcast.41, ...), custom_call_target="tpu_custom_call" | custom-call | tf_op jit(solution)/shard_map/attend/pallas_call | solution.py:220
  158.5 17.5 %all_gather.11.every_ref = bf16[128,2048]{1,0:T(8,128)(2,1)} all-gather(bf16[128,512]{1,0:T(8,128)(2,1)} %attend.1), channel_id=1, replica_groups=mesh['x'=4,'yh'=2,'z'=8,'c'=2,'tp'=4] {'tp'}, dimensions={1}, use_global_device_ids=true | all-gather | bytes 655360 | tf_op jit(solution)/shard_map/all_gather | solution.py:228
  176.1 6.0 %finish.1 = bf16[128,640]{1,0:T(8,128)(2,1)} custom-call(bf16[128,2048]{1,0:T(8,128)(2,1)} %all_gather.11.every_ref, bf16[640,640]{1,0:T(8,128)(2,1)} %fusion.39.perm_ref, bf16[128,640]{1,0:T(8,128)(2,1)} %tokens_ref.1, bf16[8,640,512]{2,1,0:T(8,128)(2,1)} %bitcast.34), custom_call_target="tpu_custom_call" | custom-call | tf_op jit(solution)/shard_map/finish/pallas_call | solution.py:229
  (34 shorter events, 0.3 us)
Async XLA Ops:
  7.2 0.7 copy-start
  8.7 36.4 %all-to-all-start = ((bf16[64,24,128]{2,1,0:T(8,128)(2,1)}), bf16[64,24,128]{2,1,0:T(8,128)(2,1)S(1)}, u32[]{:S(2)}, u32[]{:S(2)}) async-start(bf16[64,24,128]{2,1,0:T(8,128)(2,1)} %broadcast_in_dim.56), calls=%async_computation | async-start | bytes 786432 | tf_op jit(solution)/shard_map/all_to_all | solution.py:36
  28.0 121.8 %all-gather.3.cloned.1.call-start = ((), (), s32[]{:S(2)}) async-start(), calls=%async_computation.3 | async-start | bytes 5898240 | tf_op jit(solution)/shard_map/all_gather | solution.py:191
  28.1 10.0 %collective-permute-start.5 = (bf16[20,512]{1,0:T(8,128)(2,1)}, bf16[20,512]{1,0:T(8,128)(2,1)S(1)}, u32[]{:S(2)}, u32[]{:S(2)}) collective-permute-start(bf16[20,512]{1,0:T(8,128)(2,1)} %bitcast.43), channel_id=1, source_target_pairs={{0,0},{1,128},{2,256},{3,384},{128,1},{129,129},{130,257},{131,385... | collective-permute-start | bytes 61448 | tf_op jit(solution)/shard_map/ppermute | solution.py:155
  68.9 1.1 copy-start.3
  69.0 17.9 %copy-start.4 = (bf16[2560]{0:T(1024)(128)(2,1)S(1)}, bf16[2560]{0:T(1024)(128)(2,1)}, u32[]{:S(2)}) copy-start(bf16[2560]{0:T(1024)(128)(2,1)} %param.8) | copy-start | bytes 15364
  70.1 20.6 %collective-permute-start = (bf16[128,640]{1,0:T(8,128)(2,1)S(1)}, bf16[128,640]{1,0:T(8,128)(2,1)S(1)}, u32[]{:S(2)}, u32[]{:S(2)}) collective-permute-start(bf16[128,640]{1,0:T(8,128)(2,1)S(1)} %copy-done.3), channel_id=1, source_target_pairs={{0,2},{1,3},{2,0},{3,1},{4,6},{5,7},{6,4},{7,5},{8,10},{9,11},{10,... | collective-permute-start | bytes 491528 | tf_op jit(solution)/shard_map/ppermute | solution.py:152
  78.9 11.9 %collective-permute-start.1 = (bf16[128,640]{1,0:T(8,128)(2,1)S(1)}, bf16[128,640]{1,0:T(8,128)(2,1)S(1)}, u32[]{:S(2)}, u32[]{:S(2)}) collective-permute-start(bf16[128,640]{1,0:T(8,128)(2,1)S(1)} %copy-done.3), channel_id=1, source_target_pairs={{0,1},{1,2},{2,3},{3,0},{4,5},{5,6},{6,7},{7,4},{8,9},{9,10},{10,1... | collective-permute-start | bytes 491528 | tf_op jit(solution)/shard_map/ppermute | solution.py:152
  80.8 11.2 %collective-permute-start.2 = (bf16[128,640]{1,0:T(8,128)(2,1)S(1)}, bf16[128,640]{1,0:T(8,128)(2,1)S(1)}, u32[]{:S(2)}, u32[]{:S(2)}) collective-permute-start(bf16[128,640]{1,0:T(8,128)(2,1)S(1)} %copy-done.3), channel_id=1, source_target_pairs={{0,3},{1,0},{2,1},{3,2},{4,7},{5,4},{6,5},{7,6},{8,11},{9,8},{10,9... | collective-permute-start | bytes 491528 | tf_op jit(solution)/shard_map/ppermute | solution.py:152
  92.5 3.7 %collective-permute-start.3 = (bf16[64,24,128]{2,0,1:T(8,128)(2,1)S(1)}, bf16[64,24,128]{2,0,1:T(8,128)(2,1)S(1)}, u32[]{:S(2)}, u32[]{:S(2)}) collective-permute-start(bf16[64,24,128]{2,0,1:T(8,128)(2,1)S(1)} %copy.43), channel_id=1, source_target_pairs={{0,4},{4,0},{1,5},{5,1},{2,6},{6,2},{3,7},{7,3},{8,12},{12,8},{9,1... | collective-permute-start | bytes 1179656 | tf_op jit(solution)/shard_map/ppermute | solution.py:150
  96.3 1.0 copy-start.5
  98.8 10.6 %collective-permute-start.4 = (bf16[128,128]{1,0:T(8,128)(2,1)S(1)}, bf16[128,128]{1,0:T(8,128)(2,1)S(1)}, u32[]{:S(2)}, u32[]{:S(2)}) collective-permute-start(bf16[128,128]{1,0:T(8,128)(2,1)S(1)} %get-tuple-element.6), channel_id=1, source_target_pairs={{0,64},{4,68},{8,72},{12,76},{16,80},{20,84},{24,88},{28,92},{32,9... | collective-permute-start | bytes 98312 | tf_op jit(solution)/shard_map/ppermute | solution.py:179
  110.7 34.4 %all-to-all-start.2 = ((bf16[32,128,128]{2,1,0:T(8,128)(2,1)}), bf16[32,128,128]{2,1,0:T(8,128)(2,1)S(1)}, u32[]{:S(2)}, u32[]{:S(2)}) async-start(bf16[32,128,128]{2,1,0:T(8,128)(2,1)} %bitcast.6), calls=%async_computation.2 | async-start | bytes 2097152 | tf_op jit(solution)/shard_map/all_to_all | solution.py:183
  118.6 25.4 %collective-permute-start.6 = (bf16[128,128]{1,0:T(8,128)(2,1)S(1)}, bf16[128,128]{1,0:T(8,128)(2,1)S(1)}, u32[]{:S(2)}, u32[]{:S(2)}) collective-permute-start(bf16[128,128]{1,0:T(8,128)(2,1)S(1)} %get-tuple-element.6), channel_id=1, source_target_pairs={{0,2},{1,3},{2,0},{3,1},{4,6},{5,7},{6,4},{7,5},{8,10},{9,11},{10,... | collective-permute-start | bytes 98312 | tf_op jit(solution)/shard_map/ppermute | solution.py:184
  123.2 20.8 %collective-permute-start.7 = (bf16[128,128]{1,0:T(8,128)(2,1)S(1)}, bf16[128,128]{1,0:T(8,128)(2,1)S(1)}, u32[]{:S(2)}, u32[]{:S(2)}) collective-permute-start(bf16[128,128]{1,0:T(8,128)(2,1)S(1)} %get-tuple-element.6), channel_id=1, source_target_pairs={{0,1},{1,2},{2,3},{3,0},{4,5},{5,6},{6,7},{7,4},{8,9},{9,10},{10,1... | collective-permute-start | bytes 98312 | tf_op jit(solution)/shard_map/ppermute | solution.py:184
  126.6 17.4 %collective-permute-start.8 = (bf16[128,128]{1,0:T(8,128)(2,1)S(1)}, bf16[128,128]{1,0:T(8,128)(2,1)S(1)}, u32[]{:S(2)}, u32[]{:S(2)}) collective-permute-start(bf16[128,128]{1,0:T(8,128)(2,1)S(1)} %get-tuple-element.6), channel_id=1, source_target_pairs={{0,3},{1,0},{2,1},{3,2},{4,7},{5,4},{6,5},{7,6},{8,11},{9,8},{10,9... | collective-permute-start | bytes 98312 | tf_op jit(solution)/shard_map/ppermute | solution.py:184
  144.0 1.1 copy-start.2
  145.1 2.6 %copy-start.1 = (bf16[32,128,128]{2,1,0:T(8,128)(2,1)}, bf16[32,128,128]{2,1,0:T(8,128)(2,1)S(1)}, u32[]{:S(2)}) copy-start(bf16[32,128,128]{2,1,0:T(8,128)(2,1)S(1)} %all-to-all-done.2) | copy-start | bytes 3145732
  145.3 8.7 %collective-permute-start.9 = (bf16[8,4,128,128]{3,2,1,0:T(8,128)(2,1)S(1)}, bf16[8,4,128,128]{3,2,1,0:T(8,128)(2,1)}, u32[]{:S(2)}, u32[]{:S(2)}) collective-permute-start(bf16[8,4,128,128]{3,2,1,0:T(8,128)(2,1)S(1)} %broadcast_select_fusion), channel_id=1, source_target_pairs={{0,4},{4,0},{1,5},{5,1},{2,6},{6,2},{3,7},{7,3},{8,12},{12,8},{9,1... | collective-permute-start | bytes 3145736 | tf_op jit(solution)/shard_map/ppermute | solution.py:188
Sparse Core Ops, SparseCore 0:
  70.2 38.3 all-gather.2

commit v5 on v4

--- a/solution.py
+++ b/solution.py
@@ -48,14 +48,26 @@
     return ordered
 
 
-def natural_to_gathered(per, rows):
-    nat = lax.broadcasted_iota(jnp.int32, (per, per), 0)
-    gat = lax.broadcasted_iota(jnp.int32, (per, per), 1)
-    half = per // 2
+def natural_to_gathered(per, rows, slab):
+    width = per // rows * slab
+    nat = lax.broadcasted_iota(jnp.int32, (per, width), 0)
+    gat = lax.broadcasted_iota(jnp.int32, (per, width), 1)
+    half = width // 2
     core, rest = gat // half, gat % half
-    place, row = rest // rows, rest % rows
+    place, row = rest // slab, rest % slab
     source = (place * 2 + core) * rows + row
-    return (nat == source).astype(jnp.bfloat16)
+    return ((nat == source) & (row < rows)).astype(jnp.bfloat16)
+
+
+def turned(values, hot):
+    per = hot.shape[0]
+    return jnp.concatenate(
+        [
+            jnp.dot(values[:, g : g + per], hot, preferred_element_type=jnp.float32).astype(jnp.bfloat16)
+            for g in range(0, values.shape[1], per)
+        ],
+        axis=1,
+    )
 
 
 def fetch(qo_ref, at, weights_ref, sems):
@@ -87,8 +99,10 @@
 
 
 def attend_kernel(
-    queries_ref, mine_ref, partner_ref, own_ref, keys_at_ref, token_ref, first_ref, out_ref
+    queries_ref, mine_ref, partner_ref, own_ref, keys_at_ref, token_ref, first_ref, qo_ref, out_ref, weights_ref, sems
 ):
+    copies = fetch(qo_ref, 1, weights_ref, sems)
+
     def whole(t):
         far = [ref[:, t].reshape(ref.shape[0] * ref.shape[2], ref.shape[3]) for ref in (mine_ref, partner_ref)]
         return jnp.concatenate([*far, own_ref[t]], axis=0)
@@ -97,7 +111,8 @@
     values = jnp.concatenate([whole(2), whole(3)], axis=1)
     at = keys_at_ref[...]
     live = (at <= token_ref[...]) & (at >= first_ref[...])
-    for h in range(out_ref.shape[1] // HD):
+    heads = []
+    for h in range(queries_ref.shape[1] // HD):
         scores = lax.dot_general(
             queries_ref[:, h * HD : (h + 1) * HD],
             keys,
@@ -107,28 +122,20 @@
         scores = jnp.where(live, scores, -1e30)
         powered = jnp.exp(scores - jnp.max(scores, axis=1, keepdims=True))
         weights = (powered * (1.0 / jnp.sum(powered, axis=1, keepdims=True))).astype(jnp.bfloat16)
-        out_ref[:, h * HD : (h + 1) * HD] = jnp.dot(
-            weights, values, preferred_element_type=jnp.float32
-        ).astype(out_ref.dtype)
-
-
-def finish_kernel(every_ref, perm_ref, tokens_ref, qo_ref, out_ref, weights_ref, sems):
-    copies = fetch(qo_ref, 1, weights_ref, sems)
-    shard = out_ref.shape[1]
-    cols = qo_ref.shape[2]
-    turn = lambda a, b: lax.dot_general(a, b, (((1,), (1,)), ((), ())), preferred_element_type=jnp.float32)
+        heads.append(
+            jnp.dot(weights, values, preferred_element_type=jnp.float32).astype(jnp.bfloat16)
+        )
+    attended = jnp.concatenate(heads, axis=1)
+    shard = out_ref.shape[2]
     for copy in copies:
         copy.wait()
-    summed = jnp.zeros(out_ref.shape, jnp.float32)
-    for b in range(weights_ref.shape[0] // shard):
-        summed = summed + turn(every_ref[:, b * cols : (b + 1) * cols], weights_ref[b * shard : (b + 1) * shard, :])
-    first = summed.astype(jnp.bfloat16)
-    rest = summed - first.astype(jnp.float32)
-    second = rest.astype(jnp.bfloat16)
-    third = (rest - second.astype(jnp.float32)).astype(jnp.bfloat16)
-    perm = perm_ref[...]
-    natural = turn(first, perm) + (turn(second, perm) + turn(third, perm))
-    out_ref[...] = (tokens_ref[...].astype(jnp.float32) + natural).astype(out_ref.dtype)
+    for g in range(out_ref.shape[0]):
+        out_ref[g] = lax.dot_general(
+            attended,
+            weights_ref[g * shard : (g + 1) * shard, :],
+            (((1,), (1,)), ((), ())),
+            preferred_element_type=jnp.float32,
+        ).astype(out_ref.dtype)
 
 
 def per_device(tokens, seg_ids, norm_gain, w_query, w_keyval, w_out):
@@ -144,32 +151,39 @@
     both = [(0, 1), (1, 0)]
 
     share = 2 * HD // nx
-    ids = jnp.pad(seg_ids.astype(bf)[None, :], ((0, 3), (0, 0)))
+    slab = rows + 4
+    ids = jnp.pad(seg_ids.astype(bf)[None, :], ((0, 31 - rows), (0, 0)))
     kv_slab = jnp.concatenate([lax.dynamic_slice_in_dim(w_keyval, it * share, share, 1), ids], axis=0)
-    kv_core = spread(kv_slab, ("x", "yh", "z"), nx * ny * nz)
-    kv_twin = lax.ppermute(kv_core, "c", both)
+    folded = jnp.concatenate([kv_slab[i : i + 8] for i in range(0, 32, 8)], axis=1)
+    near = spread(jnp.concatenate([w_query, w_out.T, folded], axis=0), ("yh", "z"), ny * nz)
 
     others = [lax.ppermute(tokens, "tp", [(i, (i + k) % nx) for i in range(nx)]) for k in range(1, nx)]
 
-    diagonal = [(a * nx + b, b * nx + a) for a in range(nx) for b in range(nx)]
-    o_rows = lax.ppermute(w_out.T, ("x", "tp"), diagonal)
-    qo_slab = jnp.concatenate([w_query, o_rows], axis=0)
-    qo_near = spread(after(qo_slab, kv_core), ("yh", "z"), ny * nz)
+    kv_near = jnp.concatenate(
+        [near[:, 2 * rows :, i * share : (i + 1) * share] for i in range(slab // 8)], axis=1
+    )
+    kv_all = spread(kv_near, ("x", "c"), nx * nc)
+    part = nz * ny * rows
+    qo_send = jnp.concatenate(
+        [near[:, :rows].reshape(part, cols), near[:, rows : 2 * rows].reshape(part, cols)], axis=0
+    )
+    qo_all = lax.all_gather(qo_send, ("x", "c"), axis=0, tiled=False)
 
     groups = in_order([tokens, *others], it)
     normed = rms_norm(jnp.concatenate(groups, axis=1), norm_gain)
-
-    kv_zero = jnp.where(ic == 0, kv_core, kv_twin)
-    kv_one = jnp.where(ic == 0, kv_twin, kv_core)
-    all_ids = jnp.concatenate([kv_core[:, rows], kv_twin[:, rows]], axis=0).astype(jnp.int32)
+    padded = turned(normed, natural_to_gathered(shard, rows, slab))
+    kv_all, padded = lax.optimization_barrier((kv_all, padded))
+
+    all_ids = kv_all[:, :, rows].astype(jnp.int32)
     labels = jnp.arange(SEGS, dtype=jnp.int32)
     starts = jnp.sum((all_ids.reshape(-1)[None, :] < labels[:, None]).astype(jnp.int32), axis=1)
     own_start = jnp.sum(jnp.where(seg_ids[:, None] == labels[None, :], starts[None, :], 0), axis=1)
     token_index = my_index * tok + jnp.arange(tok, dtype=jnp.int32)
     cosine, sine = angles((token_index - own_start).astype(jnp.float32))
 
-    kv_rows = jnp.stack([kv_zero[:, :rows], kv_one[:, :rows]], axis=1).reshape(nx * shard, share)
-    kv_raw = jnp.dot(normed, kv_rows, preferred_element_type=jnp.float32)
+    kv_raw = jnp.dot(
+        padded, kv_all.reshape(nx * nc * ny * nz * slab, share), preferred_element_type=jnp.float32
+    )
     quarter = HD // 4
     swapped = jnp.concatenate([kv_raw[:, quarter:], kv_raw[:, :quarter]], axis=1)
     kv_share = jnp.where(it == 0, kv_raw * cosine + swapped * sine, kv_raw).astype(bf)
@@ -186,18 +200,8 @@
     kv_cache = jnp.concatenate(list(own_kv), axis=1)
     at_self = (chips == iz)[:, None, None, None] & (ic == 0)
     partner = lax.ppermute(jnp.where(at_self, own_kv[None], mine), "c", both)
-    part = nz * ny * rows
-    qo_send = jnp.concatenate([qo_near[:, :rows].reshape(part, cols), qo_near[:, rows:].reshape(part, cols)], axis=0)
-    qo_all = lax.all_gather(qo_send, ("x", "c"), axis=0, tiled=False)
-    perm = natural_to_gathered(shard, rows)
-    normed = after(normed, to_send)
-    reordered = jnp.concatenate(
-        [
-            jnp.dot(normed[:, g * shard : (g + 1) * shard], perm, preferred_element_type=jnp.float32).astype(bf)
-            for g in range(nx)
-        ],
-        axis=1,
-    )
+    perm = natural_to_gathered(shard, rows, rows)
+    reordered = turned(after(normed, to_send), perm)
     block_of_mine = my_block - (chips >= iz).astype(jnp.int32)
     block_of_partner = my_block - jnp.where(ic == 1, chips > iz, chips >= iz).astype(jnp.int32)
     first_of_mine = ((block_of_mine * nz + chips) * nc + ic) * tok
@@ -217,23 +221,22 @@
         name="queries",
     )(reordered, cosine, sine, qo_all)
     reach_back = jnp.maximum(own_start, token_index - (WINDOW - 1))
-    attended = pl.pallas_call(
+    partial = pl.pallas_call(
         attend_kernel,
-        out_shape=jax.ShapeDtypeStruct((tok, cols), bf),
-        in_specs=[vmem] * 7,
-        out_specs=vmem,
-        name="attend",
-    )(queries, mine, partner, own_kv, keys_at, token_index[:, None], reach_back[:, None])
-
-    every = lax.all_gather(attended, "tp", axis=1, tiled=True)
-    hidden = pl.pallas_call(
-        finish_kernel,
-        out_shape=jax.ShapeDtypeStruct((tok, shard), bf),
-        in_specs=[vmem, vmem, vmem, hbm],
+        out_shape=jax.ShapeDtypeStruct((nx, tok, shard), bf),
+        in_specs=[vmem] * 7 + [hbm],
         out_specs=vmem,
         scratch_shapes=scratch,
-        name="finish",
-    )(every, perm, tokens, qo_all)
+        name="attend",
+    )(queries, mine, partner, own_kv, keys_at, token_index[:, None], reach_back[:, None], qo_all)
+
+    received = lax.all_to_all(partial, "tp", 0, 0, tiled=True)
+    summed = jnp.zeros((tok, shard), jnp.float32)
+    for g in range(nx):
+        summed = summed + lax.dot_general(
+            received[g], perm, (((1,), (1,)), ((), ())), preferred_element_type=jnp.float32
+        )
+    hidden = (tokens.astype(jnp.float32) + summed).astype(bf)
     return (hidden, kv_cache)
 
 

time: 190 us -> 183 us (0.963)
  the two profiles are of different devices: /device:TPU:6 before, /device:TPU:2 now
where the time goes in v5:
time: 183 us; the launch traced here: 182 us
  waiting for transfers between devices  78.2 us (43%)
  starting transfers between devices  55.1 us (30%)
  between operations  14.6 us (8%)
  Pallas kernels  9.97 us (5%)
  matrix products  9.43 us (5%)
  other arithmetic  8.68 us (5%)
  local copies, waits for them, and re-layouts  6.46 us (4%)
    all_to_all x2, waiting for transfers between devices, spread(): return lax.all_to_all(copies, axes, 0, 0, tiled=True)  40.5 us
    all_to_all x2, starting transfers between devices, spread(): return lax.all_to_all(copies, axes, 0, 0, tiled=True)  18.7 us
    all_to_all x1, waiting for transfers between devices, per_device(): received = lax.all_to_all(partial, 'tp', 0, 0, tiled=True)  17.5 us
    ppermute x3, starting transfers between devices, per_device(): lax.ppermute(tokens, 'tp', [(i, (i + k) % nx) for i in range(nx)])  12.3 us
    ppermute x3, starting transfers between devices, per_device(): lax.ppermute(kv_share, 'tp', [(i, (i + k) % nx) for i in range(nx)])  12.2 us
    ppermute x3, waiting for transfers between devices, per_device(): lax.ppermute(kv_share, 'tp', [(i, (i + k) % nx) for i in range(nx)])  11.9 us
    ppermute x1, waiting for transfers between devices, per_device(): lax.ppermute(kv_share, SEQ, [(i, i + block) for i in range(devices - bloc...  8.16 us
    dot_general x8, matrix products, turned(): jnp.dot(values[:, g:g + per], hot, preferred_element_type=jnp.float32)  6.54 us
  transfers between devices with their start and end apart: 13, of which 6 were waited for; matrix products, arithmetic and copies ran while one was open for 11% of the time, Pallas kernels for 2%

profile of v5, /device:TPU:2, one launch (start us, length us, event | category | flops | bytes accessed | tf_op | source)
XLA Modules:
  0.0 182.5 jit_solution(2739129525867331236)
XLA Ops:
  7.2 4.6 %collective-permute-start = (bf16[128,640]{1,0:T(8,128)(2,1)}, bf16[128,640]{1,0:T(8,128)(2,1)S(1)}, u32[]{:S(2)}, u32[]{:S(2)}) collective-permute-start(bf16[128,640]{1,0:T(8,128)(2,1)} %param.6), channel_id=1, source_target_pairs={{0,2},{1,3},{2,0},{3,1},{4,6},{5,7},{6,4},{7,5},{8,10},{9,11},{10,... | collective-permute-start | bytes 491528 | tf_op jit(solution)/shard_map/ppermute | solution.py:160
  11.8 3.5 %collective-permute-start.1 = (bf16[128,640]{1,0:T(8,128)(2,1)}, bf16[128,640]{1,0:T(8,128)(2,1)S(1)}, u32[]{:S(2)}, u32[]{:S(2)}) collective-permute-start(bf16[128,640]{1,0:T(8,128)(2,1)} %param.6), channel_id=1, source_target_pairs={{0,1},{1,2},{2,3},{3,0},{4,5},{5,6},{6,7},{7,4},{8,9},{9,10},{10,1... | collective-permute-start | bytes 491528 | tf_op jit(solution)/shard_map/ppermute | solution.py:160
  15.3 4.2 %collective-permute-start.2 = (bf16[128,640]{1,0:T(8,128)(2,1)}, bf16[128,640]{1,0:T(8,128)(2,1)S(1)}, u32[]{:S(2)}, u32[]{:S(2)}) collective-permute-start(bf16[128,640]{1,0:T(8,128)(2,1)} %param.6), channel_id=1, source_target_pairs={{0,3},{1,0},{2,1},{3,2},{4,7},{5,4},{6,5},{7,6},{8,11},{9,8},{10,9... | collective-permute-start | bytes 491528 | tf_op jit(solution)/shard_map/ppermute | solution.py:160
  19.5 0.7 convert_bitcast_fusion
  20.1 0.7 constant_dynamic-slice_fusion.1
  20.8 0.7 constant_dynamic-slice_fusion
  21.5 0.8 maximum_maximum_fusion
  22.3 1.0 broadcast_in_dim.56
  23.3 13.9 %all-to-all-start = ((bf16[16,48,512]{2,1,0:T(8,128)(2,1)}), bf16[16,48,512]{2,1,0:T(8,128)(2,1)S(1)}, u32[]{:S(2)}, u32[]{:S(2)}) async-start(bf16[16,48,512]{2,1,0:T(8,128)(2,1)} %broadcast_in_dim.56), calls=%async_computation | async-start | bytes 1572864 | tf_op jit(solution)/shard_map/all_to_all | solution.py:36
  37.3 0.1 pad_add_fusion
  37.7 0.1 select_select_fusion.3
  37.8 0.2 fusion.28
  38.0 22.9 %all-to-all-done = bf16[16,48,512]{2,1,0:T(8,128)(2,1)S(1)} async-done(((bf16[16,48,512]{2,1,0:T(8,128)(2,1)}), bf16[16,48,512]{2,1,0:T(8,128)(2,1)S(1)}, u32[]{:S(2)}, u32[]{:S(2)}) %all-to-all-start) | async-done | bytes 786464 | tf_op jit(solution)/shard_map/all_to_all | solution.py:36
  60.9 0.1 fusion.79
  61.2 0.9 pad_maximum_fusion.3
  62.2 0.2 fusion.30
  62.4 0.8 convolution_convert_fusion
  63.2 0.8 convolution_convert_fusion.1
  64.0 0.8 convolution_convert_fusion.2
  64.8 1.0 broadcast_in_dim.57
  65.8 4.8 %all-to-all-start.1 = ((bf16[8,16,24,128]{3,2,1,0:T(8,128)(2,1)}), bf16[8,16,24,128]{3,2,1,0:T(8,128)(2,1)S(1)}, u32[]{:S(2)}, u32[]{:S(2)}) async-start(bf16[8,16,24,128]{3,2,1,0:T(8,128)(2,1)} %broadcast_in_dim.57), calls=%async_computation.1 | async-start | bytes 1572864 | tf_op jit(solution)/shard_map/all_to_all | solution.py:36
  70.7 0.8 convolution_convert_fusion.3
  71.5 0.1 pad_maximum_fusion
  71.6 17.6 %all-to-all-done.1 = bf16[8,16,24,128]{3,2,1,0:T(8,128)(2,1)S(1)} async-done(((bf16[8,16,24,128]{3,2,1,0:T(8,128)(2,1)}), bf16[8,16,24,128]{3,2,1,0:T(8,128)(2,1)S(1)}, u32[]{:S(2)}, u32[]{:S(2)}) %all-to-all-start.1) | async-done | bytes 786464 | tf_op jit(solution)/shard_map/all_to_all | solution.py:36
  89.1 0.1 slice_convert_fusion
  89.2 0.3 convert_reduce_fusion
  89.6 0.1 select_reduce_fusion
  89.7 0.4 fusion.82
  90.0 0.1 fusion.81
  90.1 0.3 fusion.45
  90.4 0.8 fusion.44
  91.2 1.9 %collective-permute-start.3 = (bf16[128,128]{1,0:T(8,128)(2,1)S(1)}, bf16[128,128]{1,0:T(8,128)(2,1)S(1)}, u32[]{:S(2)}, u32[]{:S(2)}) collective-permute-start(bf16[128,128]{1,0:T(8,128)(2,1)S(1)} %get-tuple-element.8), channel_id=1, source_target_pairs={{0,64},{4,68},{8,72},{12,76},{16,80},{20,84},{24,88},{28,92},{32,9... | collective-permute-start | bytes 98312 | tf_op jit(solution)/shard_map/ppermute | solution.py:193
  93.1 0.6 copy.33
  93.7 8.2 %collective-permute-done.3 = bf16[128,128]{1,0:T(8,128)(2,1)S(1)} collective-permute-done((bf16[128,128]{1,0:T(8,128)(2,1)S(1)}, bf16[128,128]{1,0:T(8,128)(2,1)S(1)}, u32[]{:S(2)}, u32[]{:S(2)}) %collective-permute-start.3) | collective-permute-done | bytes 32800 | tf_op jit(solution)/shard_map/ppermute | solution.py:193
  101.9 0.1 broadcast_select_fusion.1
  102.0 1.2 broadcast_in_dim.68
  103.2 4.4 %all-to-all-start.2 = ((bf16[32,128,128]{2,1,0:T(8,128)(2,1)}), bf16[32,128,128]{2,1,0:T(8,128)(2,1)S(1)}, u32[]{:S(2)}, u32[]{:S(2)}) async-start(bf16[32,128,128]{2,1,0:T(8,128)(2,1)} %bitcast.4), calls=%async_computation.2 | async-start | bytes 2097152 | tf_op jit(solution)/shard_map/all_to_all | solution.py:197
  107.7 0.6 iota_add_fusion.token_ref
  108.3 4.6 %collective-permute-start.4 = (bf16[128,128]{1,0:T(8,128)(2,1)S(1)}, bf16[128,128]{1,0:T(8,128)(2,1)S(1)}, u32[]{:S(2)}, u32[]{:S(2)}) collective-permute-start(bf16[128,128]{1,0:T(8,128)(2,1)S(1)} %get-tuple-element.8), channel_id=1, source_target_pairs={{0,2},{1,3},{2,0},{3,1},{4,6},{5,7},{6,4},{7,5},{8,10},{9,11},{10,... | collective-permute-start | bytes 98312 | tf_op jit(solution)/shard_map/ppermute | solution.py:198
  112.9 3.4 %collective-permute-start.5 = (bf16[128,128]{1,0:T(8,128)(2,1)S(1)}, bf16[128,128]{1,0:T(8,128)(2,1)S(1)}, u32[]{:S(2)}, u32[]{:S(2)}) collective-permute-start(bf16[128,128]{1,0:T(8,128)(2,1)S(1)} %get-tuple-element.8), channel_id=1, source_target_pairs={{0,1},{1,2},{2,3},{3,0},{4,5},{5,6},{6,7},{7,4},{8,9},{9,10},{10,1... | collective-permute-start | bytes 98312 | tf_op jit(solution)/shard_map/ppermute | solution.py:198
  116.3 4.3 %collective-permute-start.6 = (bf16[128,128]{1,0:T(8,128)(2,1)S(1)}, bf16[128,128]{1,0:T(8,128)(2,1)S(1)}, u32[]{:S(2)}, u32[]{:S(2)}) collective-permute-start(bf16[128,128]{1,0:T(8,128)(2,1)S(1)} %get-tuple-element.8), channel_id=1, source_target_pairs={{0,3},{1,0},{2,1},{3,2},{4,7},{5,4},{6,5},{7,6},{8,11},{9,8},{10,9... | collective-permute-start | bytes 98312 | tf_op jit(solution)/shard_map/ppermute | solution.py:198
  120.6 0.1 copy.28
  120.7 0.6 add_maximum_fusion.first_ref
  121.3 11.9 %collective-permute-done.4 = bf16[128,128]{1,0:T(8,128)(2,1)S(1)} collective-permute-done((bf16[128,128]{1,0:T(8,128)(2,1)S(1)}, bf16[128,128]{1,0:T(8,128)(2,1)S(1)}, u32[]{:S(2)}, u32[]{:S(2)}) %collective-permute-start.4) | collective-permute-done | bytes 32800 | tf_op jit(solution)/shard_map/ppermute | solution.py:198
  133.3 1.2 convolution_convert_fusion.4
  134.5 1.2 convolution_convert_fusion.5
  135.7 0.1 all-to-all-done.2
  135.8 0.1 broadcast_select_fusion
  135.9 2.1 %collective-permute-start.7 = (bf16[8,4,128,128]{3,2,1,0:T(8,128)(2,1)S(1)}, bf16[8,4,128,128]{3,2,1,0:T(8,128)(2,1)S(1)}, u32[]{:S(2)}, u32[]{:S(2)}) collective-permute-start(bf16[8,4,128,128]{3,2,1,0:T(8,128)(2,1)S(1)} %broadcast_select_fusion), channel_id=1, source_target_pairs={{0,4},{4,0},{1,5},{5,1},{2,6},{6,2},{3,7},{7,3},{8,12},{12,8},{9,1... | collective-permute-start | bytes 3145736 | tf_op jit(solution)/shard_map/ppermute | solution.py:202
  138.0 0.5 convolution_convert_fusion.6
  138.5 0.5 convolution_convert_fusion.7
  139.0 0.4 copy-done.6
  139.4 0.1 copy-done.7
  139.5 0.9 pad_maximum_fusion.2.normed_ref
  140.4 4.1 %queries.1.queries_ref = bf16[128,512]{1,0:T(8,128)(2,1)} custom-call(bf16[128,2560]{1,0:T(8,128)(2,1)} %pad_maximum_fusion.2.normed_ref, f32[128,128]{1,0:T(8,128)} %get-tuple-element.23.cosine_ref, f32[128,128]{1,0:T(8,128)} %get-tuple-element.9.sine_ref, bf16[8,640,512]{2,1,0:T(8,128)(2,1)} %bitcast.34), custom_call_target="tpu_custom_call" | custom-call | tf_op jit(solution)/shard_map/queries/pallas_call | solution.py:215
  144.5 0.9 copy-done.2
  145.5 5.9 %attend.1 = bf16[4,128,640]{2,1,0:T(8,128)(2,1)} custom-call(bf16[128,512]{1,0:T(8,128)(2,1)} %queries.1.queries_ref, bf16[8,4,128,128]{3,2,1,0:T(8,128)(2,1)} %bitcast.37, bf16[8,4,128,128]{3,2,1,0:T(8,128)(2,1)} %copy-done.2, bf16[4,128,128]{2,1,0:T(8,128)(2,1)} %copy-done.1, s32[1,2176]{1,0:T(1,128)} %bitcast.44, s32[128,1]{1,0:T(8,128)} %iota_add_fusion.token_ref, ...), custom_call_target="tpu_custom_call" | custom-call | tf_op jit(solution)/shard_map/attend/pallas_call | solution.py:224
  151.4 3.5 %all-to-all-start.3 = ((bf16[4,128,640]{2,1,0:T(8,128)(2,1)}), bf16[4,128,640]{2,1,0:T(8,128)(2,1)S(1)}, u32[]{:S(2)}, u32[]{:S(2)}) async-start(bf16[4,128,640]{2,1,0:T(8,128)(2,1)} %attend.1), calls=%async_computation.3 | async-start | bytes 1310720 | tf_op jit(solution)/shard_map/all_to_all | solution.py:233
  154.9 0.7 pad_maximum_fusion.5
  155.5 17.5 %all-to-all-done.3 = bf16[4,128,640]{2,1,0:T(8,128)(2,1)S(1)} async-done(((bf16[4,128,640]{2,1,0:T(8,128)(2,1)}), bf16[4,128,640]{2,1,0:T(8,128)(2,1)S(1)}, u32[]{:S(2)}, u32[]{:S(2)}) %all-to-all-start.3) | async-done | bytes 655392 | tf_op jit(solution)/shard_map/all_to_all | solution.py:233
  173.1 0.5 fusion.33
  173.5 0.5 convolution_add_fusion.2
  174.0 0.5 convolution_add_fusion.1
  174.5 1.1 fusion.32
  (48 shorter events, 0.5 us)
Async XLA Ops:
  7.2 30.5 %copy-start.5 = (bf16[128,640]{1,0:T(8,128)(2,1)S(1)}, bf16[128,640]{1,0:T(8,128)(2,1)}, u32[]{:S(2)}) copy-start(bf16[128,640]{1,0:T(8,128)(2,1)} %param.6) | copy-start | bytes 491524
  7.2 30.4 %copy-start.8 = (bf16[2560]{0:T(1024)(128)(2,1)S(1)}, bf16[2560]{0:T(1024)(128)(2,1)}, u32[]{:S(2)}) copy-start(bf16[2560]{0:T(1024)(128)(2,1)} %param.8) | copy-start | bytes 15364
  7.2 30.4 %collective-permute-start = (bf16[128,640]{1,0:T(8,128)(2,1)}, bf16[128,640]{1,0:T(8,128)(2,1)S(1)}, u32[]{:S(2)}, u32[]{:S(2)}) collective-permute-start(bf16[128,640]{1,0:T(8,128)(2,1)} %param.6), channel_id=1, source_target_pairs={{0,2},{1,3},{2,0},{3,1},{4,6},{5,7},{6,4},{7,5},{8,10},{9,11},{10,... | collective-permute-start | bytes 491528 | tf_op jit(solution)/shard_map/ppermute | solution.py:160
  11.8 25.8 %collective-permute-start.1 = (bf16[128,640]{1,0:T(8,128)(2,1)}, bf16[128,640]{1,0:T(8,128)(2,1)S(1)}, u32[]{:S(2)}, u32[]{:S(2)}) collective-permute-start(bf16[128,640]{1,0:T(8,128)(2,1)} %param.6), channel_id=1, source_target_pairs={{0,1},{1,2},{2,3},{3,0},{4,5},{5,6},{6,7},{7,4},{8,9},{9,10},{10,1... | collective-permute-start | bytes 491528 | tf_op jit(solution)/shard_map/ppermute | solution.py:160
  15.3 22.3 %collective-permute-start.2 = (bf16[128,640]{1,0:T(8,128)(2,1)}, bf16[128,640]{1,0:T(8,128)(2,1)S(1)}, u32[]{:S(2)}, u32[]{:S(2)}) collective-permute-start(bf16[128,640]{1,0:T(8,128)(2,1)} %param.6), channel_id=1, source_target_pairs={{0,3},{1,0},{2,1},{3,2},{4,7},{5,4},{6,5},{7,6},{8,11},{9,8},{10,9... | collective-permute-start | bytes 491528 | tf_op jit(solution)/shard_map/ppermute | solution.py:160
  23.3 37.6 %all-to-all-start = ((bf16[16,48,512]{2,1,0:T(8,128)(2,1)}), bf16[16,48,512]{2,1,0:T(8,128)(2,1)S(1)}, u32[]{:S(2)}, u32[]{:S(2)}) async-start(bf16[16,48,512]{2,1,0:T(8,128)(2,1)} %broadcast_in_dim.56), calls=%async_computation | async-start | bytes 1572864 | tf_op jit(solution)/shard_map/all_to_all | solution.py:36
  37.2 103.2 %all-gather.3.cloned.1.call-start = ((), (), s32[]{:S(2)}) async-start(), calls=%async_computation.4 | async-start | bytes 5898240 | tf_op jit(solution)/shard_map/all_gather | solution.py:170
  62.4 72.1 %copy-start.3 = (bf16[128,2560]{1,0:T(8,128)(2,1)}, bf16[128,2560]{1,0:T(8,128)(2,1)S(1)}, u32[]{:S(2)}) copy-start(bf16[128,2560]{1,0:T(8,128)(2,1)S(1)} %fusion.30) | copy-start | bytes 1966084
  65.8 23.3 %all-to-all-start.1 = ((bf16[8,16,24,128]{3,2,1,0:T(8,128)(2,1)}), bf16[8,16,24,128]{3,2,1,0:T(8,128)(2,1)S(1)}, u32[]{:S(2)}, u32[]{:S(2)}) async-start(bf16[8,16,24,128]{3,2,1,0:T(8,128)(2,1)} %broadcast_in_dim.57), calls=%async_computation.1 | async-start | bytes 1572864 | tf_op jit(solution)/shard_map/all_to_all | solution.py:36
  71.5 18.1 %copy-start.9 = (s32[128]{0:T(128)S(1)}, s32[128]{0:T(128)}, u32[]{:S(2)}) copy-start(s32[128]{0:T(128)} %param.7) | copy-start | bytes 1540
  91.2 10.7 %collective-permute-start.3 = (bf16[128,128]{1,0:T(8,128)(2,1)S(1)}, bf16[128,128]{1,0:T(8,128)(2,1)S(1)}, u32[]{:S(2)}, u32[]{:S(2)}) collective-permute-start(bf16[128,128]{1,0:T(8,128)(2,1)S(1)} %get-tuple-element.8), channel_id=1, source_target_pairs={{0,64},{4,68},{8,72},{12,76},{16,80},{20,84},{24,88},{28,92},{32,9... | collective-permute-start | bytes 98312 | tf_op jit(solution)/shard_map/ppermute | solution.py:193
  103.2 32.5 %all-to-all-start.2 = ((bf16[32,128,128]{2,1,0:T(8,128)(2,1)}), bf16[32,128,128]{2,1,0:T(8,128)(2,1)S(1)}, u32[]{:S(2)}, u32[]{:S(2)}) async-start(bf16[32,128,128]{2,1,0:T(8,128)(2,1)} %bitcast.4), calls=%async_computation.2 | async-start | bytes 2097152 | tf_op jit(solution)/shard_map/all_to_all | solution.py:197
  108.3 24.9 %collective-permute-start.4 = (bf16[128,128]{1,0:T(8,128)(2,1)S(1)}, bf16[128,128]{1,0:T(8,128)(2,1)S(1)}, u32[]{:S(2)}, u32[]{:S(2)}) collective-permute-start(bf16[128,128]{1,0:T(8,128)(2,1)S(1)} %get-tuple-element.8), channel_id=1, source_target_pairs={{0,2},{1,3},{2,0},{3,1},{4,6},{5,7},{6,4},{7,5},{8,10},{9,11},{10,... | collective-permute-start | bytes 98312 | tf_op jit(solution)/shard_map/ppermute | solution.py:198
  112.9 20.3 %collective-permute-start.5 = (bf16[128,128]{1,0:T(8,128)(2,1)S(1)}, bf16[128,128]{1,0:T(8,128)(2,1)S(1)}, u32[]{:S(2)}, u32[]{:S(2)}) collective-permute-start(bf16[128,128]{1,0:T(8,128)(2,1)S(1)} %get-tuple-element.8), channel_id=1, source_target_pairs={{0,1},{1,2},{2,3},{3,0},{4,5},{5,6},{6,7},{7,4},{8,9},{9,10},{10,1... | collective-permute-start | bytes 98312 | tf_op jit(solution)/shard_map/ppermute | solution.py:198
  116.3 17.0 %collective-permute-start.6 = (bf16[128,128]{1,0:T(8,128)(2,1)S(1)}, bf16[128,128]{1,0:T(8,128)(2,1)S(1)}, u32[]{:S(2)}, u32[]{:S(2)}) collective-permute-start(bf16[128,128]{1,0:T(8,128)(2,1)S(1)} %get-tuple-element.8), channel_id=1, source_target_pairs={{0,3},{1,0},{2,1},{3,2},{4,7},{5,4},{6,5},{7,6},{8,11},{9,8},{10,9... | collective-permute-start | bytes 98312 | tf_op jit(solution)/shard_map/ppermute | solution.py:198
  133.3 2.5 %copy-start.1 = (bf16[4,128,128]{2,1,0:T(8,128)(2,1)}, bf16[4,128,128]{2,1,0:T(8,128)(2,1)S(1)}, u32[]{:S(2)}) copy-start(bf16[4,128,128]{2,1,0:T(8,128)(2,1)S(1)} %pad_maximum_fusion.4.own_ref) | copy-start | bytes 393220
  135.8 2.7 %copy-start = (bf16[32,128,128]{2,1,0:T(8,128)(2,1)}, bf16[32,128,128]{2,1,0:T(8,128)(2,1)S(1)}, u32[]{:S(2)}) copy-start(bf16[32,128,128]{2,1,0:T(8,128)(2,1)S(1)} %all-to-all-done.2) | copy-start | bytes 3145732
  135.8 2.2 %copy-start.4 = (bf16[128,2560]{1,0:T(8,128)(2,1)S(1)}, bf16[128,2560]{1,0:T(8,128)(2,1)}, u32[]{:S(2)}) copy-start(bf16[128,2560]{1,0:T(8,128)(2,1)} %copy-done.3) | copy-start | bytes 1966084
  135.9 8.6 %collective-permute-start.7 = (bf16[8,4,128,128]{3,2,1,0:T(8,128)(2,1)S(1)}, bf16[8,4,128,128]{3,2,1,0:T(8,128)(2,1)S(1)}, u32[]{:S(2)}, u32[]{:S(2)}) collective-permute-start(bf16[8,4,128,128]{3,2,1,0:T(8,128)(2,1)S(1)} %broadcast_select_fusion), channel_id=1, source_target_pairs={{0,4},{4,0},{1,5},{5,1},{2,6},{6,2},{3,7},{7,3},{8,12},{12,8},{9,1... | collective-permute-start | bytes 3145736 | tf_op jit(solution)/shard_map/ppermute | solution.py:202
  138.5 0.9 copy-start.6
  138.5 1.0 copy-start.7
  144.5 1.0 copy-start.2
  151.4 21.7 %all-to-all-start.3 = ((bf16[4,128,640]{2,1,0:T(8,128)(2,1)}), bf16[4,128,640]{2,1,0:T(8,128)(2,1)S(1)}, u32[]{:S(2)}, u32[]{:S(2)}) async-start(bf16[4,128,640]{2,1,0:T(8,128)(2,1)} %attend.1), calls=%async_computation.3 | async-start | bytes 1310720 | tf_op jit(solution)/shard_map/all_to_all | solution.py:233
Sparse Core Ops, SparseCore 0:
  62.3 42.0 all-gather.2

commit v6 on v5

--- a/solution.py
+++ b/solution.py
@@ -48,14 +48,15 @@
     return ordered
 
 
-def natural_to_gathered(per, rows, slab):
+def natural_to_gathered(per, rows, slab, ny, core_first):
+    nz = per // rows // ny // 2
     width = per // rows * slab
     nat = lax.broadcasted_iota(jnp.int32, (per, width), 0)
     gat = lax.broadcasted_iota(jnp.int32, (per, width), 1)
-    half = width // 2
-    core, rest = gat // half, gat % half
-    place, row = rest // slab, rest % slab
-    source = (place * 2 + core) * rows + row
+    place, row = gat // slab, gat % slab
+    outer, z = place // nz, place % nz
+    core, half = (outer // ny, outer % ny) if core_first else (outer % 2, outer // 2)
+    source = ((half * nz + z) * 2 + core) * rows + row
     return ((nat == source) & (row < rows)).astype(jnp.bfloat16)
 
 
@@ -153,28 +154,38 @@
     share = 2 * HD // nx
     slab = rows + 4
     ids = jnp.pad(seg_ids.astype(bf)[None, :], ((0, 31 - rows), (0, 0)))
-    kv_slab = jnp.concatenate([lax.dynamic_slice_in_dim(w_keyval, it * share, share, 1), ids], axis=0)
+    chosen = w_keyval[:, (nx - 1) * share :]
+    for t in range(nx - 1):
+        chosen = jnp.where(it == t, w_keyval[:, t * share : (t + 1) * share], chosen)
+    kv_slab = jnp.concatenate([chosen, ids], axis=0)
     folded = jnp.concatenate([kv_slab[i : i + 8] for i in range(0, 32, 8)], axis=1)
-    near = spread(jnp.concatenate([w_query, w_out.T, folded], axis=0), ("yh", "z"), ny * nz)
+    near = spread(jnp.concatenate([w_query, w_out.T, folded], axis=0), "z", nz)
 
     others = [lax.ppermute(tokens, "tp", [(i, (i + k) % nx) for i in range(nx)]) for k in range(1, nx)]
 
     kv_near = jnp.concatenate(
         [near[:, 2 * rows :, i * share : (i + 1) * share] for i in range(slab // 8)], axis=1
     )
-    kv_all = spread(kv_near, ("x", "c"), nx * nc)
-    part = nz * ny * rows
+    kv_mine = spread(kv_near, ("x", "yh"), nx * ny)
+    kv_twin = lax.ppermute(kv_mine, "c", both)
+    part = nz * rows
     qo_send = jnp.concatenate(
         [near[:, :rows].reshape(part, cols), near[:, rows : 2 * rows].reshape(part, cols)], axis=0
     )
-    qo_all = lax.all_gather(qo_send, ("x", "c"), axis=0, tiled=False)
-
-    groups = in_order([tokens, *others], it)
-    normed = rms_norm(jnp.concatenate(groups, axis=1), norm_gain)
-    padded = turned(normed, natural_to_gathered(shard, rows, slab))
-    kv_all, padded = lax.optimization_barrier((kv_all, padded))
-
-    all_ids = kv_all[:, :, rows].astype(jnp.int32)
+    qo_all = lax.all_gather(qo_send, ("x", "yh", "c"), axis=0, tiled=False)
+
+    normed = rms_norm(jnp.concatenate(in_order([tokens, *others], it), axis=1), norm_gain)
+    padded = turned(normed, natural_to_gathered(shard, rows, slab, ny, True))
+    half = ny * nz * slab
+    of_core = [
+        jnp.concatenate([padded[:, i * half : (i + 1) * half] for i in range(c, nx * nc, nc)], axis=1)
+        for c in range(nc)
+    ]
+    for_mine = jnp.where(ic == 0, of_core[0], of_core[1])
+    for_twin = jnp.where(ic == 0, of_core[1], of_core[0])
+    kv_mine, for_mine, for_twin = lax.optimization_barrier((kv_mine, for_mine, for_twin))
+
+    all_ids = jnp.concatenate([kv_mine[:, :, rows], kv_twin[:, :, rows]], axis=0).astype(jnp.int32)
     labels = jnp.arange(SEGS, dtype=jnp.int32)
     starts = jnp.sum((all_ids.reshape(-1)[None, :] < labels[:, None]).astype(jnp.int32), axis=1)
     own_start = jnp.sum(jnp.where(seg_ids[:, None] == labels[None, :], starts[None, :], 0), axis=1)
@@ -182,8 +193,8 @@
     cosine, sine = angles((token_index - own_start).astype(jnp.float32))
 
     kv_raw = jnp.dot(
-        padded, kv_all.reshape(nx * nc * ny * nz * slab, share), preferred_element_type=jnp.float32
-    )
+        for_mine, kv_mine.reshape(nx * half, share), preferred_element_type=jnp.float32
+    ) + jnp.dot(for_twin, kv_twin.reshape(nx * half, share), preferred_element_type=jnp.float32)
     quarter = HD // 4
     swapped = jnp.concatenate([kv_raw[:, quarter:], kv_raw[:, :quarter]], axis=1)
     kv_share = jnp.where(it == 0, kv_raw * cosine + swapped * sine, kv_raw).astype(bf)
@@ -200,7 +211,7 @@
     kv_cache = jnp.concatenate(list(own_kv), axis=1)
     at_self = (chips == iz)[:, None, None, None] & (ic == 0)
     partner = lax.ppermute(jnp.where(at_self, own_kv[None], mine), "c", both)
-    perm = natural_to_gathered(shard, rows, rows)
+    perm = natural_to_gathered(shard, rows, rows, ny, False)
     reordered = turned(after(normed, to_send), perm)
     block_of_mine = my_block - (chips >= iz).astype(jnp.int32)
     block_of_partner = my_block - jnp.where(ic == 1, chips > iz, chips >= iz).astype(jnp.int32)
@@ -211,7 +222,7 @@
 
     vmem = pl.BlockSpec(memory_space=pltpu.VMEM)
     hbm = pl.BlockSpec(memory_space=pl.ANY)
-    scratch = [pltpu.VMEM((nx * nc * part, cols), bf), pltpu.SemaphoreType.DMA((nx * nc,))]
+    scratch = [pltpu.VMEM((nx * shard, cols), bf), pltpu.SemaphoreType.DMA((nx * ny * nc,))]
     queries = pl.pallas_call(
         queries_kernel,
         out_shape=jax.ShapeDtypeStruct((tok, cols), bf),

time: 183 us -> 196 us (1.071)
  waiting for transfers between devices: 78.2 us -> 84.9 us
  starting transfers between devices: 55.1 us -> 60.2 us
  matrix products: 9.43 us -> 11.4 us
    all_to_all x1, waiting for transfers between devices: 0.08 us -> 30.6 us  [per_device(): lax.all_to_all(to_send, ('z', 'tp'), 0, 0, tiled=True)]
    all_to_all x2, waiting for transfers between devices: 40.5 us -> 26.8 us  [spread(): return lax.all_to_all(copies, axes, 0, 0, tiled=True)]
    ppermute x3, waiting for transfers between devices: 11.9 us -> 0.01 us  [per_device(): lax.ppermute(kv_share, 'tp', [(i, (i + k) % nx) for i in range(nx)])]
    all_to_all x1, starting transfers between devices: 3.49 us -> 5.51 us  [per_device(): received = lax.all_to_all(partial, 'tp', 0, 0, tiled=True)]
  transfers between devices with their start and end apart: 13 -> 14, of which waited for: 6 -> 6; matrix products, arithmetic and copies ran while one was open for 11% -> 11% of each run, Pallas kernels for 2% -> 2%
where the time goes in v6:
time: 196 us; the launch traced here: 195 us
  waiting for transfers between devices  84.9 us (43%)
  starting transfers between devices  60.2 us (31%)
  between operations  14.6 us (7%)
  matrix products  11.4 us (6%)
  Pallas kernels  10.2 us (5%)
  other arithmetic  9.23 us (5%)
  local copies, waits for them, and re-layouts  4.95 us (3%)
    all_to_all x1, waiting for transfers between devices, per_device(): lax.all_to_all(to_send, ('z', 'tp'), 0, 0, tiled=True)  30.6 us
    all_to_all x2, waiting for transfers between devices, spread(): return lax.all_to_all(copies, axes, 0, 0, tiled=True)  26.8 us
    all_to_all x2, starting transfers between devices, spread(): return lax.all_to_all(copies, axes, 0, 0, tiled=True)  18.6 us
    all_to_all x1, waiting for transfers between devices, per_device(): received = lax.all_to_all(partial, 'tp', 0, 0, tiled=True)  17.3 us
    ppermute x3, starting transfers between devices, per_device(): lax.ppermute(tokens, 'tp', [(i, (i + k) % nx) for i in range(nx)])  12.3 us
    ppermute x3, starting transfers between devices, per_device(): lax.ppermute(kv_share, 'tp', [(i, (i + k) % nx) for i in range(nx)])  11.9 us
    ppermute x1, waiting for transfers between devices, per_device(): lax.ppermute(kv_share, SEQ, [(i, i + block) for i in range(devices - bloc...  8.96 us
    dot_general x8, matrix products, turned(): jnp.dot(values[:, g:g + per], hot, preferred_element_type=jnp.float32)  8.29 us
  transfers between devices with their start and end apart: 14, of which 6 were waited for; matrix products, arithmetic and copies ran while one was open for 11% of the time, Pallas kernels for 2%

profile of v6, /device:TPU:2, one launch (start us, length us, event | category | flops | bytes accessed | tf_op | source)
XLA Modules:
  0.0 195.5 jit_solution(3945631193742754024)
XLA Ops:
  7.2 4.6 %collective-permute-start = (bf16[128,640]{1,0:T(8,128)(2,1)}, bf16[128,640]{1,0:T(8,128)(2,1)S(1)}, u32[]{:S(2)}, u32[]{:S(2)}) collective-permute-start(bf16[128,640]{1,0:T(8,128)(2,1)} %param.6), channel_id=1, source_target_pairs={{0,2},{1,3},{2,0},{3,1},{4,6},{5,7},{6,4},{7,5},{8,10},{9,11},{10,... | collective-permute-start | bytes 491528 | tf_op jit(solution)/shard_map/ppermute | solution.py:164
  11.8 3.5 %collective-permute-start.1 = (bf16[128,640]{1,0:T(8,128)(2,1)}, bf16[128,640]{1,0:T(8,128)(2,1)S(1)}, u32[]{:S(2)}, u32[]{:S(2)}) collective-permute-start(bf16[128,640]{1,0:T(8,128)(2,1)} %param.6), channel_id=1, source_target_pairs={{0,1},{1,2},{2,3},{3,0},{4,5},{5,6},{6,7},{7,4},{8,9},{9,10},{10,1... | collective-permute-start | bytes 491528 | tf_op jit(solution)/shard_map/ppermute | solution.py:164
  15.3 4.2 %collective-permute-start.2 = (bf16[128,640]{1,0:T(8,128)(2,1)}, bf16[128,640]{1,0:T(8,128)(2,1)S(1)}, u32[]{:S(2)}, u32[]{:S(2)}) collective-permute-start(bf16[128,640]{1,0:T(8,128)(2,1)} %param.6), channel_id=1, source_target_pairs={{0,3},{1,0},{2,1},{3,2},{4,7},{5,4},{6,5},{7,6},{8,11},{9,8},{10,9... | collective-permute-start | bytes 491528 | tf_op jit(solution)/shard_map/ppermute | solution.py:164
  19.5 0.7 convert_bitcast_fusion
  20.1 0.7 select_select_fusion.10
  20.9 0.8 maximum_maximum_fusion
  21.7 0.8 broadcast_in_dim.56
  22.5 10.3 %all-to-all-start = ((bf16[8,48,512]{2,1,0:T(8,128)(2,1)}), bf16[8,48,512]{2,1,0:T(8,128)(2,1)S(1)}, u32[]{:S(2)}, u32[]{:S(2)}) async-start(bf16[8,48,512]{2,1,0:T(8,128)(2,1)} %broadcast_in_dim.56), calls=%async_computation | async-start | bytes 786432 | tf_op jit(solution)/shard_map/all_to_all | solution.py:36
  33.0 0.1 pad_add_fusion
  33.1 0.1 add_bitcast_fusion
  33.2 0.7 convert_element_type.77
  33.9 0.6 copy.36
  34.5 0.6 iota_add_fusion.token_ref
  35.1 0.1 select_select_fusion.5
  35.3 0.2 fusion.30
  35.5 0.2 fusion.32
  35.7 0.8 convolution_convert_fusion.3
  36.6 10.0 %all-to-all-done = bf16[8,48,512]{2,1,0:T(8,128)(2,1)S(1)} async-done(((bf16[8,48,512]{2,1,0:T(8,128)(2,1)}), bf16[8,48,512]{2,1,0:T(8,128)(2,1)S(1)}, u32[]{:S(2)}, u32[]{:S(2)}) %all-to-all-start) | async-done | bytes 393248 | tf_op jit(solution)/shard_map/all_to_all | solution.py:36
  46.6 0.1 fusion.82
  46.8 0.7 pad_maximum_fusion.4
  47.6 0.8 convolution_convert_fusion.2
  48.4 0.8 convolution_convert_fusion.1
  49.2 0.8 convolution_convert_fusion
  50.1 0.8 broadcast_in_dim.57
  50.9 8.3 %all-to-all-start.1 = ((bf16[8,8,24,128]{3,2,1,0:T(8,128)(2,1)}), bf16[8,8,24,128]{3,2,1,0:T(8,128)(2,1)S(1)}, u32[]{:S(2)}, u32[]{:S(2)}) async-start(bf16[8,8,24,128]{3,2,1,0:T(8,128)(2,1)} %broadcast_in_dim.57), calls=%async_computation.1 | async-start | bytes 786432 | tf_op jit(solution)/shard_map/all_to_all | solution.py:36
  59.3 16.7 %all-to-all-done.1 = bf16[8,8,24,128]{3,2,1,0:T(8,128)(2,1)S(1)} async-done(((bf16[8,8,24,128]{3,2,1,0:T(8,128)(2,1)}), bf16[8,8,24,128]{3,2,1,0:T(8,128)(2,1)S(1)}, u32[]{:S(2)}, u32[]{:S(2)}) %all-to-all-start.1) | async-done | bytes 393248 | tf_op jit(solution)/shard_map/all_to_all | solution.py:36
  76.0 1.9 collective-permute-start.3
  77.9 0.1 broadcast_select_fusion.1
  78.1 0.3 fusion.90
  78.3 1.2 collective-permute-done.3
  79.7 0.3 convert_reduce_fusion
  80.0 0.1 select_reduce_fusion
  80.1 0.3 convolution_add_fusion.3
  80.3 0.1 fusion.88
  80.4 0.3 fusion.48
  80.7 0.8 fusion.46
  81.5 4.2 %collective-permute-start.5 = (bf16[128,128]{1,0:T(8,128)(2,1)S(1)}, bf16[128,128]{1,0:T(8,128)(2,1)S(1)}, u32[]{:S(2)}, u32[]{:S(2)}) collective-permute-start(bf16[128,128]{1,0:T(8,128)(2,1)S(1)} %get-tuple-element.10), channel_id=1, source_target_pairs={{0,2},{1,3},{2,0},{3,1},{4,6},{5,7},{6,4},{7,5},{8,10},{9,11},{10,... | collective-permute-start | bytes 98312 | tf_op jit(solution)/shard_map/ppermute | solution.py:209
  85.8 1.9 collective-permute-start.6
  87.7 5.7 %collective-permute-start.7 = (bf16[128,128]{1,0:T(8,128)(2,1)S(1)}, bf16[128,128]{1,0:T(8,128)(2,1)S(1)}, u32[]{:S(2)}, u32[]{:S(2)}) collective-permute-start(bf16[128,128]{1,0:T(8,128)(2,1)S(1)} %get-tuple-element.10), channel_id=1, source_target_pairs={{0,3},{1,0},{2,1},{3,2},{4,7},{5,4},{6,5},{7,6},{8,11},{9,8},{10,9... | collective-permute-start | bytes 98312 | tf_op jit(solution)/shard_map/ppermute | solution.py:209
  93.4 3.1 %collective-permute-start.4 = (bf16[128,128]{1,0:T(8,128)(2,1)S(1)}, bf16[128,128]{1,0:T(8,128)(2,1)S(1)}, u32[]{:S(2)}, u32[]{:S(2)}) collective-permute-start(bf16[128,128]{1,0:T(8,128)(2,1)S(1)} %get-tuple-element.10), channel_id=1, source_target_pairs={{0,64},{4,68},{8,72},{12,76},{16,80},{20,84},{24,88},{28,92},{32,9... | collective-permute-start | bytes 98312 | tf_op jit(solution)/shard_map/ppermute | solution.py:204
  96.5 0.1 copy.24
  96.6 0.6 add_maximum_fusion.first_ref
  97.2 9.0 %collective-permute-done.4 = bf16[128,128]{1,0:T(8,128)(2,1)S(1)} collective-permute-done((bf16[128,128]{1,0:T(8,128)(2,1)S(1)}, bf16[128,128]{1,0:T(8,128)(2,1)S(1)}, u32[]{:S(2)}, u32[]{:S(2)}) %collective-permute-start.4) | collective-permute-done | bytes 32800 | tf_op jit(solution)/shard_map/ppermute | solution.py:204
  106.2 0.1 broadcast_select_fusion.3
  106.3 1.2 broadcast_in_dim.68
  107.5 4.8 %all-to-all-start.2 = ((bf16[32,128,128]{2,1,0:T(8,128)(2,1)}), bf16[32,128,128]{2,1,0:T(8,128)(2,1)S(1)}, u32[]{:S(2)}, u32[]{:S(2)}) async-start(bf16[32,128,128]{2,1,0:T(8,128)(2,1)} %bitcast.5), calls=%async_computation.2 | async-start | bytes 2097152 | tf_op jit(solution)/shard_map/all_to_all | solution.py:208
  112.5 1.2 convolution_convert_fusion.5
  113.7 1.2 convolution_convert_fusion.6
  114.9 1.2 convolution_convert_fusion.7
  116.1 30.6 %all-to-all-done.2 = bf16[32,128,128]{2,1,0:T(8,128)(2,1)S(1)} async-done(((bf16[32,128,128]{2,1,0:T(8,128)(2,1)}), bf16[32,128,128]{2,1,0:T(8,128)(2,1)S(1)}, u32[]{:S(2)}, u32[]{:S(2)}) %all-to-all-start.2) | async-done | bytes 1048608 | tf_op jit(solution)/shard_map/all_to_all | solution.py:208
  146.7 0.1 broadcast_select_fusion
  146.9 2.1 %collective-permute-start.8 = (bf16[8,4,128,128]{3,2,1,0:T(8,128)(2,1)S(1)}, bf16[8,4,128,128]{3,2,1,0:T(8,128)(2,1)S(1)}, u32[]{:S(2)}, u32[]{:S(2)}) collective-permute-start(bf16[8,4,128,128]{3,2,1,0:T(8,128)(2,1)S(1)} %broadcast_select_fusion), channel_id=1, source_target_pairs={{0,4},{4,0},{1,5},{5,1},{2,6},{6,2},{3,7},{7,3},{8,12},{12,8},{9,1... | collective-permute-start | bytes 3145736 | tf_op jit(solution)/shard_map/ppermute | solution.py:213
  148.9 1.4 convolution_convert_fusion.4
  150.4 0.9 pad_maximum_fusion.1.normed_ref
  151.3 4.3 %queries.1.queries_ref = bf16[128,512]{1,0:T(8,128)(2,1)} custom-call(bf16[128,2560]{1,0:T(8,128)(2,1)} %pad_maximum_fusion.1.normed_ref, f32[128,128]{1,0:T(8,128)} %get-tuple-element.35.cosine_ref, f32[128,128]{1,0:T(8,128)} %get-tuple-element.11.sine_ref, bf16[16,320,512]{2,1,0:T(8,128)(2,1)} %bitcast.47), custom_call_target="tpu_custom_call" | custom-call | tf_op jit(solution)/shard_map/queries/pallas_call | solution.py:226
  155.6 1.0 copy-done.2
  156.6 5.9 %attend.1 = bf16[4,128,640]{2,1,0:T(8,128)(2,1)} custom-call(bf16[128,512]{1,0:T(8,128)(2,1)} %queries.1.queries_ref, bf16[8,4,128,128]{3,2,1,0:T(8,128)(2,1)} %bitcast.50, bf16[8,4,128,128]{3,2,1,0:T(8,128)(2,1)} %copy-done.2, bf16[4,128,128]{2,1,0:T(8,128)(2,1)} %copy-done.1, s32[1,2176]{1,0:T(1,128)} %bitcast.59, s32[128,1]{1,0:T(8,128)} %iota_add_fusion.token_ref, ...), custom_call_target="tpu_custom_call" | custom-call | tf_op jit(solution)/shard_map/attend/pallas_call | solution.py:235
  162.5 5.5 %all-to-all-start.3 = ((bf16[4,128,640]{2,1,0:T(8,128)(2,1)}), bf16[4,128,640]{2,1,0:T(8,128)(2,1)S(1)}, u32[]{:S(2)}, u32[]{:S(2)}) async-start(bf16[4,128,640]{2,1,0:T(8,128)(2,1)} %attend.1), calls=%async_computation.3 | async-start | bytes 1310720 | tf_op jit(solution)/shard_map/all_to_all | solution.py:244
  168.0 0.7 pad_maximum_fusion.6
  168.7 17.3 %all-to-all-done.3 = bf16[4,128,640]{2,1,0:T(8,128)(2,1)S(1)} async-done(((bf16[4,128,640]{2,1,0:T(8,128)(2,1)}), bf16[4,128,640]{2,1,0:T(8,128)(2,1)S(1)}, u32[]{:S(2)}, u32[]{:S(2)}) %all-to-all-start.3) | async-done | bytes 655392 | tf_op jit(solution)/shard_map/all_to_all | solution.py:244
  186.0 0.5 fusion.35
  186.5 0.5 convolution_add_fusion.2
  187.0 0.5 convolution_add_fusion.1
  187.5 1.2 fusion.34
  (57 shorter events, 0.6 us)
Async XLA Ops:
  7.2 28.0 %copy-start.4 = (bf16[128,640]{1,0:T(8,128)(2,1)S(1)}, bf16[128,640]{1,0:T(8,128)(2,1)}, u32[]{:S(2)}) copy-start(bf16[128,640]{1,0:T(8,128)(2,1)} %param.6) | copy-start | bytes 491524
  7.2 27.9 %collective-permute-start = (bf16[128,640]{1,0:T(8,128)(2,1)}, bf16[128,640]{1,0:T(8,128)(2,1)S(1)}, u32[]{:S(2)}, u32[]{:S(2)}) collective-permute-start(bf16[128,640]{1,0:T(8,128)(2,1)} %param.6), channel_id=1, source_target_pairs={{0,2},{1,3},{2,0},{3,1},{4,6},{5,7},{6,4},{7,5},{8,10},{9,11},{10,... | collective-permute-start | bytes 491528 | tf_op jit(solution)/shard_map/ppermute | solution.py:164
  11.8 23.3 %collective-permute-start.1 = (bf16[128,640]{1,0:T(8,128)(2,1)}, bf16[128,640]{1,0:T(8,128)(2,1)S(1)}, u32[]{:S(2)}, u32[]{:S(2)}) collective-permute-start(bf16[128,640]{1,0:T(8,128)(2,1)} %param.6), channel_id=1, source_target_pairs={{0,1},{1,2},{2,3},{3,0},{4,5},{5,6},{6,7},{7,4},{8,9},{9,10},{10,1... | collective-permute-start | bytes 491528 | tf_op jit(solution)/shard_map/ppermute | solution.py:164
  15.3 19.8 %collective-permute-start.2 = (bf16[128,640]{1,0:T(8,128)(2,1)}, bf16[128,640]{1,0:T(8,128)(2,1)S(1)}, u32[]{:S(2)}, u32[]{:S(2)}) collective-permute-start(bf16[128,640]{1,0:T(8,128)(2,1)} %param.6), channel_id=1, source_target_pairs={{0,3},{1,0},{2,1},{3,2},{4,7},{5,4},{6,5},{7,6},{8,11},{9,8},{10,9... | collective-permute-start | bytes 491528 | tf_op jit(solution)/shard_map/ppermute | solution.py:164
  22.5 24.2 %all-to-all-start = ((bf16[8,48,512]{2,1,0:T(8,128)(2,1)}), bf16[8,48,512]{2,1,0:T(8,128)(2,1)S(1)}, u32[]{:S(2)}, u32[]{:S(2)}) async-start(bf16[8,48,512]{2,1,0:T(8,128)(2,1)} %broadcast_in_dim.56), calls=%async_computation | async-start | bytes 786432 | tf_op jit(solution)/shard_map/all_to_all | solution.py:36
  32.8 118.5 %all-gather.3.cloned.1.call-start = ((), (), s32[]{:S(2)}) async-start(), calls=%async_computation.4 | async-start | bytes 5570560 | tf_op jit(solution)/shard_map/all_gather | solution.py:175
  35.7 79.2 %copy-start.3 = (bf16[128,2560]{1,0:T(8,128)(2,1)}, bf16[128,2560]{1,0:T(8,128)(2,1)S(1)}, u32[]{:S(2)}) copy-start(bf16[128,2560]{1,0:T(8,128)(2,1)S(1)} %fusion.32) | copy-start | bytes 1966084
  50.9 25.1 %all-to-all-start.1 = ((bf16[8,8,24,128]{3,2,1,0:T(8,128)(2,1)}), bf16[8,8,24,128]{3,2,1,0:T(8,128)(2,1)S(1)}, u32[]{:S(2)}, u32[]{:S(2)}) async-start(bf16[8,8,24,128]{3,2,1,0:T(8,128)(2,1)} %broadcast_in_dim.57), calls=%async_computation.1 | async-start | bytes 786432 | tf_op jit(solution)/shard_map/all_to_all | solution.py:36
  59.2 20.8 %copy-start.8 = (s32[128]{0:T(128)S(1)}, s32[128]{0:T(128)}, u32[]{:S(2)}) copy-start(s32[128]{0:T(128)} %param.7) | copy-start | bytes 1540
  76.0 3.6 %collective-permute-start.3 = (bf16[8,8,24,128]{3,2,1,0:T(8,128)(2,1)S(1)}, bf16[8,8,24,128]{3,2,1,0:T(8,128)(2,1)S(1)}, u32[]{:S(2)}, u32[]{:S(2)}) collective-permute-start(bf16[8,8,24,128]{3,2,1,0:T(8,128)(2,1)S(1)} %all-to-all-done.1), channel_id=1, source_target_pairs={{0,4},{4,0},{1,5},{5,1},{2,6},{6,2},{3,7},{7,3},{8,12},{12,8},{9,1... | collective-permute-start | bytes 1179656 | tf_op jit(solution)/shard_map/ppermute | solution.py:170
  81.5 30.9 %collective-permute-start.5 = (bf16[128,128]{1,0:T(8,128)(2,1)S(1)}, bf16[128,128]{1,0:T(8,128)(2,1)S(1)}, u32[]{:S(2)}, u32[]{:S(2)}) collective-permute-start(bf16[128,128]{1,0:T(8,128)(2,1)S(1)} %get-tuple-element.10), channel_id=1, source_target_pairs={{0,2},{1,3},{2,0},{3,1},{4,6},{5,7},{6,4},{7,5},{8,10},{9,11},{10,... | collective-permute-start | bytes 98312 | tf_op jit(solution)/shard_map/ppermute | solution.py:209
  85.8 26.6 %collective-permute-start.6 = (bf16[128,128]{1,0:T(8,128)(2,1)S(1)}, bf16[128,128]{1,0:T(8,128)(2,1)S(1)}, u32[]{:S(2)}, u32[]{:S(2)}) collective-permute-start(bf16[128,128]{1,0:T(8,128)(2,1)S(1)} %get-tuple-element.10), channel_id=1, source_target_pairs={{0,1},{1,2},{2,3},{3,0},{4,5},{5,6},{6,7},{7,4},{8,9},{9,10},{10,1... | collective-permute-start | bytes 98312 | tf_op jit(solution)/shard_map/ppermute | solution.py:209
  87.7 24.7 %collective-permute-start.7 = (bf16[128,128]{1,0:T(8,128)(2,1)S(1)}, bf16[128,128]{1,0:T(8,128)(2,1)S(1)}, u32[]{:S(2)}, u32[]{:S(2)}) collective-permute-start(bf16[128,128]{1,0:T(8,128)(2,1)S(1)} %get-tuple-element.10), channel_id=1, source_target_pairs={{0,3},{1,0},{2,1},{3,2},{4,7},{5,4},{6,5},{7,6},{8,11},{9,8},{10,9... | collective-permute-start | bytes 98312 | tf_op jit(solution)/shard_map/ppermute | solution.py:209
  93.4 12.8 %collective-permute-start.4 = (bf16[128,128]{1,0:T(8,128)(2,1)S(1)}, bf16[128,128]{1,0:T(8,128)(2,1)S(1)}, u32[]{:S(2)}, u32[]{:S(2)}) collective-permute-start(bf16[128,128]{1,0:T(8,128)(2,1)S(1)} %get-tuple-element.10), channel_id=1, source_target_pairs={{0,64},{4,68},{8,72},{12,76},{16,80},{20,84},{24,88},{28,92},{32,9... | collective-permute-start | bytes 98312 | tf_op jit(solution)/shard_map/ppermute | solution.py:204
  107.5 39.1 %all-to-all-start.2 = ((bf16[32,128,128]{2,1,0:T(8,128)(2,1)}), bf16[32,128,128]{2,1,0:T(8,128)(2,1)S(1)}, u32[]{:S(2)}, u32[]{:S(2)}) async-start(bf16[32,128,128]{2,1,0:T(8,128)(2,1)} %bitcast.5), calls=%async_computation.2 | async-start | bytes 2097152 | tf_op jit(solution)/shard_map/all_to_all | solution.py:208
  112.5 34.2 %copy-start.1 = (bf16[4,128,128]{2,1,0:T(8,128)(2,1)}, bf16[4,128,128]{2,1,0:T(8,128)(2,1)S(1)}, u32[]{:S(2)}) copy-start(bf16[4,128,128]{2,1,0:T(8,128)(2,1)S(1)} %pad_maximum_fusion.5.own_ref) | copy-start | bytes 393220
  146.7 3.7 %copy-start = (bf16[32,128,128]{2,1,0:T(8,128)(2,1)}, bf16[32,128,128]{2,1,0:T(8,128)(2,1)S(1)}, u32[]{:S(2)}) copy-start(bf16[32,128,128]{2,1,0:T(8,128)(2,1)S(1)} %all-to-all-done.2) | copy-start | bytes 3145732
  146.8 3.5 %copy-start.5 = (bf16[128,640]{1,0:T(8,128)(2,1)S(1)}, bf16[128,640]{1,0:T(8,128)(2,1)}, u32[]{:S(2)}) copy-start(bf16[128,640]{1,0:T(8,128)(2,1)} %convolution_convert_fusion.5) | copy-start | bytes 491524
  146.8 3.5 %copy-start.6 = (bf16[128,640]{1,0:T(8,128)(2,1)S(1)}, bf16[128,640]{1,0:T(8,128)(2,1)}, u32[]{:S(2)}) copy-start(bf16[128,640]{1,0:T(8,128)(2,1)} %convolution_convert_fusion.6) | copy-start | bytes 491524
  146.9 3.5 %copy-start.7 = (bf16[128,640]{1,0:T(8,128)(2,1)S(1)}, bf16[128,640]{1,0:T(8,128)(2,1)}, u32[]{:S(2)}) copy-start(bf16[128,640]{1,0:T(8,128)(2,1)} %convolution_convert_fusion.7) | copy-start | bytes 491524
  146.9 8.7 %collective-permute-start.8 = (bf16[8,4,128,128]{3,2,1,0:T(8,128)(2,1)S(1)}, bf16[8,4,128,128]{3,2,1,0:T(8,128)(2,1)S(1)}, u32[]{:S(2)}, u32[]{:S(2)}) collective-permute-start(bf16[8,4,128,128]{3,2,1,0:T(8,128)(2,1)S(1)} %broadcast_select_fusion), channel_id=1, source_target_pairs={{0,4},{4,0},{1,5},{5,1},{2,6},{6,2},{3,7},{7,3},{8,12},{12,8},{9,1... | collective-permute-start | bytes 3145736 | tf_op jit(solution)/shard_map/ppermute | solution.py:213
  155.6 1.0 copy-start.2
  162.5 23.5 %all-to-all-start.3 = ((bf16[4,128,640]{2,1,0:T(8,128)(2,1)}), bf16[4,128,640]{2,1,0:T(8,128)(2,1)S(1)}, u32[]{:S(2)}, u32[]{:S(2)}) async-start(bf16[4,128,640]{2,1,0:T(8,128)(2,1)} %attend.1), calls=%async_computation.3 | async-start | bytes 1310720 | tf_op jit(solution)/shard_map/all_to_all | solution.py:244
Sparse Core Ops, SparseCore 0:
  47.7 85.4 all-gather.2

commit v7 on v6

--- a/solution.py
+++ b/solution.py
@@ -48,14 +48,14 @@
     return ordered
 
 
-def natural_to_gathered(per, rows, slab, ny, core_first):
+def natural_to_gathered(per, rows, slab, ny, z_first):
     nz = per // rows // ny // 2
     width = per // rows * slab
     nat = lax.broadcasted_iota(jnp.int32, (per, width), 0)
     gat = lax.broadcasted_iota(jnp.int32, (per, width), 1)
     place, row = gat // slab, gat % slab
-    outer, z = place // nz, place % nz
-    core, half = (outer // ny, outer % ny) if core_first else (outer % 2, outer // 2)
+    core, rest = place // (ny * nz), place % (ny * nz)
+    z, half = (rest // ny, rest % ny) if z_first else (rest % nz, rest // nz)
     source = ((half * nz + z) * 2 + core) * rows + row
     return ((nat == source) & (row < rows)).astype(jnp.bfloat16)
 
@@ -159,23 +159,27 @@
         chosen = jnp.where(it == t, w_keyval[:, t * share : (t + 1) * share], chosen)
     kv_slab = jnp.concatenate([chosen, ids], axis=0)
     folded = jnp.concatenate([kv_slab[i : i + 8] for i in range(0, 32, 8)], axis=1)
-    near = spread(jnp.concatenate([w_query, w_out.T, folded], axis=0), "z", nz)
-
-    others = [lax.ppermute(tokens, "tp", [(i, (i + k) % nx) for i in range(nx)]) for k in range(1, nx)]
-
-    kv_near = jnp.concatenate(
-        [near[:, 2 * rows :, i * share : (i + 1) * share] for i in range(slab // 8)], axis=1
-    )
+    near = spread(folded, "z", nz)
+    kv_near = jnp.concatenate([near[:, :, i * share : (i + 1) * share] for i in range(slab // 8)], axis=1)
     kv_mine = spread(kv_near, ("x", "yh"), nx * ny)
     kv_twin = lax.ppermute(kv_mine, "c", both)
-    part = nz * rows
+
+    others = [lax.ppermute(tokens, "tp", [(i, (i + k) % nx) for i in range(nx)]) for k in range(1, nx)]
+
+    qo_own = jnp.concatenate([w_query, w_out.T], axis=0)
+    qo_other = lax.ppermute(qo_own, "yh", both)
+    low = jnp.where(iy == 0, qo_own, qo_other)
+    high = jnp.where(iy == 0, qo_other, qo_own)
+    qo_pair = jnp.concatenate([low[:rows], high[:rows], low[rows:], high[rows:]], axis=0)
+    qo_near = spread(after(qo_pair, kv_mine), "z", nz)
+    part = nz * ny * rows
     qo_send = jnp.concatenate(
-        [near[:, :rows].reshape(part, cols), near[:, rows : 2 * rows].reshape(part, cols)], axis=0
+        [qo_near[:, : ny * rows].reshape(part, cols), qo_near[:, ny * rows :].reshape(part, cols)], axis=0
     )
-    qo_all = lax.all_gather(qo_send, ("x", "yh", "c"), axis=0, tiled=False)
+    qo_all = lax.all_gather(qo_send, ("x", "c"), axis=0, tiled=False)
 
     normed = rms_norm(jnp.concatenate(in_order([tokens, *others], it), axis=1), norm_gain)
-    padded = turned(normed, natural_to_gathered(shard, rows, slab, ny, True))
+    padded = turned(normed, natural_to_gathered(shard, rows, slab, ny, False))
     half = ny * nz * slab
     of_core = [
         jnp.concatenate([padded[:, i * half : (i + 1) * half] for i in range(c, nx * nc, nc)], axis=1)
@@ -204,6 +208,7 @@
     before = lax.ppermute(kv_share, SEQ, [(i, i + block) for i in range(devices - block)])
     chips = jnp.arange(nz, dtype=jnp.int32)
     to_send = jnp.where((chips > iz)[:, None, None], kv_share[None], before[None])
+    to_send = after(to_send, qo_send)
     to_send = jnp.broadcast_to(to_send[:, None], (nz, nx, tok, share)).reshape(nz * nx, tok, share)
     mine = lax.all_to_all(to_send, ("z", "tp"), 0, 0, tiled=True).reshape(nz, nx, tok, share)
     rest = [lax.ppermute(kv_share, "tp", [(i, (i + k) % nx) for i in range(nx)]) for k in range(1, nx)]
@@ -211,7 +216,7 @@
     kv_cache = jnp.concatenate(list(own_kv), axis=1)
     at_self = (chips == iz)[:, None, None, None] & (ic == 0)
     partner = lax.ppermute(jnp.where(at_self, own_kv[None], mine), "c", both)
-    perm = natural_to_gathered(shard, rows, rows, ny, False)
+    perm = natural_to_gathered(shard, rows, rows, ny, True)
     reordered = turned(after(normed, to_send), perm)
     block_of_mine = my_block - (chips >= iz).astype(jnp.int32)
     block_of_partner = my_block - jnp.where(ic == 1, chips > iz, chips >= iz).astype(jnp.int32)
@@ -222,7 +227,7 @@
 
     vmem = pl.BlockSpec(memory_space=pltpu.VMEM)
     hbm = pl.BlockSpec(memory_space=pl.ANY)
-    scratch = [pltpu.VMEM((nx * shard, cols), bf), pltpu.SemaphoreType.DMA((nx * ny * nc,))]
+    scratch = [pltpu.VMEM((nx * shard, cols), bf), pltpu.SemaphoreType.DMA((nx * nc,))]
     queries = pl.pallas_call(
         queries_kernel,
         out_shape=jax.ShapeDtypeStruct((tok, cols), bf),

time: 196 us -> 195 us (level)
  the two profiles are of different devices: /device:TPU:2 before, /device:TPU:56 now
where the time goes in v7:
time: 195 us; the launch traced here: 194 us
  starting transfers between devices  72.1 us (37%)
  waiting for transfers between devices  69.7 us (36%)
  between operations  14.7 us (8%)
  matrix products  11.5 us (6%)
  other arithmetic  10.2 us (5%)
  Pallas kernels  9.96 us (5%)
  local copies, waits for them, and re-layouts  5.63 us (3%)
    all_to_all x3, starting transfers between devices, spread(): return lax.all_to_all(copies, axes, 0, 0, tiled=True)  26.7 us
    all_to_all x1, waiting for transfers between devices, per_device(): lax.all_to_all(to_send, ('z', 'tp'), 0, 0, tiled=True)  22.9 us
    all_to_all x3, waiting for transfers between devices, spread(): return lax.all_to_all(copies, axes, 0, 0, tiled=True)  22.2 us
    all_to_all x1, waiting for transfers between devices, per_device(): received = lax.all_to_all(partial, 'tp', 0, 0, tiled=True)  14.9 us
    ppermute x3, starting transfers between devices, per_device(): lax.ppermute(kv_share, 'tp', [(i, (i + k) % nx) for i in range(nx)])  10.2 us
    ppermute x3, starting transfers between devices, per_device(): lax.ppermute(tokens, 'tp', [(i, (i + k) % nx) for i in range(nx)])  10 us
    dot_general x8, matrix products, turned(): jnp.dot(values[:, g:g + per], hot, preferred_element_type=jnp.float32)  8.36 us
    ppermute x1, starting transfers between devices, per_device(): lax.ppermute(kv_share, SEQ, [(i, i + block) for i in range(devices - bloc...  7.48 us
  transfers between devices with their start and end apart: 16, of which 7 were waited for; matrix products, arithmetic and copies ran while one was open for 11% of the time, Pallas kernels for 2%

profile of v7, /device:TPU:56, one launch (start us, length us, event | category | flops | bytes accessed | tf_op | source)
XLA Modules:
  0.0 193.8 jit_solution(16623628248392717549)
XLA Ops:
  7.2 4.2 %collective-permute-start = (bf16[128,640]{1,0:T(8,128)(2,1)}, bf16[128,640]{1,0:T(8,128)(2,1)S(1)}, u32[]{:S(2)}, u32[]{:S(2)}) collective-permute-start(bf16[128,640]{1,0:T(8,128)(2,1)} %param.6), channel_id=1, source_target_pairs={{0,2},{1,3},{2,0},{3,1},{4,6},{5,7},{6,4},{7,5},{8,10},{9,11},{10,... | collective-permute-start | bytes 491528 | tf_op jit(solution)/shard_map/ppermute | solution.py:167
  11.4 3.5 %collective-permute-start.1 = (bf16[128,640]{1,0:T(8,128)(2,1)}, bf16[128,640]{1,0:T(8,128)(2,1)S(1)}, u32[]{:S(2)}, u32[]{:S(2)}) collective-permute-start(bf16[128,640]{1,0:T(8,128)(2,1)} %param.6), channel_id=1, source_target_pairs={{0,1},{1,2},{2,3},{3,0},{4,5},{5,6},{6,7},{7,4},{8,9},{9,10},{10,1... | collective-permute-start | bytes 491528 | tf_op jit(solution)/shard_map/ppermute | solution.py:167
  14.8 2.4 %collective-permute-start.2 = (bf16[128,640]{1,0:T(8,128)(2,1)}, bf16[128,640]{1,0:T(8,128)(2,1)S(1)}, u32[]{:S(2)}, u32[]{:S(2)}) collective-permute-start(bf16[128,640]{1,0:T(8,128)(2,1)} %param.6), channel_id=1, source_target_pairs={{0,3},{1,0},{2,1},{3,2},{4,7},{5,4},{6,5},{7,6},{8,11},{9,8},{10,9... | collective-permute-start | bytes 491528 | tf_op jit(solution)/shard_map/ppermute | solution.py:167
  17.2 0.7 convert_bitcast_fusion
  17.9 0.7 select_select_fusion.10
  18.7 0.6 broadcast_in_dim.58
  19.3 10.3 %all-to-all-start = ((bf16[8,8,512]{2,1,0:T(8,128)(2,1)}), bf16[8,8,512]{2,1,0:T(8,128)(2,1)S(1)}, u32[]{:S(2)}, u32[]{:S(2)}) async-start(bf16[8,8,512]{2,1,0:T(8,128)(2,1)} %broadcast_in_dim.58), calls=%async_computation | async-start | bytes 131072 | tf_op jit(solution)/shard_map/all_to_all | solution.py:36
  29.6 0.8 pad_maximum_fusion.11
  30.4 3.4 %collective-permute-start.5 = (bf16[40,512]{1,0:T(8,128)(2,1)S(1)}, bf16[40,512]{1,0:T(8,128)(2,1)S(1)}, u32[]{:S(2)}, u32[]{:S(2)}) collective-permute-start(bf16[40,512]{1,0:T(8,128)(2,1)S(1)} %pad_maximum_fusion.11), channel_id=1, source_target_pairs={{0,64},{64,0},{1,65},{65,1},{2,66},{66,2},{3,67},{67,3},{4,68},{68... | collective-permute-start | bytes 122888 | tf_op jit(solution)/shard_map/ppermute | solution.py:170
  34.0 0.6 iota_add_fusion.token_ref
  34.8 0.7 convert_element_type.77
  35.5 0.6 copy.36
  36.1 4.1 %collective-permute-done.5 = bf16[40,512]{1,0:T(8,128)(2,1)S(1)} collective-permute-done((bf16[40,512]{1,0:T(8,128)(2,1)S(1)}, bf16[40,512]{1,0:T(8,128)(2,1)S(1)}, u32[]{:S(2)}, u32[]{:S(2)}) %collective-permute-start.5) | collective-permute-done | bytes 40992 | tf_op jit(solution)/shard_map/ppermute | solution.py:170
  40.2 0.8 broadcast_select_fusion.5
  41.0 0.8 broadcast_in_dim.59
  41.8 9.7 %all-to-all-start.1 = ((bf16[8,8,24,128]{3,2,1,0:T(8,128)(2,1)}), bf16[8,8,24,128]{3,2,1,0:T(8,128)(2,1)S(1)}, u32[]{:S(2)}, u32[]{:S(2)}) async-start(bf16[8,8,24,128]{3,2,1,0:T(8,128)(2,1)} %broadcast_in_dim.59), calls=%async_computation.1 | async-start | bytes 786432 | tf_op jit(solution)/shard_map/all_to_all | solution.py:36
  51.6 0.1 select_select_fusion.5
  51.7 0.2 fusion.30
  51.9 7.4 %all-to-all-done.1 = bf16[8,8,24,128]{3,2,1,0:T(8,128)(2,1)S(1)} async-done(((bf16[8,8,24,128]{3,2,1,0:T(8,128)(2,1)}), bf16[8,8,24,128]{3,2,1,0:T(8,128)(2,1)S(1)}, u32[]{:S(2)}, u32[]{:S(2)}) %all-to-all-start.1) | async-done | bytes 393248 | tf_op jit(solution)/shard_map/all_to_all | solution.py:36
  59.4 0.9 broadcast_in_dim.70
  60.3 6.7 %all-to-all-start.2 = ((bf16[8,80,512]{2,1,0:T(8,128)(2,1)}), bf16[8,80,512]{2,1,0:T(8,128)(2,1)S(1)}, u32[]{:S(2)}, u32[]{:S(2)}) async-start(bf16[8,80,512]{2,1,0:T(8,128)(2,1)} %broadcast_in_dim.70), calls=%async_computation.2 | async-start | bytes 1310720 | tf_op jit(solution)/shard_map/all_to_all | solution.py:36
  67.0 0.2 fusion.32
  67.2 0.8 convolution_convert_fusion
  68.0 14.7 %all-to-all-done.2 = bf16[8,80,512]{2,1,0:T(8,128)(2,1)S(1)} async-done(((bf16[8,80,512]{2,1,0:T(8,128)(2,1)}), bf16[8,80,512]{2,1,0:T(8,128)(2,1)S(1)}, u32[]{:S(2)}, u32[]{:S(2)}) %all-to-all-start.2) | async-done | bytes 655392 | tf_op jit(solution)/shard_map/all_to_all | solution.py:36
  82.8 0.9 pad_maximum_fusion.1
  83.8 0.8 convolution_convert_fusion.1
  84.6 0.8 convolution_convert_fusion.2
  85.5 0.8 convolution_convert_fusion.3
  86.4 1.9 collective-permute-start.3
  88.3 0.1 broadcast_select_fusion.1
  88.5 0.3 fusion.92
  88.8 1.2 collective-permute-done.3
  90.1 0.3 convert_reduce_fusion
  90.4 0.1 select_reduce_fusion
  90.5 0.3 convolution_add_fusion.3
  90.8 0.3 fusion.48
  91.1 0.8 fusion.46
  91.9 7.5 %collective-permute-start.4 = (bf16[128,128]{1,0:T(8,128)(2,1)S(1)}, bf16[128,128]{1,0:T(8,128)(2,1)S(1)}, u32[]{:S(2)}, u32[]{:S(2)}) collective-permute-start(bf16[128,128]{1,0:T(8,128)(2,1)S(1)} %get-tuple-element.14), channel_id=1, source_target_pairs={{0,64},{4,68},{8,72},{12,76},{16,80},{20,84},{24,88},{28,92},{32,9... | collective-permute-start | bytes 98312 | tf_op jit(solution)/shard_map/ppermute | solution.py:208
  99.4 4.0 %collective-permute-start.6 = (bf16[128,128]{1,0:T(8,128)(2,1)S(1)}, bf16[128,128]{1,0:T(8,128)(2,1)S(1)}, u32[]{:S(2)}, u32[]{:S(2)}) collective-permute-start(bf16[128,128]{1,0:T(8,128)(2,1)S(1)} %get-tuple-element.14), channel_id=1, source_target_pairs={{0,2},{1,3},{2,0},{3,1},{4,6},{5,7},{6,4},{7,5},{8,10},{9,11},{10,... | collective-permute-start | bytes 98312 | tf_op jit(solution)/shard_map/ppermute | solution.py:214
  103.4 3.8 %collective-permute-start.7 = (bf16[128,128]{1,0:T(8,128)(2,1)S(1)}, bf16[128,128]{1,0:T(8,128)(2,1)S(1)}, u32[]{:S(2)}, u32[]{:S(2)}) collective-permute-start(bf16[128,128]{1,0:T(8,128)(2,1)S(1)} %get-tuple-element.14), channel_id=1, source_target_pairs={{0,1},{1,2},{2,3},{3,0},{4,5},{5,6},{6,7},{7,4},{8,9},{9,10},{10,1... | collective-permute-start | bytes 98312 | tf_op jit(solution)/shard_map/ppermute | solution.py:214
  107.2 2.5 %collective-permute-start.8 = (bf16[128,128]{1,0:T(8,128)(2,1)S(1)}, bf16[128,128]{1,0:T(8,128)(2,1)S(1)}, u32[]{:S(2)}, u32[]{:S(2)}) collective-permute-start(bf16[128,128]{1,0:T(8,128)(2,1)S(1)} %get-tuple-element.14), channel_id=1, source_target_pairs={{0,3},{1,0},{2,1},{3,2},{4,7},{5,4},{6,5},{7,6},{8,11},{9,8},{10,9... | collective-permute-start | bytes 98312 | tf_op jit(solution)/shard_map/ppermute | solution.py:214
  109.7 0.1 copy.24
  109.8 0.6 add_maximum_fusion.first_ref
  110.4 4.4 %collective-permute-done.8 = bf16[128,128]{1,0:T(8,128)(2,1)S(1)} collective-permute-done((bf16[128,128]{1,0:T(8,128)(2,1)S(1)}, bf16[128,128]{1,0:T(8,128)(2,1)S(1)}, u32[]{:S(2)}, u32[]{:S(2)}) %collective-permute-start.8) | collective-permute-done | bytes 32800 | tf_op jit(solution)/shard_map/ppermute | solution.py:214
  115.0 1.2 broadcast_in_dim.71
  116.2 5.3 %all-to-all-start.3 = ((bf16[32,128,128]{2,1,0:T(8,128)(2,1)}), bf16[32,128,128]{2,1,0:T(8,128)(2,1)S(1)}, u32[]{:S(2)}, u32[]{:S(2)}) async-start(bf16[32,128,128]{2,1,0:T(8,128)(2,1)} %bitcast.7), calls=%async_computation.3 | async-start | bytes 2097152 | tf_op jit(solution)/shard_map/all_to_all | solution.py:213
  121.5 1.2 convolution_convert_fusion.4
  122.7 1.2 convolution_convert_fusion.5
  123.9 1.2 convolution_convert_fusion.6
  125.1 22.9 %all-to-all-done.3 = bf16[32,128,128]{2,1,0:T(8,128)(2,1)S(1)} async-done(((bf16[32,128,128]{2,1,0:T(8,128)(2,1)}), bf16[32,128,128]{2,1,0:T(8,128)(2,1)S(1)}, u32[]{:S(2)}, u32[]{:S(2)}) %all-to-all-start.3) | async-done | bytes 1048608 | tf_op jit(solution)/shard_map/all_to_all | solution.py:213
  148.0 0.1 broadcast_select_fusion
  148.2 2.1 %collective-permute-start.9 = (bf16[8,4,128,128]{3,2,1,0:T(8,128)(2,1)S(1)}, bf16[8,4,128,128]{3,2,1,0:T(8,128)(2,1)S(1)}, u32[]{:S(2)}, u32[]{:S(2)}) collective-permute-start(bf16[8,4,128,128]{3,2,1,0:T(8,128)(2,1)S(1)} %broadcast_select_fusion), channel_id=1, source_target_pairs={{0,4},{4,0},{1,5},{5,1},{2,6},{6,2},{3,7},{7,3},{8,12},{12,8},{9,1... | collective-permute-start | bytes 3145736 | tf_op jit(solution)/shard_map/ppermute | solution.py:218
  150.2 1.4 convolution_convert_fusion.7
  151.7 0.9 pad_maximum_fusion.2.normed_ref
  152.6 4.1 %queries.1.queries_ref = bf16[128,512]{1,0:T(8,128)(2,1)} custom-call(bf16[128,2560]{1,0:T(8,128)(2,1)} %pad_maximum_fusion.2.normed_ref, f32[128,128]{1,0:T(8,128)} %get-tuple-element.38.cosine_ref, f32[128,128]{1,0:T(8,128)} %get-tuple-element.15.sine_ref, bf16[8,640,512]{2,1,0:T(8,128)(2,1)} %bitcast.49), custom_call_target="tpu_custom_call" | custom-call | tf_op jit(solution)/shard_map/queries/pallas_call | solution.py:231
  156.8 1.0 copy-done.2
  157.7 5.9 %attend.1 = bf16[4,128,640]{2,1,0:T(8,128)(2,1)} custom-call(bf16[128,512]{1,0:T(8,128)(2,1)} %queries.1.queries_ref, bf16[8,4,128,128]{3,2,1,0:T(8,128)(2,1)} %bitcast.52, bf16[8,4,128,128]{3,2,1,0:T(8,128)(2,1)} %copy-done.2, bf16[4,128,128]{2,1,0:T(8,128)(2,1)} %copy-done.1, s32[1,2176]{1,0:T(1,128)} %bitcast.65, s32[128,1]{1,0:T(8,128)} %iota_add_fusion.token_ref, ...), custom_call_target="tpu_custom_call" | custom-call | tf_op jit(solution)/shard_map/attend/pallas_call | solution.py:240
  163.6 5.1 %all-to-all-start.4 = ((bf16[4,128,640]{2,1,0:T(8,128)(2,1)}), bf16[4,128,640]{2,1,0:T(8,128)(2,1)S(1)}, u32[]{:S(2)}, u32[]{:S(2)}) async-start(bf16[4,128,640]{2,1,0:T(8,128)(2,1)} %attend.1), calls=%async_computation.4 | async-start | bytes 1310720 | tf_op jit(solution)/shard_map/all_to_all | solution.py:249
  168.7 0.7 pad_maximum_fusion.6
  169.4 14.9 %all-to-all-done.4 = bf16[4,128,640]{2,1,0:T(8,128)(2,1)S(1)} async-done(((bf16[4,128,640]{2,1,0:T(8,128)(2,1)}), bf16[4,128,640]{2,1,0:T(8,128)(2,1)S(1)}, u32[]{:S(2)}, u32[]{:S(2)}) %all-to-all-start.4) | async-done | bytes 655392 | tf_op jit(solution)/shard_map/all_to_all | solution.py:249
  184.3 0.5 fusion.35
  184.8 0.5 convolution_add_fusion.2
  185.3 0.5 convolution_add_fusion.1
  185.8 1.2 fusion.34
  (65 shorter events, 0.9 us)
Async XLA Ops:
  7.2 44.4 %copy-start.4 = (bf16[128,640]{1,0:T(8,128)(2,1)S(1)}, bf16[128,640]{1,0:T(8,128)(2,1)}, u32[]{:S(2)}) copy-start(bf16[128,640]{1,0:T(8,128)(2,1)} %param.6) | copy-start | bytes 491524
  7.2 44.4 %collective-permute-start = (bf16[128,640]{1,0:T(8,128)(2,1)}, bf16[128,640]{1,0:T(8,128)(2,1)S(1)}, u32[]{:S(2)}, u32[]{:S(2)}) collective-permute-start(bf16[128,640]{1,0:T(8,128)(2,1)} %param.6), channel_id=1, source_target_pairs={{0,2},{1,3},{2,0},{3,1},{4,6},{5,7},{6,4},{7,5},{8,10},{9,11},{10,... | collective-permute-start | bytes 491528 | tf_op jit(solution)/shard_map/ppermute | solution.py:167
  11.4 40.2 %collective-permute-start.1 = (bf16[128,640]{1,0:T(8,128)(2,1)}, bf16[128,640]{1,0:T(8,128)(2,1)S(1)}, u32[]{:S(2)}, u32[]{:S(2)}) collective-permute-start(bf16[128,640]{1,0:T(8,128)(2,1)} %param.6), channel_id=1, source_target_pairs={{0,1},{1,2},{2,3},{3,0},{4,5},{5,6},{6,7},{7,4},{8,9},{9,10},{10,1... | collective-permute-start | bytes 491528 | tf_op jit(solution)/shard_map/ppermute | solution.py:167
  14.8 36.7 %collective-permute-start.2 = (bf16[128,640]{1,0:T(8,128)(2,1)}, bf16[128,640]{1,0:T(8,128)(2,1)S(1)}, u32[]{:S(2)}, u32[]{:S(2)}) collective-permute-start(bf16[128,640]{1,0:T(8,128)(2,1)} %param.6), channel_id=1, source_target_pairs={{0,3},{1,0},{2,1},{3,2},{4,7},{5,4},{6,5},{7,6},{8,11},{9,8},{10,9... | collective-permute-start | bytes 491528 | tf_op jit(solution)/shard_map/ppermute | solution.py:167
  19.3 21.7 %all-to-all-start = ((bf16[8,8,512]{2,1,0:T(8,128)(2,1)}), bf16[8,8,512]{2,1,0:T(8,128)(2,1)S(1)}, u32[]{:S(2)}, u32[]{:S(2)}) async-start(bf16[8,8,512]{2,1,0:T(8,128)(2,1)} %broadcast_in_dim.58), calls=%async_computation | async-start | bytes 131072 | tf_op jit(solution)/shard_map/all_to_all | solution.py:36
  30.4 9.8 %collective-permute-start.5 = (bf16[40,512]{1,0:T(8,128)(2,1)S(1)}, bf16[40,512]{1,0:T(8,128)(2,1)S(1)}, u32[]{:S(2)}, u32[]{:S(2)}) collective-permute-start(bf16[40,512]{1,0:T(8,128)(2,1)S(1)} %pad_maximum_fusion.11), channel_id=1, source_target_pairs={{0,64},{64,0},{1,65},{65,1},{2,66},{66,2},{3,67},{67,3},{4,68},{68... | collective-permute-start | bytes 122888 | tf_op jit(solution)/shard_map/ppermute | solution.py:170
  41.8 17.5 %all-to-all-start.1 = ((bf16[8,8,24,128]{3,2,1,0:T(8,128)(2,1)}), bf16[8,8,24,128]{3,2,1,0:T(8,128)(2,1)S(1)}, u32[]{:S(2)}, u32[]{:S(2)}) async-start(bf16[8,8,24,128]{3,2,1,0:T(8,128)(2,1)} %broadcast_in_dim.59), calls=%async_computation.1 | async-start | bytes 786432 | tf_op jit(solution)/shard_map/all_to_all | solution.py:36
  60.3 22.5 %all-to-all-start.2 = ((bf16[8,80,512]{2,1,0:T(8,128)(2,1)}), bf16[8,80,512]{2,1,0:T(8,128)(2,1)S(1)}, u32[]{:S(2)}, u32[]{:S(2)}) async-start(bf16[8,80,512]{2,1,0:T(8,128)(2,1)} %broadcast_in_dim.70), calls=%async_computation.2 | async-start | bytes 1310720 | tf_op jit(solution)/shard_map/all_to_all | solution.py:36
  66.9 85.7 %all-gather.3.cloned.1.call-start = ((), (), s32[]{:S(2)}) async-start(), calls=%async_computation.5 | async-start | bytes 5898240 | tf_op jit(solution)/shard_map/all_gather | solution.py:179
  67.2 56.7 %copy-start.3 = (bf16[128,2560]{1,0:T(8,128)(2,1)}, bf16[128,2560]{1,0:T(8,128)(2,1)S(1)}, u32[]{:S(2)}) copy-start(bf16[128,2560]{1,0:T(8,128)(2,1)S(1)} %fusion.32) | copy-start | bytes 1966084
  86.3 4.0 %copy-start.8 = (s32[128]{0:T(128)S(1)}, s32[128]{0:T(128)}, u32[]{:S(2)}) copy-start(s32[128]{0:T(128)} %param.7) | copy-start | bytes 1540
  86.4 3.6 %collective-permute-start.3 = (bf16[8,8,24,128]{3,2,1,0:T(8,128)(2,1)S(1)}, bf16[8,8,24,128]{3,2,1,0:T(8,128)(2,1)S(1)}, u32[]{:S(2)}, u32[]{:S(2)}) collective-permute-start(bf16[8,8,24,128]{3,2,1,0:T(8,128)(2,1)S(1)} %all-to-all-done.1), channel_id=1, source_target_pairs={{0,4},{4,0},{1,5},{5,1},{2,6},{6,2},{3,7},{7,3},{8,12},{12,8},{9,1... | collective-permute-start | bytes 1179656 | tf_op jit(solution)/shard_map/ppermute | solution.py:165
  91.9 22.9 %collective-permute-start.4 = (bf16[128,128]{1,0:T(8,128)(2,1)S(1)}, bf16[128,128]{1,0:T(8,128)(2,1)S(1)}, u32[]{:S(2)}, u32[]{:S(2)}) collective-permute-start(bf16[128,128]{1,0:T(8,128)(2,1)S(1)} %get-tuple-element.14), channel_id=1, source_target_pairs={{0,64},{4,68},{8,72},{12,76},{16,80},{20,84},{24,88},{28,92},{32,9... | collective-permute-start | bytes 98312 | tf_op jit(solution)/shard_map/ppermute | solution.py:208
  99.4 11.0 %collective-permute-start.6 = (bf16[128,128]{1,0:T(8,128)(2,1)S(1)}, bf16[128,128]{1,0:T(8,128)(2,1)S(1)}, u32[]{:S(2)}, u32[]{:S(2)}) collective-permute-start(bf16[128,128]{1,0:T(8,128)(2,1)S(1)} %get-tuple-element.14), channel_id=1, source_target_pairs={{0,2},{1,3},{2,0},{3,1},{4,6},{5,7},{6,4},{7,5},{8,10},{9,11},{10,... | collective-permute-start | bytes 98312 | tf_op jit(solution)/shard_map/ppermute | solution.py:214
  103.4 7.0 %collective-permute-start.7 = (bf16[128,128]{1,0:T(8,128)(2,1)S(1)}, bf16[128,128]{1,0:T(8,128)(2,1)S(1)}, u32[]{:S(2)}, u32[]{:S(2)}) collective-permute-start(bf16[128,128]{1,0:T(8,128)(2,1)S(1)} %get-tuple-element.14), channel_id=1, source_target_pairs={{0,1},{1,2},{2,3},{3,0},{4,5},{5,6},{6,7},{7,4},{8,9},{9,10},{10,1... | collective-permute-start | bytes 98312 | tf_op jit(solution)/shard_map/ppermute | solution.py:214
  107.2 7.6 %collective-permute-start.8 = (bf16[128,128]{1,0:T(8,128)(2,1)S(1)}, bf16[128,128]{1,0:T(8,128)(2,1)S(1)}, u32[]{:S(2)}, u32[]{:S(2)}) collective-permute-start(bf16[128,128]{1,0:T(8,128)(2,1)S(1)} %get-tuple-element.14), channel_id=1, source_target_pairs={{0,3},{1,0},{2,1},{3,2},{4,7},{5,4},{6,5},{7,6},{8,11},{9,8},{10,9... | collective-permute-start | bytes 98312 | tf_op jit(solution)/shard_map/ppermute | solution.py:214
  114.9 33.2 %copy-start.1 = (bf16[4,128,128]{2,1,0:T(8,128)(2,1)}, bf16[4,128,128]{2,1,0:T(8,128)(2,1)S(1)}, u32[]{:S(2)}) copy-start(bf16[4,128,128]{2,1,0:T(8,128)(2,1)S(1)} %pad_maximum_fusion.5.own_ref) | copy-start | bytes 393220
  116.2 31.8 %all-to-all-start.3 = ((bf16[32,128,128]{2,1,0:T(8,128)(2,1)}), bf16[32,128,128]{2,1,0:T(8,128)(2,1)S(1)}, u32[]{:S(2)}, u32[]{:S(2)}) async-start(bf16[32,128,128]{2,1,0:T(8,128)(2,1)} %bitcast.7), calls=%async_computation.3 | async-start | bytes 2097152 | tf_op jit(solution)/shard_map/all_to_all | solution.py:213
  148.0 3.7 %copy-start = (bf16[32,128,128]{2,1,0:T(8,128)(2,1)}, bf16[32,128,128]{2,1,0:T(8,128)(2,1)S(1)}, u32[]{:S(2)}) copy-start(bf16[32,128,128]{2,1,0:T(8,128)(2,1)S(1)} %all-to-all-done.3) | copy-start | bytes 3145732
  148.2 3.5 %copy-start.5 = (bf16[128,640]{1,0:T(8,128)(2,1)S(1)}, bf16[128,640]{1,0:T(8,128)(2,1)}, u32[]{:S(2)}) copy-start(bf16[128,640]{1,0:T(8,128)(2,1)} %convolution_convert_fusion.4) | copy-start | bytes 491524
  148.2 3.5 %copy-start.6 = (bf16[128,640]{1,0:T(8,128)(2,1)S(1)}, bf16[128,640]{1,0:T(8,128)(2,1)}, u32[]{:S(2)}) copy-start(bf16[128,640]{1,0:T(8,128)(2,1)} %convolution_convert_fusion.5) | copy-start | bytes 491524
  148.2 3.5 %copy-start.7 = (bf16[128,640]{1,0:T(8,128)(2,1)S(1)}, bf16[128,640]{1,0:T(8,128)(2,1)}, u32[]{:S(2)}) copy-start(bf16[128,640]{1,0:T(8,128)(2,1)} %convolution_convert_fusion.6) | copy-start | bytes 491524
  148.2 8.6 %collective-permute-start.9 = (bf16[8,4,128,128]{3,2,1,0:T(8,128)(2,1)S(1)}, bf16[8,4,128,128]{3,2,1,0:T(8,128)(2,1)S(1)}, u32[]{:S(2)}, u32[]{:S(2)}) collective-permute-start(bf16[8,4,128,128]{3,2,1,0:T(8,128)(2,1)S(1)} %broadcast_select_fusion), channel_id=1, source_target_pairs={{0,4},{4,0},{1,5},{5,1},{2,6},{6,2},{3,7},{7,3},{8,12},{12,8},{9,1... | collective-permute-start | bytes 3145736 | tf_op jit(solution)/shard_map/ppermute | solution.py:218
  156.8 1.0 copy-start.2
  163.6 20.7 %all-to-all-start.4 = ((bf16[4,128,640]{2,1,0:T(8,128)(2,1)}), bf16[4,128,640]{2,1,0:T(8,128)(2,1)S(1)}, u32[]{:S(2)}, u32[]{:S(2)}) async-start(bf16[4,128,640]{2,1,0:T(8,128)(2,1)} %attend.1), calls=%async_computation.4 | async-start | bytes 1310720 | tf_op jit(solution)/shard_map/all_to_all | solution.py:249
Sparse Core Ops, SparseCore 0:
  83.9 37.0 all-gather.2

commit v8 on v5

--- a/solution.py
+++ b/solution.py
@@ -153,7 +153,10 @@
     share = 2 * HD // nx
     slab = rows + 4
     ids = jnp.pad(seg_ids.astype(bf)[None, :], ((0, 31 - rows), (0, 0)))
-    kv_slab = jnp.concatenate([lax.dynamic_slice_in_dim(w_keyval, it * share, share, 1), ids], axis=0)
+    chosen = w_keyval[:, (nx - 1) * share :]
+    for t in range(nx - 1):
+        chosen = jnp.where(it == t, w_keyval[:, t * share : (t + 1) * share], chosen)
+    kv_slab = jnp.concatenate([chosen, ids], axis=0)
     folded = jnp.concatenate([kv_slab[i : i + 8] for i in range(0, 32, 8)], axis=1)
     near = spread(jnp.concatenate([w_query, w_out.T, folded], axis=0), ("yh", "z"), ny * nz)
 

time: 183 us -> 183 us (level)
  transfers between devices with their start and end apart: 13 -> 13, of which waited for: 6 -> 6; matrix products, arithmetic and copies ran while one was open for 11% -> 10% of each run, Pallas kernels for 2% -> 2%
where the time goes in v8:
time: 183 us; the launch traced here: 182 us
  waiting for transfers between devices  78.4 us (43%)
  starting transfers between devices  55.1 us (30%)
  between operations  14.6 us (8%)
  Pallas kernels  9.97 us (5%)
  matrix products  9.43 us (5%)
  other arithmetic  8.74 us (5%)
  local copies, waits for them, and re-layouts  5.77 us (3%)
    all_to_all x2, waiting for transfers between devices, spread(): return lax.all_to_all(copies, axes, 0, 0, tiled=True)  40.5 us
    all_to_all x2, starting transfers between devices, spread(): return lax.all_to_all(copies, axes, 0, 0, tiled=True)  18.7 us
    all_to_all x1, waiting for transfers between devices, per_device(): received = lax.all_to_all(partial, 'tp', 0, 0, tiled=True)  17.5 us
    ppermute x3, starting transfers between devices, per_device(): lax.ppermute(tokens, 'tp', [(i, (i + k) % nx) for i in range(nx)])  12.3 us
    ppermute x3, starting transfers between devices, per_device(): lax.ppermute(kv_share, 'tp', [(i, (i + k) % nx) for i in range(nx)])  12.2 us
    ppermute x3, waiting for transfers between devices, per_device(): lax.ppermute(kv_share, 'tp', [(i, (i + k) % nx) for i in range(nx)])  11.9 us
    ppermute x1, waiting for transfers between devices, per_device(): lax.ppermute(kv_share, SEQ, [(i, i + block) for i in range(devices - bloc...  8.16 us
    dot_general x8, matrix products, turned(): jnp.dot(values[:, g:g + per], hot, preferred_element_type=jnp.float32)  6.54 us
  transfers between devices with their start and end apart: 13, of which 6 were waited for; matrix products, arithmetic and copies ran while one was open for 10% of the time, Pallas kernels for 2%

profile of v8, /device:TPU:2, one launch (start us, length us, event | category | flops | bytes accessed | tf_op | source)
XLA Modules:
  0.0 182.0 jit_solution(8151916365044457201)
XLA Ops:
  7.2 4.6 %collective-permute-start = (bf16[128,640]{1,0:T(8,128)(2,1)}, bf16[128,640]{1,0:T(8,128)(2,1)S(1)}, u32[]{:S(2)}, u32[]{:S(2)}) collective-permute-start(bf16[128,640]{1,0:T(8,128)(2,1)} %param.6), channel_id=1, source_target_pairs={{0,2},{1,3},{2,0},{3,1},{4,6},{5,7},{6,4},{7,5},{8,10},{9,11},{10,... | collective-permute-start | bytes 491528 | tf_op jit(solution)/shard_map/ppermute | solution.py:163
  11.8 3.5 %collective-permute-start.1 = (bf16[128,640]{1,0:T(8,128)(2,1)}, bf16[128,640]{1,0:T(8,128)(2,1)S(1)}, u32[]{:S(2)}, u32[]{:S(2)}) collective-permute-start(bf16[128,640]{1,0:T(8,128)(2,1)} %param.6), channel_id=1, source_target_pairs={{0,1},{1,2},{2,3},{3,0},{4,5},{5,6},{6,7},{7,4},{8,9},{9,10},{10,1... | collective-permute-start | bytes 491528 | tf_op jit(solution)/shard_map/ppermute | solution.py:163
  15.3 4.2 %collective-permute-start.2 = (bf16[128,640]{1,0:T(8,128)(2,1)}, bf16[128,640]{1,0:T(8,128)(2,1)S(1)}, u32[]{:S(2)}, u32[]{:S(2)}) collective-permute-start(bf16[128,640]{1,0:T(8,128)(2,1)} %param.6), channel_id=1, source_target_pairs={{0,3},{1,0},{2,1},{3,2},{4,7},{5,4},{6,5},{7,6},{8,11},{9,8},{10,9... | collective-permute-start | bytes 491528 | tf_op jit(solution)/shard_map/ppermute | solution.py:163
  19.5 0.7 convert_bitcast_fusion
  20.1 0.7 select_select_fusion.8
  20.9 0.8 maximum_maximum_fusion
  21.7 1.0 broadcast_in_dim.56
  22.7 13.9 %all-to-all-start = ((bf16[16,48,512]{2,1,0:T(8,128)(2,1)}), bf16[16,48,512]{2,1,0:T(8,128)(2,1)S(1)}, u32[]{:S(2)}, u32[]{:S(2)}) async-start(bf16[16,48,512]{2,1,0:T(8,128)(2,1)} %broadcast_in_dim.56), calls=%async_computation | async-start | bytes 1572864 | tf_op jit(solution)/shard_map/all_to_all | solution.py:36
  36.7 0.1 pad_add_fusion
  36.8 0.1 add_bitcast_fusion
  37.0 0.1 select_select_fusion.3
  37.2 0.2 fusion.28
  37.4 22.9 %all-to-all-done = bf16[16,48,512]{2,1,0:T(8,128)(2,1)S(1)} async-done(((bf16[16,48,512]{2,1,0:T(8,128)(2,1)}), bf16[16,48,512]{2,1,0:T(8,128)(2,1)S(1)}, u32[]{:S(2)}, u32[]{:S(2)}) %all-to-all-start) | async-done | bytes 786464 | tf_op jit(solution)/shard_map/all_to_all | solution.py:36
  60.3 0.1 fusion.79
  60.6 0.9 pad_maximum_fusion.3
  61.5 0.2 fusion.30
  61.8 0.8 convolution_convert_fusion
  62.6 0.8 convolution_convert_fusion.1
  63.4 0.8 convolution_convert_fusion.2
  64.2 1.0 broadcast_in_dim.57
  65.2 4.8 %all-to-all-start.1 = ((bf16[8,16,24,128]{3,2,1,0:T(8,128)(2,1)}), bf16[8,16,24,128]{3,2,1,0:T(8,128)(2,1)S(1)}, u32[]{:S(2)}, u32[]{:S(2)}) async-start(bf16[8,16,24,128]{3,2,1,0:T(8,128)(2,1)} %broadcast_in_dim.57), calls=%async_computation.1 | async-start | bytes 1572864 | tf_op jit(solution)/shard_map/all_to_all | solution.py:36
  70.1 0.8 convolution_convert_fusion.3
  70.8 0.1 pad_maximum_fusion
  70.9 17.6 %all-to-all-done.1 = bf16[8,16,24,128]{3,2,1,0:T(8,128)(2,1)S(1)} async-done(((bf16[8,16,24,128]{3,2,1,0:T(8,128)(2,1)}), bf16[8,16,24,128]{3,2,1,0:T(8,128)(2,1)S(1)}, u32[]{:S(2)}, u32[]{:S(2)}) %all-to-all-start.1) | async-done | bytes 786464 | tf_op jit(solution)/shard_map/all_to_all | solution.py:36
  88.5 0.1 slice_convert_fusion
  88.6 0.3 convert_reduce_fusion
  88.9 0.1 select_reduce_fusion
  89.0 0.4 fusion.83
  89.4 0.1 fusion.81
  89.5 0.3 fusion.45
  89.8 0.8 fusion.44
  90.6 1.9 %collective-permute-start.3 = (bf16[128,128]{1,0:T(8,128)(2,1)S(1)}, bf16[128,128]{1,0:T(8,128)(2,1)S(1)}, u32[]{:S(2)}, u32[]{:S(2)}) collective-permute-start(bf16[128,128]{1,0:T(8,128)(2,1)S(1)} %get-tuple-element.8), channel_id=1, source_target_pairs={{0,64},{4,68},{8,72},{12,76},{16,80},{20,84},{24,88},{28,92},{32,9... | collective-permute-start | bytes 98312 | tf_op jit(solution)/shard_map/ppermute | solution.py:196
  92.5 0.6 copy.33
  93.1 8.2 %collective-permute-done.3 = bf16[128,128]{1,0:T(8,128)(2,1)S(1)} collective-permute-done((bf16[128,128]{1,0:T(8,128)(2,1)S(1)}, bf16[128,128]{1,0:T(8,128)(2,1)S(1)}, u32[]{:S(2)}, u32[]{:S(2)}) %collective-permute-start.3) | collective-permute-done | bytes 32800 | tf_op jit(solution)/shard_map/ppermute | solution.py:196
  101.3 0.1 broadcast_select_fusion.1
  101.4 1.2 broadcast_in_dim.68
  102.6 4.4 %all-to-all-start.2 = ((bf16[32,128,128]{2,1,0:T(8,128)(2,1)}), bf16[32,128,128]{2,1,0:T(8,128)(2,1)S(1)}, u32[]{:S(2)}, u32[]{:S(2)}) async-start(bf16[32,128,128]{2,1,0:T(8,128)(2,1)} %bitcast.4), calls=%async_computation.2 | async-start | bytes 2097152 | tf_op jit(solution)/shard_map/all_to_all | solution.py:200
  107.1 0.6 iota_add_fusion.token_ref
  107.7 4.6 %collective-permute-start.4 = (bf16[128,128]{1,0:T(8,128)(2,1)S(1)}, bf16[128,128]{1,0:T(8,128)(2,1)S(1)}, u32[]{:S(2)}, u32[]{:S(2)}) collective-permute-start(bf16[128,128]{1,0:T(8,128)(2,1)S(1)} %get-tuple-element.8), channel_id=1, source_target_pairs={{0,2},{1,3},{2,0},{3,1},{4,6},{5,7},{6,4},{7,5},{8,10},{9,11},{10,... | collective-permute-start | bytes 98312 | tf_op jit(solution)/shard_map/ppermute | solution.py:201
  112.3 3.4 %collective-permute-start.5 = (bf16[128,128]{1,0:T(8,128)(2,1)S(1)}, bf16[128,128]{1,0:T(8,128)(2,1)S(1)}, u32[]{:S(2)}, u32[]{:S(2)}) collective-permute-start(bf16[128,128]{1,0:T(8,128)(2,1)S(1)} %get-tuple-element.8), channel_id=1, source_target_pairs={{0,1},{1,2},{2,3},{3,0},{4,5},{5,6},{6,7},{7,4},{8,9},{9,10},{10,1... | collective-permute-start | bytes 98312 | tf_op jit(solution)/shard_map/ppermute | solution.py:201
  115.7 4.3 %collective-permute-start.6 = (bf16[128,128]{1,0:T(8,128)(2,1)S(1)}, bf16[128,128]{1,0:T(8,128)(2,1)S(1)}, u32[]{:S(2)}, u32[]{:S(2)}) collective-permute-start(bf16[128,128]{1,0:T(8,128)(2,1)S(1)} %get-tuple-element.8), channel_id=1, source_target_pairs={{0,3},{1,0},{2,1},{3,2},{4,7},{5,4},{6,5},{7,6},{8,11},{9,8},{10,9... | collective-permute-start | bytes 98312 | tf_op jit(solution)/shard_map/ppermute | solution.py:201
  119.9 0.1 copy.28
  120.0 0.6 add_maximum_fusion.first_ref
  120.7 11.9 %collective-permute-done.4 = bf16[128,128]{1,0:T(8,128)(2,1)S(1)} collective-permute-done((bf16[128,128]{1,0:T(8,128)(2,1)S(1)}, bf16[128,128]{1,0:T(8,128)(2,1)S(1)}, u32[]{:S(2)}, u32[]{:S(2)}) %collective-permute-start.4) | collective-permute-done | bytes 32800 | tf_op jit(solution)/shard_map/ppermute | solution.py:201
  132.7 1.2 convolution_convert_fusion.4
  133.9 1.2 convolution_convert_fusion.5
  135.1 0.2 all-to-all-done.2
  135.3 0.1 broadcast_select_fusion
  135.4 2.1 %collective-permute-start.7 = (bf16[8,4,128,128]{3,2,1,0:T(8,128)(2,1)S(1)}, bf16[8,4,128,128]{3,2,1,0:T(8,128)(2,1)S(1)}, u32[]{:S(2)}, u32[]{:S(2)}) collective-permute-start(bf16[8,4,128,128]{3,2,1,0:T(8,128)(2,1)S(1)} %broadcast_select_fusion), channel_id=1, source_target_pairs={{0,4},{4,0},{1,5},{5,1},{2,6},{6,2},{3,7},{7,3},{8,12},{12,8},{9,1... | collective-permute-start | bytes 3145736 | tf_op jit(solution)/shard_map/ppermute | solution.py:205
  137.5 0.5 convolution_convert_fusion.6
  138.0 0.5 convolution_convert_fusion.7
  138.5 0.4 copy-done.6
  138.9 0.1 copy-done.7
  139.0 0.9 pad_maximum_fusion.2.normed_ref
  139.9 4.1 %queries.1.queries_ref = bf16[128,512]{1,0:T(8,128)(2,1)} custom-call(bf16[128,2560]{1,0:T(8,128)(2,1)} %pad_maximum_fusion.2.normed_ref, f32[128,128]{1,0:T(8,128)} %get-tuple-element.23.cosine_ref, f32[128,128]{1,0:T(8,128)} %get-tuple-element.9.sine_ref, bf16[8,640,512]{2,1,0:T(8,128)(2,1)} %bitcast.34), custom_call_target="tpu_custom_call" | custom-call | tf_op jit(solution)/shard_map/queries/pallas_call | solution.py:218
  144.0 0.9 copy-done.2
  145.0 5.9 %attend.1 = bf16[4,128,640]{2,1,0:T(8,128)(2,1)} custom-call(bf16[128,512]{1,0:T(8,128)(2,1)} %queries.1.queries_ref, bf16[8,4,128,128]{3,2,1,0:T(8,128)(2,1)} %bitcast.37, bf16[8,4,128,128]{3,2,1,0:T(8,128)(2,1)} %copy-done.2, bf16[4,128,128]{2,1,0:T(8,128)(2,1)} %copy-done.1, s32[1,2176]{1,0:T(1,128)} %bitcast.44, s32[128,1]{1,0:T(8,128)} %iota_add_fusion.token_ref, ...), custom_call_target="tpu_custom_call" | custom-call | tf_op jit(solution)/shard_map/attend/pallas_call | solution.py:227
  150.8 3.5 %all-to-all-start.3 = ((bf16[4,128,640]{2,1,0:T(8,128)(2,1)}), bf16[4,128,640]{2,1,0:T(8,128)(2,1)S(1)}, u32[]{:S(2)}, u32[]{:S(2)}) async-start(bf16[4,128,640]{2,1,0:T(8,128)(2,1)} %attend.1), calls=%async_computation.3 | async-start | bytes 1310720 | tf_op jit(solution)/shard_map/all_to_all | solution.py:236
  154.4 0.7 pad_maximum_fusion.5
  155.0 17.5 %all-to-all-done.3 = bf16[4,128,640]{2,1,0:T(8,128)(2,1)S(1)} async-done(((bf16[4,128,640]{2,1,0:T(8,128)(2,1)}), bf16[4,128,640]{2,1,0:T(8,128)(2,1)S(1)}, u32[]{:S(2)}, u32[]{:S(2)}) %all-to-all-start.3) | async-done | bytes 655392 | tf_op jit(solution)/shard_map/all_to_all | solution.py:236
  172.6 0.5 fusion.33
  173.0 0.5 convolution_add_fusion.2
  173.5 0.5 convolution_add_fusion.1
  174.0 1.1 fusion.32
  (48 shorter events, 0.5 us)
Async XLA Ops:
  7.2 29.9 %copy-start.5 = (bf16[128,640]{1,0:T(8,128)(2,1)S(1)}, bf16[128,640]{1,0:T(8,128)(2,1)}, u32[]{:S(2)}) copy-start(bf16[128,640]{1,0:T(8,128)(2,1)} %param.6) | copy-start | bytes 491524
  7.2 29.8 %copy-start.8 = (bf16[2560]{0:T(1024)(128)(2,1)S(1)}, bf16[2560]{0:T(1024)(128)(2,1)}, u32[]{:S(2)}) copy-start(bf16[2560]{0:T(1024)(128)(2,1)} %param.8) | copy-start | bytes 15364
  7.2 29.8 %collective-permute-start = (bf16[128,640]{1,0:T(8,128)(2,1)}, bf16[128,640]{1,0:T(8,128)(2,1)S(1)}, u32[]{:S(2)}, u32[]{:S(2)}) collective-permute-start(bf16[128,640]{1,0:T(8,128)(2,1)} %param.6), channel_id=1, source_target_pairs={{0,2},{1,3},{2,0},{3,1},{4,6},{5,7},{6,4},{7,5},{8,10},{9,11},{10,... | collective-permute-start | bytes 491528 | tf_op jit(solution)/shard_map/ppermute | solution.py:163
  11.8 25.2 %collective-permute-start.1 = (bf16[128,640]{1,0:T(8,128)(2,1)}, bf16[128,640]{1,0:T(8,128)(2,1)S(1)}, u32[]{:S(2)}, u32[]{:S(2)}) collective-permute-start(bf16[128,640]{1,0:T(8,128)(2,1)} %param.6), channel_id=1, source_target_pairs={{0,1},{1,2},{2,3},{3,0},{4,5},{5,6},{6,7},{7,4},{8,9},{9,10},{10,1... | collective-permute-start | bytes 491528 | tf_op jit(solution)/shard_map/ppermute | solution.py:163
  15.3 21.7 %collective-permute-start.2 = (bf16[128,640]{1,0:T(8,128)(2,1)}, bf16[128,640]{1,0:T(8,128)(2,1)S(1)}, u32[]{:S(2)}, u32[]{:S(2)}) collective-permute-start(bf16[128,640]{1,0:T(8,128)(2,1)} %param.6), channel_id=1, source_target_pairs={{0,3},{1,0},{2,1},{3,2},{4,7},{5,4},{6,5},{7,6},{8,11},{9,8},{10,9... | collective-permute-start | bytes 491528 | tf_op jit(solution)/shard_map/ppermute | solution.py:163
  22.7 37.6 %all-to-all-start = ((bf16[16,48,512]{2,1,0:T(8,128)(2,1)}), bf16[16,48,512]{2,1,0:T(8,128)(2,1)S(1)}, u32[]{:S(2)}, u32[]{:S(2)}) async-start(bf16[16,48,512]{2,1,0:T(8,128)(2,1)} %broadcast_in_dim.56), calls=%async_computation | async-start | bytes 1572864 | tf_op jit(solution)/shard_map/all_to_all | solution.py:36
  36.6 103.3 %all-gather.3.cloned.1.call-start = ((), (), s32[]{:S(2)}) async-start(), calls=%async_computation.4 | async-start | bytes 5898240 | tf_op jit(solution)/shard_map/all_gather | solution.py:173
  61.8 72.1 %copy-start.3 = (bf16[128,2560]{1,0:T(8,128)(2,1)}, bf16[128,2560]{1,0:T(8,128)(2,1)S(1)}, u32[]{:S(2)}) copy-start(bf16[128,2560]{1,0:T(8,128)(2,1)S(1)} %fusion.30) | copy-start | bytes 1966084
  65.2 23.3 %all-to-all-start.1 = ((bf16[8,16,24,128]{3,2,1,0:T(8,128)(2,1)}), bf16[8,16,24,128]{3,2,1,0:T(8,128)(2,1)S(1)}, u32[]{:S(2)}, u32[]{:S(2)}) async-start(bf16[8,16,24,128]{3,2,1,0:T(8,128)(2,1)} %broadcast_in_dim.57), calls=%async_computation.1 | async-start | bytes 1572864 | tf_op jit(solution)/shard_map/all_to_all | solution.py:36
  70.8 18.1 %copy-start.9 = (s32[128]{0:T(128)S(1)}, s32[128]{0:T(128)}, u32[]{:S(2)}) copy-start(s32[128]{0:T(128)} %param.7) | copy-start | bytes 1540
  90.6 10.7 %collective-permute-start.3 = (bf16[128,128]{1,0:T(8,128)(2,1)S(1)}, bf16[128,128]{1,0:T(8,128)(2,1)S(1)}, u32[]{:S(2)}, u32[]{:S(2)}) collective-permute-start(bf16[128,128]{1,0:T(8,128)(2,1)S(1)} %get-tuple-element.8), channel_id=1, source_target_pairs={{0,64},{4,68},{8,72},{12,76},{16,80},{20,84},{24,88},{28,92},{32,9... | collective-permute-start | bytes 98312 | tf_op jit(solution)/shard_map/ppermute | solution.py:196
  102.6 32.7 %all-to-all-start.2 = ((bf16[32,128,128]{2,1,0:T(8,128)(2,1)}), bf16[32,128,128]{2,1,0:T(8,128)(2,1)S(1)}, u32[]{:S(2)}, u32[]{:S(2)}) async-start(bf16[32,128,128]{2,1,0:T(8,128)(2,1)} %bitcast.4), calls=%async_computation.2 | async-start | bytes 2097152 | tf_op jit(solution)/shard_map/all_to_all | solution.py:200
  107.7 24.9 %collective-permute-start.4 = (bf16[128,128]{1,0:T(8,128)(2,1)S(1)}, bf16[128,128]{1,0:T(8,128)(2,1)S(1)}, u32[]{:S(2)}, u32[]{:S(2)}) collective-permute-start(bf16[128,128]{1,0:T(8,128)(2,1)S(1)} %get-tuple-element.8), channel_id=1, source_target_pairs={{0,2},{1,3},{2,0},{3,1},{4,6},{5,7},{6,4},{7,5},{8,10},{9,11},{10,... | collective-permute-start | bytes 98312 | tf_op jit(solution)/shard_map/ppermute | solution.py:201
  112.3 20.4 %collective-permute-start.5 = (bf16[128,128]{1,0:T(8,128)(2,1)S(1)}, bf16[128,128]{1,0:T(8,128)(2,1)S(1)}, u32[]{:S(2)}, u32[]{:S(2)}) collective-permute-start(bf16[128,128]{1,0:T(8,128)(2,1)S(1)} %get-tuple-element.8), channel_id=1, source_target_pairs={{0,1},{1,2},{2,3},{3,0},{4,5},{5,6},{6,7},{7,4},{8,9},{9,10},{10,1... | collective-permute-start | bytes 98312 | tf_op jit(solution)/shard_map/ppermute | solution.py:201
  115.7 17.0 %collective-permute-start.6 = (bf16[128,128]{1,0:T(8,128)(2,1)S(1)}, bf16[128,128]{1,0:T(8,128)(2,1)S(1)}, u32[]{:S(2)}, u32[]{:S(2)}) collective-permute-start(bf16[128,128]{1,0:T(8,128)(2,1)S(1)} %get-tuple-element.8), channel_id=1, source_target_pairs={{0,3},{1,0},{2,1},{3,2},{4,7},{5,4},{6,5},{7,6},{8,11},{9,8},{10,9... | collective-permute-start | bytes 98312 | tf_op jit(solution)/shard_map/ppermute | solution.py:201
  132.7 2.6 %copy-start.1 = (bf16[4,128,128]{2,1,0:T(8,128)(2,1)}, bf16[4,128,128]{2,1,0:T(8,128)(2,1)S(1)}, u32[]{:S(2)}) copy-start(bf16[4,128,128]{2,1,0:T(8,128)(2,1)S(1)} %pad_maximum_fusion.4.own_ref) | copy-start | bytes 393220
  135.3 2.7 %copy-start = (bf16[32,128,128]{2,1,0:T(8,128)(2,1)}, bf16[32,128,128]{2,1,0:T(8,128)(2,1)S(1)}, u32[]{:S(2)}) copy-start(bf16[32,128,128]{2,1,0:T(8,128)(2,1)S(1)} %all-to-all-done.2) | copy-start | bytes 3145732
  135.3 2.2 %copy-start.4 = (bf16[128,2560]{1,0:T(8,128)(2,1)S(1)}, bf16[128,2560]{1,0:T(8,128)(2,1)}, u32[]{:S(2)}) copy-start(bf16[128,2560]{1,0:T(8,128)(2,1)} %copy-done.3) | copy-start | bytes 1966084
  135.4 8.6 %collective-permute-start.7 = (bf16[8,4,128,128]{3,2,1,0:T(8,128)(2,1)S(1)}, bf16[8,4,128,128]{3,2,1,0:T(8,128)(2,1)S(1)}, u32[]{:S(2)}, u32[]{:S(2)}) collective-permute-start(bf16[8,4,128,128]{3,2,1,0:T(8,128)(2,1)S(1)} %broadcast_select_fusion), channel_id=1, source_target_pairs={{0,4},{4,0},{1,5},{5,1},{2,6},{6,2},{3,7},{7,3},{8,12},{12,8},{9,1... | collective-permute-start | bytes 3145736 | tf_op jit(solution)/shard_map/ppermute | solution.py:205
  138.0 0.9 copy-start.6
  138.0 1.0 copy-start.7
  144.0 1.0 copy-start.2
  150.8 21.7 %all-to-all-start.3 = ((bf16[4,128,640]{2,1,0:T(8,128)(2,1)}), bf16[4,128,640]{2,1,0:T(8,128)(2,1)S(1)}, u32[]{:S(2)}, u32[]{:S(2)}) async-start(bf16[4,128,640]{2,1,0:T(8,128)(2,1)} %attend.1), calls=%async_computation.3 | async-start | bytes 1310720 | tf_op jit(solution)/shard_map/all_to_all | solution.py:236
Sparse Core Ops, SparseCore 0:
  61.6 42.0 all-gather.2

commit v9 on v8

--- a/solution.py
+++ b/solution.py
@@ -158,26 +158,34 @@
         chosen = jnp.where(it == t, w_keyval[:, t * share : (t + 1) * share], chosen)
     kv_slab = jnp.concatenate([chosen, ids], axis=0)
     folded = jnp.concatenate([kv_slab[i : i + 8] for i in range(0, 32, 8)], axis=1)
-    near = spread(jnp.concatenate([w_query, w_out.T, folded], axis=0), ("yh", "z"), ny * nz)
-
-    others = [lax.ppermute(tokens, "tp", [(i, (i + k) % nx) for i in range(nx)]) for k in range(1, nx)]
-
-    kv_near = jnp.concatenate(
-        [near[:, 2 * rows :, i * share : (i + 1) * share] for i in range(slab // 8)], axis=1
-    )
-    kv_all = spread(kv_near, ("x", "c"), nx * nc)
-    part = nz * ny * rows
+    near = spread(folded, ("yh", "z"), ny * nz)
+
+    ring = lambda k: [(i, (i + k) % nx) for i in range(nx)]
+    others = [lax.ppermute(tokens, "tp", ring(k)) for k in range(1, nx)]
+
+    qo_near = spread(after(jnp.concatenate([w_query, w_out.T], axis=0), near), ("yh", "z"), ny * nz)
+    part = ny * nz * rows
     qo_send = jnp.concatenate(
-        [near[:, :rows].reshape(part, cols), near[:, rows : 2 * rows].reshape(part, cols)], axis=0
+        [qo_near[:, :rows].reshape(part, cols), qo_near[:, rows:].reshape(part, cols)], axis=0
     )
     qo_all = lax.all_gather(qo_send, ("x", "c"), axis=0, tiled=False)
 
-    groups = in_order([tokens, *others], it)
-    normed = rms_norm(jnp.concatenate(groups, axis=1), norm_gain)
+    kv_near = jnp.concatenate([near[:, :, i * share : (i + 1) * share] for i in range(slab // 8)], axis=1)
+    kv_far_x = [lax.ppermute(kv_near, "x", ring(k)) for k in range(1, nx)]
+    kv_mine = jnp.stack(in_order([kv_near, *kv_far_x], ix))
+    kv_twin = lax.ppermute(kv_mine, "c", both)
+
+    normed = rms_norm(jnp.concatenate(in_order([tokens, *others], it), axis=1), norm_gain)
     padded = turned(normed, natural_to_gathered(shard, rows, slab))
-    kv_all, padded = lax.optimization_barrier((kv_all, padded))
-
-    all_ids = kv_all[:, :, rows].astype(jnp.int32)
+    half = ny * nz * slab
+    of_core = [
+        jnp.concatenate([padded[:, i * half : (i + 1) * half] for i in range(c, nx * nc, nc)], axis=1)
+        for c in range(nc)
+    ]
+    for_mine = jnp.where(ic == 0, of_core[0], of_core[1])
+    for_twin = jnp.where(ic == 0, of_core[1], of_core[0])
+
+    all_ids = jnp.concatenate([kv_mine[:, :, rows], kv_twin[:, :, rows]], axis=0).astype(jnp.int32)
     labels = jnp.arange(SEGS, dtype=jnp.int32)
     starts = jnp.sum((all_ids.reshape(-1)[None, :] < labels[:, None]).astype(jnp.int32), axis=1)
     own_start = jnp.sum(jnp.where(seg_ids[:, None] == labels[None, :], starts[None, :], 0), axis=1)
@@ -185,8 +193,8 @@
     cosine, sine = angles((token_index - own_start).astype(jnp.float32))
 
     kv_raw = jnp.dot(
-        padded, kv_all.reshape(nx * nc * ny * nz * slab, share), preferred_element_type=jnp.float32
-    )
+        for_mine, kv_mine.reshape(nx * half, share), preferred_element_type=jnp.float32
+    ) + jnp.dot(for_twin, kv_twin.reshape(nx * half, share), preferred_element_type=jnp.float32)
     quarter = HD // 4
     swapped = jnp.concatenate([kv_raw[:, quarter:], kv_raw[:, :quarter]], axis=1)
     kv_share = jnp.where(it == 0, kv_raw * cosine + swapped * sine, kv_raw).astype(bf)
@@ -196,6 +204,7 @@
     before = lax.ppermute(kv_share, SEQ, [(i, i + block) for i in range(devices - block)])
     chips = jnp.arange(nz, dtype=jnp.int32)
     to_send = jnp.where((chips > iz)[:, None, None], kv_share[None], before[None])
+    to_send = after(to_send, qo_send)
     to_send = jnp.broadcast_to(to_send[:, None], (nz, nx, tok, share)).reshape(nz * nx, tok, share)
     mine = lax.all_to_all(to_send, ("z", "tp"), 0, 0, tiled=True).reshape(nz, nx, tok, share)
     rest = [lax.ppermute(kv_share, "tp", [(i, (i + k) % nx) for i in range(nx)]) for k in range(1, nx)]
@@ -214,7 +223,7 @@
 
     vmem = pl.BlockSpec(memory_space=pltpu.VMEM)
     hbm = pl.BlockSpec(memory_space=pl.ANY)
-    scratch = [pltpu.VMEM((nx * nc * part, cols), bf), pltpu.SemaphoreType.DMA((nx * nc,))]
+    scratch = [pltpu.VMEM((nx * shard, cols), bf), pltpu.SemaphoreType.DMA((nx * nc,))]
     queries = pl.pallas_call(
         queries_kernel,
         out_shape=jax.ShapeDtypeStruct((tok, cols), bf),

time: 183 us -> 194 us (1.060)
  the two profiles are of different devices: /device:TPU:2 before, /device:TPU:6 now
where the time goes in v9:
time: 194 us; the launch traced here: 193 us
  waiting for transfers between devices  72.8 us (38%)
  starting transfers between devices  70.7 us (36%)
  between operations  14.9 us (8%)
  Pallas kernels  9.96 us (5%)
  other arithmetic  8.93 us (5%)
  matrix products  8.93 us (5%)
  local copies, waits for them, and re-layouts  6.77 us (3%)
    all_to_all x2, waiting for transfers between devices, spread(): return lax.all_to_all(copies, axes, 0, 0, tiled=True)  27.1 us
    all_to_all x1, waiting for transfers between devices, per_device(): received = lax.all_to_all(partial, 'tp', 0, 0, tiled=True)  17.5 us
    all_to_all x2, starting transfers between devices, spread(): return lax.all_to_all(copies, axes, 0, 0, tiled=True)  17.5 us
    ppermute x3, waiting for transfers between devices, per_device(): lax.ppermute(kv_share, 'tp', [(i, (i + k) % nx) for i in range(nx)])  13.9 us
    ppermute x3, starting transfers between devices, per_device(): lax.ppermute(kv_share, 'tp', [(i, (i + k) % nx) for i in range(nx)])  12.2 us
    ppermute x3, starting transfers between devices, per_device(): others = [lax.ppermute(tokens, 'tp', ring(k)) for k in range(1, nx)]  12.1 us
    ppermute x3, starting transfers between devices, per_device(): kv_far_x = [lax.ppermute(kv_near, 'x', ring(k)) for k in range(1, nx)]  9.24 us
    ppermute x3, waiting for transfers between devices, per_device(): kv_far_x = [lax.ppermute(kv_near, 'x', ring(k)) for k in range(1, nx)]  7.92 us
  transfers between devices with their start and end apart: 17, of which 8 were waited for; matrix products, arithmetic and copies ran while one was open for 9% of the time, Pallas kernels for 2%

profile of v9, /device:TPU:6, one launch (start us, length us, event | category | flops | bytes accessed | tf_op | source)
XLA Modules:
  0.0 193.0 jit_solution(15683317701588834541)
XLA Ops:
  7.2 4.5 %collective-permute-start = (bf16[128,640]{1,0:T(8,128)(2,1)}, bf16[128,640]{1,0:T(8,128)(2,1)S(1)}, u32[]{:S(2)}, u32[]{:S(2)}) collective-permute-start(bf16[128,640]{1,0:T(8,128)(2,1)} %param.6), channel_id=1, source_target_pairs={{0,2},{1,3},{2,0},{3,1},{4,6},{5,7},{6,4},{7,5},{8,10},{9,11},{10,... | collective-permute-start | bytes 491528 | tf_op jit(solution)/shard_map/ppermute | solution.py:164
  11.7 3.5 %collective-permute-start.1 = (bf16[128,640]{1,0:T(8,128)(2,1)}, bf16[128,640]{1,0:T(8,128)(2,1)S(1)}, u32[]{:S(2)}, u32[]{:S(2)}) collective-permute-start(bf16[128,640]{1,0:T(8,128)(2,1)} %param.6), channel_id=1, source_target_pairs={{0,1},{1,2},{2,3},{3,0},{4,5},{5,6},{6,7},{7,4},{8,9},{9,10},{10,1... | collective-permute-start | bytes 491528 | tf_op jit(solution)/shard_map/ppermute | solution.py:164
  15.2 4.2 %collective-permute-start.2 = (bf16[128,640]{1,0:T(8,128)(2,1)}, bf16[128,640]{1,0:T(8,128)(2,1)S(1)}, u32[]{:S(2)}, u32[]{:S(2)}) collective-permute-start(bf16[128,640]{1,0:T(8,128)(2,1)} %param.6), channel_id=1, source_target_pairs={{0,3},{1,0},{2,1},{3,2},{4,7},{5,4},{6,5},{7,6},{8,11},{9,8},{10,9... | collective-permute-start | bytes 491528 | tf_op jit(solution)/shard_map/ppermute | solution.py:164
  19.3 0.7 convert_bitcast_fusion
  20.0 0.7 select_select_fusion.8
  20.8 0.7 broadcast_in_dim.56
  21.5 13.9 %all-to-all-start = ((bf16[16,8,512]{2,1,0:T(8,128)(2,1)}), bf16[16,8,512]{2,1,0:T(8,128)(2,1)S(1)}, u32[]{:S(2)}, u32[]{:S(2)}) async-start(bf16[16,8,512]{2,1,0:T(8,128)(2,1)} %broadcast_in_dim.56), calls=%async_computation | async-start | bytes 262144 | tf_op jit(solution)/shard_map/all_to_all | solution.py:36
  35.8 0.7 convert_element_type.77
  36.5 0.8 pad_maximum_fusion.14
  37.3 1.0 select_select_fusion.3
  38.3 0.2 fusion.28
  38.6 9.3 %all-to-all-done = bf16[16,8,512]{2,1,0:T(8,128)(2,1)S(1)} async-done(((bf16[16,8,512]{2,1,0:T(8,128)(2,1)}), bf16[16,8,512]{2,1,0:T(8,128)(2,1)S(1)}, u32[]{:S(2)}, u32[]{:S(2)}) %all-to-all-start) | async-done | bytes 131104 | tf_op jit(solution)/shard_map/all_to_all | solution.py:36
  47.8 0.9 broadcast_in_dim.67
  48.7 3.6 %all-to-all-start.1 = ((bf16[16,40,512]{2,1,0:T(8,128)(2,1)}), bf16[16,40,512]{2,1,0:T(8,128)(2,1)S(1)}, u32[]{:S(2)}, u32[]{:S(2)}) async-start(bf16[16,40,512]{2,1,0:T(8,128)(2,1)} %broadcast_in_dim.67), calls=%async_computation.1 | async-start | bytes 1310720 | tf_op jit(solution)/shard_map/all_to_all | solution.py:36
  52.4 0.2 fusion.30
  52.6 0.8 convolution_convert_fusion
  53.4 17.8 %all-to-all-done.1 = bf16[16,40,512]{2,1,0:T(8,128)(2,1)S(1)} async-done(((bf16[16,40,512]{2,1,0:T(8,128)(2,1)}), bf16[16,40,512]{2,1,0:T(8,128)(2,1)S(1)}, u32[]{:S(2)}, u32[]{:S(2)}) %all-to-all-start.1) | async-done | bytes 655392 | tf_op jit(solution)/shard_map/all_to_all | solution.py:36
  71.2 0.1 fusion.86
  71.6 0.9 copy-done.1
  72.5 0.8 convolution_convert_fusion.1
  73.3 0.8 convolution_convert_fusion.2
  74.1 0.8 convolution_convert_fusion.3
  75.0 3.3 %collective-permute-start.3 = (bf16[16,24,128]{2,1,0:T(8,128)(2,1)S(1)}, bf16[16,24,128]{2,1,0:T(8,128)(2,1)S(1)}, u32[]{:S(2)}, u32[]{:S(2)}) collective-permute-start(bf16[16,24,128]{2,1,0:T(8,128)(2,1)S(1)} %pad_maximum_fusion.7), channel_id=1, source_target_pairs={{0,256},{128,384},{256,0},{384,128},{1,257},{129,385},{257,1},{385... | collective-permute-start | bytes 294920 | tf_op jit(solution)/shard_map/ppermute | solution.py:174
  78.3 4.0 %collective-permute-start.4 = (bf16[16,24,128]{2,1,0:T(8,128)(2,1)S(1)}, bf16[16,24,128]{2,1,0:T(8,128)(2,1)S(1)}, u32[]{:S(2)}, u32[]{:S(2)}) collective-permute-start(bf16[16,24,128]{2,1,0:T(8,128)(2,1)S(1)} %pad_maximum_fusion.7), channel_id=1, source_target_pairs={{0,128},{128,256},{256,384},{384,0},{1,129},{129,257},{257,385},{3... | collective-permute-start | bytes 294920 | tf_op jit(solution)/shard_map/ppermute | solution.py:174
  82.3 1.9 collective-permute-start.5
  84.3 1.3 collective-permute-done.4
  85.6 6.6 %collective-permute-done.5 = bf16[16,24,128]{2,1,0:T(8,128)(2,1)S(1)} collective-permute-done((bf16[16,24,128]{2,1,0:T(8,128)(2,1)S(1)}, bf16[16,24,128]{2,1,0:T(8,128)(2,1)S(1)}, u32[]{:S(2)}, u32[]{:S(2)}) %collective-permute-start.5) | collective-permute-done | bytes 98336 | tf_op jit(solution)/shard_map/ppermute | solution.py:174
  92.4 1.9 collective-permute-start.6
  94.5 0.3 fusion.34
  94.7 1.3 collective-permute-done.6
  96.1 0.3 convert_reduce_fusion
  96.6 0.3 convolution_add_fusion.3
  96.9 0.3 fusion.50
  97.2 0.8 fusion.49
  98.0 5.0 %collective-permute-start.7 = (bf16[128,128]{1,0:T(8,128)(2,1)S(1)}, bf16[128,128]{1,0:T(8,128)(2,1)S(1)}, u32[]{:S(2)}, u32[]{:S(2)}) collective-permute-start(bf16[128,128]{1,0:T(8,128)(2,1)S(1)} %get-tuple-element.8), channel_id=1, source_target_pairs={{0,64},{4,68},{8,72},{12,76},{16,80},{20,84},{24,88},{28,92},{32,9... | collective-permute-start | bytes 98312 | tf_op jit(solution)/shard_map/ppermute | solution.py:204
  103.1 0.6 copy.36
  103.7 5.0 %collective-permute-done.7 = bf16[128,128]{1,0:T(8,128)(2,1)S(1)} collective-permute-done((bf16[128,128]{1,0:T(8,128)(2,1)S(1)}, bf16[128,128]{1,0:T(8,128)(2,1)S(1)}, u32[]{:S(2)}, u32[]{:S(2)}) %collective-permute-start.7) | collective-permute-done | bytes 32800 | tf_op jit(solution)/shard_map/ppermute | solution.py:204
  108.7 1.2 broadcast_in_dim.68
  110.0 7.1 %all-to-all-start.2 = ((bf16[32,128,128]{2,1,0:T(8,128)(2,1)}), bf16[32,128,128]{2,1,0:T(8,128)(2,1)S(1)}, u32[]{:S(2)}, u32[]{:S(2)}) async-start(bf16[32,128,128]{2,1,0:T(8,128)(2,1)} %bitcast.9), calls=%async_computation.2 | async-start | bytes 2097152 | tf_op jit(solution)/shard_map/all_to_all | solution.py:209
  117.1 4.6 %collective-permute-start.8 = (bf16[128,128]{1,0:T(8,128)(2,1)S(1)}, bf16[128,128]{1,0:T(8,128)(2,1)S(1)}, u32[]{:S(2)}, u32[]{:S(2)}) collective-permute-start(bf16[128,128]{1,0:T(8,128)(2,1)S(1)} %get-tuple-element.8), channel_id=1, source_target_pairs={{0,2},{1,3},{2,0},{3,1},{4,6},{5,7},{6,4},{7,5},{8,10},{9,11},{10,... | collective-permute-start | bytes 98312 | tf_op jit(solution)/shard_map/ppermute | solution.py:210
  121.7 3.4 %collective-permute-start.9 = (bf16[128,128]{1,0:T(8,128)(2,1)S(1)}, bf16[128,128]{1,0:T(8,128)(2,1)S(1)}, u32[]{:S(2)}, u32[]{:S(2)}) collective-permute-start(bf16[128,128]{1,0:T(8,128)(2,1)S(1)} %get-tuple-element.8), channel_id=1, source_target_pairs={{0,1},{1,2},{2,3},{3,0},{4,5},{5,6},{6,7},{7,4},{8,9},{9,10},{10,1... | collective-permute-start | bytes 98312 | tf_op jit(solution)/shard_map/ppermute | solution.py:210
  125.1 4.3 %collective-permute-start.10 = (bf16[128,128]{1,0:T(8,128)(2,1)S(1)}, bf16[128,128]{1,0:T(8,128)(2,1)S(1)}, u32[]{:S(2)}, u32[]{:S(2)}) collective-permute-start(bf16[128,128]{1,0:T(8,128)(2,1)S(1)} %get-tuple-element.8), channel_id=1, source_target_pairs={{0,3},{1,0},{2,1},{3,2},{4,7},{5,4},{6,5},{7,6},{8,11},{9,8},{10,9... | collective-permute-start | bytes 98312 | tf_op jit(solution)/shard_map/ppermute | solution.py:210
  129.4 0.1 copy.24
  129.5 0.7 add_maximum_fusion
  130.2 13.9 %collective-permute-done.8 = bf16[128,128]{1,0:T(8,128)(2,1)S(1)} collective-permute-done((bf16[128,128]{1,0:T(8,128)(2,1)S(1)}, bf16[128,128]{1,0:T(8,128)(2,1)S(1)}, u32[]{:S(2)}, u32[]{:S(2)}) %collective-permute-start.8) | collective-permute-done | bytes 32800 | tf_op jit(solution)/shard_map/ppermute | solution.py:210
  144.2 0.5 convolution_convert_fusion.4
  144.7 1.2 convolution_convert_fusion.5
  145.9 0.1 broadcast_select_fusion
  146.0 2.1 %collective-permute-start.11 = (bf16[8,4,128,128]{3,2,1,0:T(8,128)(2,1)S(1)}, bf16[8,4,128,128]{3,2,1,0:T(8,128)(2,1)S(1)}, u32[]{:S(2)}, u32[]{:S(2)}) collective-permute-start(bf16[8,4,128,128]{3,2,1,0:T(8,128)(2,1)S(1)} %broadcast_select_fusion), channel_id=1, source_target_pairs={{0,4},{4,0},{1,5},{5,1},{2,6},{6,2},{3,7},{7,3},{8,12},{12,8},{9,1... | collective-permute-start | bytes 3145736 | tf_op jit(solution)/shard_map/ppermute | solution.py:214
  148.1 0.5 convolution_convert_fusion.6
  148.6 0.5 convolution_convert_fusion.7
  149.1 0.4 copy-done.7
  149.5 0.9 pad_maximum_fusion.1.normed_ref
  150.4 4.1 %queries.1.queries_ref = bf16[128,512]{1,0:T(8,128)(2,1)} custom-call(bf16[128,2560]{1,0:T(8,128)(2,1)} %pad_maximum_fusion.1.normed_ref, f32[128,128]{1,0:T(8,128)} %get-tuple-element.35.cosine_ref, f32[128,128]{1,0:T(8,128)} %get-tuple-element.9.sine_ref, bf16[8,640,512]{2,1,0:T(8,128)(2,1)} %bitcast.50), custom_call_target="tpu_custom_call" | custom-call | tf_op jit(solution)/shard_map/queries/pallas_call | solution.py:227
  154.5 1.0 copy-done.3
  155.5 5.9 %attend.1 = bf16[4,128,640]{2,1,0:T(8,128)(2,1)} custom-call(bf16[128,512]{1,0:T(8,128)(2,1)} %queries.1.queries_ref, bf16[8,4,128,128]{3,2,1,0:T(8,128)(2,1)} %bitcast.53, bf16[8,4,128,128]{3,2,1,0:T(8,128)(2,1)} %copy-done.3, bf16[4,128,128]{2,1,0:T(8,128)(2,1)} %copy-done.2, s32[1,2176]{1,0:T(1,128)} %bitcast.62, s32[128,1]{1,0:T(8,128)} %get-tuple-element.51.token_ref, ...), custom_call_target="tpu_custom_call" | custom-call | tf_op jit(solution)/shard_map/attend/pallas_call | solution.py:236
  161.4 3.5 %all-to-all-start.3 = ((bf16[4,128,640]{2,1,0:T(8,128)(2,1)}), bf16[4,128,640]{2,1,0:T(8,128)(2,1)S(1)}, u32[]{:S(2)}, u32[]{:S(2)}) async-start(bf16[4,128,640]{2,1,0:T(8,128)(2,1)} %attend.1), calls=%async_computation.3 | async-start | bytes 1310720 | tf_op jit(solution)/shard_map/all_to_all | solution.py:245
  164.9 0.7 pad_maximum_fusion.6
  165.6 17.5 %all-to-all-done.3 = bf16[4,128,640]{2,1,0:T(8,128)(2,1)S(1)} async-done(((bf16[4,128,640]{2,1,0:T(8,128)(2,1)}), bf16[4,128,640]{2,1,0:T(8,128)(2,1)S(1)}, u32[]{:S(2)}, u32[]{:S(2)}) %all-to-all-start.3) | async-done | bytes 655392 | tf_op jit(solution)/shard_map/all_to_all | solution.py:245
  183.1 0.5 fusion.38
  183.6 0.5 convolution_add_fusion.2
  184.1 0.5 convolution_add_fusion.1
  184.5 0.4 copy-done.6
  185.0 1.1 fusion.32
  (68 shorter events, 1.4 us)
Async XLA Ops:
  7.2 30.1 %collective-permute-start = (bf16[128,640]{1,0:T(8,128)(2,1)}, bf16[128,640]{1,0:T(8,128)(2,1)S(1)}, u32[]{:S(2)}, u32[]{:S(2)}) collective-permute-start(bf16[128,640]{1,0:T(8,128)(2,1)} %param.6), channel_id=1, source_target_pairs={{0,2},{1,3},{2,0},{3,1},{4,6},{5,7},{6,4},{7,5},{8,10},{9,11},{10,... | collective-permute-start | bytes 491528 | tf_op jit(solution)/shard_map/ppermute | solution.py:164
  11.7 25.6 %collective-permute-start.1 = (bf16[128,640]{1,0:T(8,128)(2,1)}, bf16[128,640]{1,0:T(8,128)(2,1)S(1)}, u32[]{:S(2)}, u32[]{:S(2)}) collective-permute-start(bf16[128,640]{1,0:T(8,128)(2,1)} %param.6), channel_id=1, source_target_pairs={{0,1},{1,2},{2,3},{3,0},{4,5},{5,6},{6,7},{7,4},{8,9},{9,10},{10,1... | collective-permute-start | bytes 491528 | tf_op jit(solution)/shard_map/ppermute | solution.py:164
  15.2 22.1 %collective-permute-start.2 = (bf16[128,640]{1,0:T(8,128)(2,1)}, bf16[128,640]{1,0:T(8,128)(2,1)S(1)}, u32[]{:S(2)}, u32[]{:S(2)}) collective-permute-start(bf16[128,640]{1,0:T(8,128)(2,1)} %param.6), channel_id=1, source_target_pairs={{0,3},{1,0},{2,1},{3,2},{4,7},{5,4},{6,5},{7,6},{8,11},{9,8},{10,9... | collective-permute-start | bytes 491528 | tf_op jit(solution)/shard_map/ppermute | solution.py:164
  21.5 26.4 %all-to-all-start = ((bf16[16,8,512]{2,1,0:T(8,128)(2,1)}), bf16[16,8,512]{2,1,0:T(8,128)(2,1)S(1)}, u32[]{:S(2)}, u32[]{:S(2)}) async-start(bf16[16,8,512]{2,1,0:T(8,128)(2,1)} %broadcast_in_dim.56), calls=%async_computation | async-start | bytes 262144 | tf_op jit(solution)/shard_map/all_to_all | solution.py:36
  48.7 22.5 %all-to-all-start.1 = ((bf16[16,40,512]{2,1,0:T(8,128)(2,1)}), bf16[16,40,512]{2,1,0:T(8,128)(2,1)S(1)}, u32[]{:S(2)}, u32[]{:S(2)}) async-start(bf16[16,40,512]{2,1,0:T(8,128)(2,1)} %broadcast_in_dim.67), calls=%async_computation.1 | async-start | bytes 1310720 | tf_op jit(solution)/shard_map/all_to_all | solution.py:36
  52.3 98.1 %all-gather.3.cloned.1.call-start = ((), (), s32[]{:S(2)}) async-start(), calls=%async_computation.4 | async-start | bytes 5898240 | tf_op jit(solution)/shard_map/all_gather | solution.py:171
  52.6 92.1 %copy-start.4 = (bf16[128,2560]{1,0:T(8,128)(2,1)}, bf16[128,2560]{1,0:T(8,128)(2,1)S(1)}, u32[]{:S(2)}) copy-start(bf16[128,2560]{1,0:T(8,128)(2,1)S(1)} %fusion.30) | copy-start | bytes 1966084
  71.6 0.9 copy-start.1
  75.0 9.3 %collective-permute-start.3 = (bf16[16,24,128]{2,1,0:T(8,128)(2,1)S(1)}, bf16[16,24,128]{2,1,0:T(8,128)(2,1)S(1)}, u32[]{:S(2)}, u32[]{:S(2)}) collective-permute-start(bf16[16,24,128]{2,1,0:T(8,128)(2,1)S(1)} %pad_maximum_fusion.7), channel_id=1, source_target_pairs={{0,256},{128,384},{256,0},{384,128},{1,257},{129,385},{257,1},{385... | collective-permute-start | bytes 294920 | tf_op jit(solution)/shard_map/ppermute | solution.py:174
  78.3 7.3 %collective-permute-start.4 = (bf16[16,24,128]{2,1,0:T(8,128)(2,1)S(1)}, bf16[16,24,128]{2,1,0:T(8,128)(2,1)S(1)}, u32[]{:S(2)}, u32[]{:S(2)}) collective-permute-start(bf16[16,24,128]{2,1,0:T(8,128)(2,1)S(1)} %pad_maximum_fusion.7), channel_id=1, source_target_pairs={{0,128},{128,256},{256,384},{384,0},{1,129},{129,257},{257,385},{3... | collective-permute-start | bytes 294920 | tf_op jit(solution)/shard_map/ppermute | solution.py:174
  82.3 9.9 %collective-permute-start.5 = (bf16[16,24,128]{2,1,0:T(8,128)(2,1)S(1)}, bf16[16,24,128]{2,1,0:T(8,128)(2,1)S(1)}, u32[]{:S(2)}, u32[]{:S(2)}) collective-permute-start(bf16[16,24,128]{2,1,0:T(8,128)(2,1)S(1)} %pad_maximum_fusion.7), channel_id=1, source_target_pairs={{0,384},{128,0},{256,128},{384,256},{1,385},{129,1},{257,129},{385... | collective-permute-start | bytes 294920 | tf_op jit(solution)/shard_map/ppermute | solution.py:174
  92.4 3.6 %collective-permute-start.6 = (bf16[4,16,24,128]{3,2,1,0:T(8,128)(2,1)S(1)}, bf16[4,16,24,128]{3,2,1,0:T(8,128)(2,1)S(1)}, u32[]{:S(2)}, u32[]{:S(2)}) collective-permute-start(bf16[4,16,24,128]{3,2,1,0:T(8,128)(2,1)S(1)} %pad_maximum_fusion.4), channel_id=1, source_target_pairs={{0,4},{4,0},{1,5},{5,1},{2,6},{6,2},{3,7},{7,3},{8,12},{12,8},{9,1... | collective-permute-start | bytes 1179656 | tf_op jit(solution)/shard_map/ppermute | solution.py:176
  94.5 2.0 %copy-start.8 = (s32[128]{0:T(128)S(1)}, s32[128]{0:T(128)}, u32[]{:S(2)}) copy-start(s32[128]{0:T(128)} %param.7) | copy-start | bytes 1540
  98.0 10.6 %collective-permute-start.7 = (bf16[128,128]{1,0:T(8,128)(2,1)S(1)}, bf16[128,128]{1,0:T(8,128)(2,1)S(1)}, u32[]{:S(2)}, u32[]{:S(2)}) collective-permute-start(bf16[128,128]{1,0:T(8,128)(2,1)S(1)} %get-tuple-element.8), channel_id=1, source_target_pairs={{0,64},{4,68},{8,72},{12,76},{16,80},{20,84},{24,88},{28,92},{32,9... | collective-permute-start | bytes 98312 | tf_op jit(solution)/shard_map/ppermute | solution.py:204
  110.0 35.9 %all-to-all-start.2 = ((bf16[32,128,128]{2,1,0:T(8,128)(2,1)}), bf16[32,128,128]{2,1,0:T(8,128)(2,1)S(1)}, u32[]{:S(2)}, u32[]{:S(2)}) async-start(bf16[32,128,128]{2,1,0:T(8,128)(2,1)} %bitcast.9), calls=%async_computation.2 | async-start | bytes 2097152 | tf_op jit(solution)/shard_map/all_to_all | solution.py:209
  117.1 26.9 %collective-permute-start.8 = (bf16[128,128]{1,0:T(8,128)(2,1)S(1)}, bf16[128,128]{1,0:T(8,128)(2,1)S(1)}, u32[]{:S(2)}, u32[]{:S(2)}) collective-permute-start(bf16[128,128]{1,0:T(8,128)(2,1)S(1)} %get-tuple-element.8), channel_id=1, source_target_pairs={{0,2},{1,3},{2,0},{3,1},{4,6},{5,7},{6,4},{7,5},{8,10},{9,11},{10,... | collective-permute-start | bytes 98312 | tf_op jit(solution)/shard_map/ppermute | solution.py:210
  121.7 22.3 %collective-permute-start.9 = (bf16[128,128]{1,0:T(8,128)(2,1)S(1)}, bf16[128,128]{1,0:T(8,128)(2,1)S(1)}, u32[]{:S(2)}, u32[]{:S(2)}) collective-permute-start(bf16[128,128]{1,0:T(8,128)(2,1)S(1)} %get-tuple-element.8), channel_id=1, source_target_pairs={{0,1},{1,2},{2,3},{3,0},{4,5},{5,6},{6,7},{7,4},{8,9},{9,10},{10,1... | collective-permute-start | bytes 98312 | tf_op jit(solution)/shard_map/ppermute | solution.py:210
  125.1 19.0 %collective-permute-start.10 = (bf16[128,128]{1,0:T(8,128)(2,1)S(1)}, bf16[128,128]{1,0:T(8,128)(2,1)S(1)}, u32[]{:S(2)}, u32[]{:S(2)}) collective-permute-start(bf16[128,128]{1,0:T(8,128)(2,1)S(1)} %get-tuple-element.8), channel_id=1, source_target_pairs={{0,3},{1,0},{2,1},{3,2},{4,7},{5,4},{6,5},{7,6},{8,11},{9,8},{10,9... | collective-permute-start | bytes 98312 | tf_op jit(solution)/shard_map/ppermute | solution.py:210
  144.1 1.7 copy-start.2
  145.9 2.7 %copy-start = (bf16[32,128,128]{2,1,0:T(8,128)(2,1)}, bf16[32,128,128]{2,1,0:T(8,128)(2,1)S(1)}, u32[]{:S(2)}) copy-start(bf16[32,128,128]{2,1,0:T(8,128)(2,1)S(1)} %all-to-all-done.2) | copy-start | bytes 3145732
  145.9 2.2 %copy-start.5 = (bf16[128,2560]{1,0:T(8,128)(2,1)S(1)}, bf16[128,2560]{1,0:T(8,128)(2,1)}, u32[]{:S(2)}) copy-start(bf16[128,2560]{1,0:T(8,128)(2,1)} %copy-done.4) | copy-start | bytes 1966084
  146.0 8.5 %collective-permute-start.11 = (bf16[8,4,128,128]{3,2,1,0:T(8,128)(2,1)S(1)}, bf16[8,4,128,128]{3,2,1,0:T(8,128)(2,1)S(1)}, u32[]{:S(2)}, u32[]{:S(2)}) collective-permute-start(bf16[8,4,128,128]{3,2,1,0:T(8,128)(2,1)S(1)} %broadcast_select_fusion), channel_id=1, source_target_pairs={{0,4},{4,0},{1,5},{5,1},{2,6},{6,2},{3,7},{7,3},{8,12},{12,8},{9,1... | collective-permute-start | bytes 3145736 | tf_op jit(solution)/shard_map/ppermute | solution.py:214
  148.6 0.9 copy-start.7
  154.5 1.0 copy-start.3
  161.4 21.7 %all-to-all-start.3 = ((bf16[4,128,640]{2,1,0:T(8,128)(2,1)}), bf16[4,128,640]{2,1,0:T(8,128)(2,1)S(1)}, u32[]{:S(2)}, u32[]{:S(2)}) async-start(bf16[4,128,640]{2,1,0:T(8,128)(2,1)} %attend.1), calls=%async_computation.3 | async-start | bytes 1310720 | tf_op jit(solution)/shard_map/all_to_all | solution.py:245
  184.1 0.9 copy-start.6
Sparse Core Ops, SparseCore 0:
  72.6 36.0 all-gather.2

commit v10 on v8

--- a/solution.py
+++ b/solution.py
@@ -98,33 +98,60 @@
         )
 
 
+def scores_of(queries_ref, h, keys, live):
+    scores = lax.dot_general(
+        queries_ref[:, h * HD : (h + 1) * HD], keys, (((1,), (1,)), ((), ())), preferred_element_type=jnp.float32
+    )
+    return jnp.where(live, scores, -1e30)
+
+
+def near_kernel(queries_ref, mine_ref, own_ref, keys_at_ref, token_ref, first_ref, sums_ref, stats_ref):
+    def whole(t):
+        far = mine_ref[:, t].reshape(mine_ref.shape[0] * mine_ref.shape[2], mine_ref.shape[3])
+        return jnp.concatenate([far, own_ref[t]], axis=0)
+
+    keys = jnp.concatenate([whole(0), whole(1)], axis=1)
+    values = jnp.concatenate([whole(2), whole(3)], axis=1)
+    at = keys_at_ref[...]
+    live = (at <= token_ref[...]) & (at >= first_ref[...])
+    heads = queries_ref.shape[1] // HD
+    for h in range(heads):
+        scores = scores_of(queries_ref, h, keys, live)
+        peak = jnp.max(scores, axis=1, keepdims=True)
+        powered = jnp.exp(scores - peak)
+        stats_ref[h] = jnp.broadcast_to(peak, stats_ref.shape[1:])
+        stats_ref[heads + h] = jnp.broadcast_to(
+            jnp.sum(powered, axis=1, keepdims=True), stats_ref.shape[1:]
+        )
+        sums_ref[:, h * HD : (h + 1) * HD] = jnp.dot(
+            powered.astype(jnp.bfloat16), values, preferred_element_type=jnp.float32
+        )
+
+
 def attend_kernel(
-    queries_ref, mine_ref, partner_ref, own_ref, keys_at_ref, token_ref, first_ref, qo_ref, out_ref, weights_ref, sems
+    queries_ref, partner_ref, keys_at_ref, token_ref, first_ref, sums_ref, stats_ref, qo_ref, out_ref, weights_ref, sems
 ):
     copies = fetch(qo_ref, 1, weights_ref, sems)
-
-    def whole(t):
-        far = [ref[:, t].reshape(ref.shape[0] * ref.shape[2], ref.shape[3]) for ref in (mine_ref, partner_ref)]
-        return jnp.concatenate([*far, own_ref[t]], axis=0)
-
+    whole = lambda t: partner_ref[:, t].reshape(
+        partner_ref.shape[0] * partner_ref.shape[2], partner_ref.shape[3]
+    )
     keys = jnp.concatenate([whole(0), whole(1)], axis=1)
     values = jnp.concatenate([whole(2), whole(3)], axis=1)
     at = keys_at_ref[...]
     live = (at <= token_ref[...]) & (at >= first_ref[...])
     heads = []
-    for h in range(queries_ref.shape[1] // HD):
-        scores = lax.dot_general(
-            queries_ref[:, h * HD : (h + 1) * HD],
-            keys,
-            (((1,), (1,)), ((), ())),
-            preferred_element_type=jnp.float32,
-        )
-        scores = jnp.where(live, scores, -1e30)
-        powered = jnp.exp(scores - jnp.max(scores, axis=1, keepdims=True))
-        weights = (powered * (1.0 / jnp.sum(powered, axis=1, keepdims=True))).astype(jnp.bfloat16)
-        heads.append(
-            jnp.dot(weights, values, preferred_element_type=jnp.float32).astype(jnp.bfloat16)
-        )
+    count = queries_ref.shape[1] // HD
+    for h in range(count):
+        scores = scores_of(queries_ref, h, keys, live)
+        before = stats_ref[h][:, :1]
+        peak = jnp.maximum(before, jnp.max(scores, axis=1, keepdims=True))
+        powered = jnp.exp(scores - peak)
+        shrink = jnp.exp(before - peak)
+        total = shrink * stats_ref[count + h][:, :1] + jnp.sum(powered, axis=1, keepdims=True)
+        summed = shrink * sums_ref[:, h * HD : (h + 1) * HD] + jnp.dot(
+            powered.astype(jnp.bfloat16), values, preferred_element_type=jnp.float32
+        )
+        heads.append((summed * (1.0 / total)).astype(jnp.bfloat16))
     attended = jnp.concatenate(heads, axis=1)
     shard = out_ref.shape[2]
     for copy in copies:
@@ -165,19 +192,27 @@
     kv_near = jnp.concatenate(
         [near[:, 2 * rows :, i * share : (i + 1) * share] for i in range(slab // 8)], axis=1
     )
-    kv_all = spread(kv_near, ("x", "c"), nx * nc)
+    kv_mine = spread(kv_near, "x", nx)
+    kv_twin = lax.ppermute(kv_mine, "c", both)
     part = nz * ny * rows
     qo_send = jnp.concatenate(
         [near[:, :rows].reshape(part, cols), near[:, rows : 2 * rows].reshape(part, cols)], axis=0
     )
     qo_all = lax.all_gather(qo_send, ("x", "c"), axis=0, tiled=False)
 
-    groups = in_order([tokens, *others], it)
-    normed = rms_norm(jnp.concatenate(groups, axis=1), norm_gain)
+    *others, _ = lax.optimization_barrier((*others, qo_send))
+    normed = rms_norm(jnp.concatenate(in_order([tokens, *others], it), axis=1), norm_gain)
     padded = turned(normed, natural_to_gathered(shard, rows, slab))
-    kv_all, padded = lax.optimization_barrier((kv_all, padded))
-
-    all_ids = kv_all[:, :, rows].astype(jnp.int32)
+    half = ny * nz * slab
+    of_core = [
+        jnp.concatenate([padded[:, i * half : (i + 1) * half] for i in range(c, nx * nc, nc)], axis=1)
+        for c in range(nc)
+    ]
+    for_mine = jnp.where(ic == 0, of_core[0], of_core[1])
+    for_twin = jnp.where(ic == 0, of_core[1], of_core[0])
+    kv_mine, for_mine, for_twin = lax.optimization_barrier((kv_mine, for_mine, for_twin))
+
+    all_ids = jnp.concatenate([kv_mine[:, :, rows], kv_twin[:, :, rows]], axis=0).astype(jnp.int32)
     labels = jnp.arange(SEGS, dtype=jnp.int32)
     starts = jnp.sum((all_ids.reshape(-1)[None, :] < labels[:, None]).astype(jnp.int32), axis=1)
     own_start = jnp.sum(jnp.where(seg_ids[:, None] == labels[None, :], starts[None, :], 0), axis=1)
@@ -185,8 +220,8 @@
     cosine, sine = angles((token_index - own_start).astype(jnp.float32))
 
     kv_raw = jnp.dot(
-        padded, kv_all.reshape(nx * nc * ny * nz * slab, share), preferred_element_type=jnp.float32
-    )
+        for_mine, kv_mine.reshape(nx * half, share), preferred_element_type=jnp.float32
+    ) + jnp.dot(for_twin, kv_twin.reshape(nx * half, share), preferred_element_type=jnp.float32)
     quarter = HD // 4
     swapped = jnp.concatenate([kv_raw[:, quarter:], kv_raw[:, :quarter]], axis=1)
     kv_share = jnp.where(it == 0, kv_raw * cosine + swapped * sine, kv_raw).astype(bf)
@@ -209,8 +244,10 @@
     block_of_partner = my_block - jnp.where(ic == 1, chips > iz, chips >= iz).astype(jnp.int32)
     first_of_mine = ((block_of_mine * nz + chips) * nc + ic) * tok
     first_of_partner = ((block_of_partner * nz + chips) * nc + 1 - ic) * tok
-    firsts = jnp.concatenate([first_of_mine, first_of_partner, my_index[None] * tok])
-    keys_at = (firsts[:, None] + jnp.arange(tok, dtype=jnp.int32)[None, :]).reshape(1, -1)
+    along = jnp.arange(tok, dtype=jnp.int32)[None, :]
+    near_firsts = jnp.concatenate([first_of_mine, my_index[None] * tok])
+    near_at = (near_firsts[:, None] + along).reshape(1, -1)
+    far_at = (first_of_partner[:, None] + along).reshape(1, -1)
 
     vmem = pl.BlockSpec(memory_space=pltpu.VMEM)
     hbm = pl.BlockSpec(memory_space=pl.ANY)
@@ -224,6 +261,18 @@
         name="queries",
     )(reordered, cosine, sine, qo_all)
     reach_back = jnp.maximum(own_start, token_index - (WINDOW - 1))
+    token_at, first_at = token_index[:, None], reach_back[:, None]
+    heads = cols // HD
+    sums, stats = pl.pallas_call(
+        near_kernel,
+        out_shape=(
+            jax.ShapeDtypeStruct((tok, cols), jnp.float32),
+            jax.ShapeDtypeStruct((2 * heads, tok, share), jnp.float32),
+        ),
+        in_specs=[vmem] * 6,
+        out_specs=(vmem, vmem),
+        name="near",
+    )(queries, mine, own_kv, near_at, token_at, first_at)
     partial = pl.pallas_call(
         attend_kernel,
         out_shape=jax.ShapeDtypeStruct((nx, tok, shard), bf),
@@ -231,7 +280,7 @@
         out_specs=vmem,
         scratch_shapes=scratch,
         name="attend",
-    )(queries, mine, partner, own_kv, keys_at, token_index[:, None], reach_back[:, None], qo_all)
+    )(queries, partner, far_at, token_at, first_at, sums, stats, qo_all)
 
     received = lax.all_to_all(partial, "tp", 0, 0, tiled=True)
     summed = jnp.zeros((tok, shard), jnp.float32)

time: 183 us -> 178 us (0.973)
  the two profiles are of different devices: /device:TPU:2 before, /device:TPU:56 now
where the time goes in v10:
time: 178 us; the launch traced here: 177 us
  waiting for transfers between devices  66.3 us (37%)
  starting transfers between devices  59.1 us (33%)
  between operations  14.7 us (8%)
  Pallas kernels  12.3 us (7%)
  matrix products  9.61 us (5%)
  other arithmetic  8.53 us (5%)
  local copies, waits for them, and re-layouts  6.64 us (4%)
    all_to_all x2, starting transfers between devices, spread(): return lax.all_to_all(copies, axes, 0, 0, tiled=True)  20 us
    all_to_all x2, waiting for transfers between devices, spread(): return lax.all_to_all(copies, axes, 0, 0, tiled=True)  17.7 us
    all_to_all x1, waiting for transfers between devices, per_device(): received = lax.all_to_all(partial, 'tp', 0, 0, tiled=True)  15.2 us
    ppermute x3, waiting for transfers between devices, per_device(): lax.ppermute(kv_share, 'tp', [(i, (i + k) % nx) for i in range(nx)])  14.2 us
    ppermute x3, waiting for transfers between devices, per_device(): lax.ppermute(tokens, 'tp', [(i, (i + k) % nx) for i in range(nx)])  10.7 us
    ppermute x3, starting transfers between devices, per_device(): lax.ppermute(tokens, 'tp', [(i, (i + k) % nx) for i in range(nx)])  9.88 us
    all_to_all x1, starting transfers between devices, per_device(): lax.all_to_all(to_send, ('z', 'tp'), 0, 0, tiled=True)  8.87 us
    ppermute x3, starting transfers between devices, per_device(): lax.ppermute(kv_share, 'tp', [(i, (i + k) % nx) for i in range(nx)])  8.65 us
  transfers between devices with their start and end apart: 14, of which 8 were waited for; matrix products, arithmetic and copies ran while one was open for 9% of the time, Pallas kernels for 4%

profile of v10, /device:TPU:56, one launch (start us, length us, event | category | flops | bytes accessed | tf_op | source)
XLA Modules:
  0.0 177.2 jit_solution(2515964192373124065)
XLA Ops:
  7.2 0.7 convert_bitcast_fusion
  7.9 0.7 select_select_fusion.8
  8.7 0.8 maximum_maximum_fusion
  9.5 1.0 broadcast_in_dim.55
  10.4 15.7 %all-to-all-start = ((bf16[16,48,512]{2,1,0:T(8,128)(2,1)}), bf16[16,48,512]{2,1,0:T(8,128)(2,1)S(1)}, u32[]{:S(2)}, u32[]{:S(2)}) async-start(bf16[16,48,512]{2,1,0:T(8,128)(2,1)} %broadcast_in_dim.55), calls=%async_computation | async-start | bytes 1572864 | tf_op jit(solution)/shard_map/all_to_all | solution.py:36
  26.2 4.8 %collective-permute-start = (bf16[128,640]{1,0:T(8,128)(2,1)S(1)}, bf16[128,640]{1,0:T(8,128)(2,1)S(1)}, u32[]{:S(2)}, u32[]{:S(2)}) collective-permute-start(bf16[128,640]{1,0:T(8,128)(2,1)S(1)} %copy-done.6), channel_id=1, source_target_pairs={{0,1},{1,2},{2,3},{3,0},{4,5},{5,6},{6,7},{7,4},{8,9},{9,10},{10,1... | collective-permute-start | bytes 491528 | tf_op jit(solution)/shard_map/ppermute | solution.py:190
  31.0 1.9 %collective-permute-start.1 = (bf16[128,640]{1,0:T(8,128)(2,1)S(1)}, bf16[128,640]{1,0:T(8,128)(2,1)S(1)}, u32[]{:S(2)}, u32[]{:S(2)}) collective-permute-start(bf16[128,640]{1,0:T(8,128)(2,1)S(1)} %copy-done.6), channel_id=1, source_target_pairs={{0,2},{1,3},{2,0},{3,1},{4,6},{5,7},{6,4},{7,5},{8,10},{9,11},{10,... | collective-permute-start | bytes 491528 | tf_op jit(solution)/shard_map/ppermute | solution.py:190
  33.0 3.1 %collective-permute-start.2 = (bf16[128,640]{1,0:T(8,128)(2,1)S(1)}, bf16[128,640]{1,0:T(8,128)(2,1)S(1)}, u32[]{:S(2)}, u32[]{:S(2)}) collective-permute-start(bf16[128,640]{1,0:T(8,128)(2,1)S(1)} %copy-done.6), channel_id=1, source_target_pairs={{0,3},{1,0},{2,1},{3,2},{4,7},{5,4},{6,5},{7,6},{8,11},{9,8},{10,9... | collective-permute-start | bytes 491528 | tf_op jit(solution)/shard_map/ppermute | solution.py:190
  36.5 10.3 %all-to-all-done = bf16[16,48,512]{2,1,0:T(8,128)(2,1)S(1)} async-done(((bf16[16,48,512]{2,1,0:T(8,128)(2,1)}), bf16[16,48,512]{2,1,0:T(8,128)(2,1)S(1)}, u32[]{:S(2)}, u32[]{:S(2)}) %all-to-all-start) | async-done | bytes 786464 | tf_op jit(solution)/shard_map/all_to_all | solution.py:36
  46.8 0.1 fusion.80
  47.1 0.8 copy-done.1
  48.0 0.2 collective-permute-done
  48.2 10.5 %collective-permute-done.1 = bf16[128,640]{1,0:T(8,128)(2,1)S(1)} collective-permute-done((bf16[128,640]{1,0:T(8,128)(2,1)S(1)}, bf16[128,640]{1,0:T(8,128)(2,1)S(1)}, u32[]{:S(2)}, u32[]{:S(2)}) %collective-permute-start.1) | collective-permute-done | bytes 163872 | tf_op jit(solution)/shard_map/ppermute | solution.py:190
  58.7 0.1 select_select_fusion.3
  58.8 0.2 fusion.28
  59.1 0.8 broadcast_in_dim.57
  59.9 4.3 %all-to-all-start.1 = ((bf16[4,16,24,128]{3,2,1,0:T(8,128)(2,1)}), bf16[4,16,24,128]{3,2,1,0:T(8,128)(2,1)S(1)}, u32[]{:S(2)}, u32[]{:S(2)}) async-start(bf16[4,16,24,128]{3,2,1,0:T(8,128)(2,1)} %broadcast_in_dim.57), calls=%async_computation.1 | async-start | bytes 786432 | tf_op jit(solution)/shard_map/all_to_all | solution.py:36
  64.2 0.2 fusion.30
  64.4 0.8 convolution_convert_fusion.3
  65.2 0.8 convolution_convert_fusion.2
  66.1 0.8 convolution_convert_fusion.1
  66.9 0.8 convolution_convert_fusion
  67.7 7.4 %all-to-all-done.1 = bf16[4,16,24,128]{3,2,1,0:T(8,128)(2,1)S(1)} async-done(((bf16[4,16,24,128]{3,2,1,0:T(8,128)(2,1)}), bf16[4,16,24,128]{3,2,1,0:T(8,128)(2,1)S(1)}, u32[]{:S(2)}, u32[]{:S(2)}) %all-to-all-start.1) | async-done | bytes 393248 | tf_op jit(solution)/shard_map/all_to_all | solution.py:36
  75.2 1.9 %collective-permute-start.3 = (bf16[4,16,24,128]{3,2,1,0:T(8,128)(2,1)S(1)}, bf16[4,16,24,128]{3,2,1,0:T(8,128)(2,1)S(1)}, u32[]{:S(2)}, u32[]{:S(2)}) collective-permute-start(bf16[4,16,24,128]{3,2,1,0:T(8,128)(2,1)S(1)} %all-to-all-done.1), channel_id=1, source_target_pairs={{0,4},{4,0},{1,5},{5,1},{2,6},{6,2},{3,7},{7,3},{8,12},{12,8},{9,1... | collective-permute-start | bytes 1179656 | tf_op jit(solution)/shard_map/ppermute | solution.py:196
  77.1 0.1 broadcast_select_fusion.1
  77.3 0.2 fusion.87
  77.5 1.4 collective-permute-done.3
  79.0 0.3 convert_reduce_fusion
  79.3 0.1 select_reduce_fusion
  79.4 0.3 convolution_add_fusion.3
  79.7 0.3 fusion.45
  80.1 0.8 fusion.44
  80.8 1.9 %collective-permute-start.4 = (bf16[128,128]{1,0:T(8,128)(2,1)S(1)}, bf16[128,128]{1,0:T(8,128)(2,1)S(1)}, u32[]{:S(2)}, u32[]{:S(2)}) collective-permute-start(bf16[128,128]{1,0:T(8,128)(2,1)S(1)} %get-tuple-element.20), channel_id=1, source_target_pairs={{0,64},{4,68},{8,72},{12,76},{16,80},{20,84},{24,88},{28,92},{32,9... | collective-permute-start | bytes 98312 | tf_op jit(solution)/shard_map/ppermute | solution.py:231
  82.8 0.6 copy.36
  83.4 7.2 %collective-permute-done.4 = bf16[128,128]{1,0:T(8,128)(2,1)S(1)} collective-permute-done((bf16[128,128]{1,0:T(8,128)(2,1)S(1)}, bf16[128,128]{1,0:T(8,128)(2,1)S(1)}, u32[]{:S(2)}, u32[]{:S(2)}) %collective-permute-start.4) | collective-permute-done | bytes 32800 | tf_op jit(solution)/shard_map/ppermute | solution.py:231
  90.6 1.2 broadcast_in_dim.68
  91.9 8.9 %all-to-all-start.2 = ((bf16[32,128,128]{2,1,0:T(8,128)(2,1)}), bf16[32,128,128]{2,1,0:T(8,128)(2,1)S(1)}, u32[]{:S(2)}, u32[]{:S(2)}) async-start(bf16[32,128,128]{2,1,0:T(8,128)(2,1)} %bitcast.5), calls=%async_computation.2 | async-start | bytes 2097152 | tf_op jit(solution)/shard_map/all_to_all | solution.py:235
  100.8 0.6 iota_add_fusion.token_ref
  101.4 0.7 iota_add_fusion.1
  102.1 2.5 %collective-permute-start.5 = (bf16[128,128]{1,0:T(8,128)(2,1)S(1)}, bf16[128,128]{1,0:T(8,128)(2,1)S(1)}, u32[]{:S(2)}, u32[]{:S(2)}) collective-permute-start(bf16[128,128]{1,0:T(8,128)(2,1)S(1)} %get-tuple-element.20), channel_id=1, source_target_pairs={{0,2},{1,3},{2,0},{3,1},{4,6},{5,7},{6,4},{7,5},{8,10},{9,11},{10,... | collective-permute-start | bytes 98312 | tf_op jit(solution)/shard_map/ppermute | solution.py:236
  104.6 4.3 %collective-permute-start.6 = (bf16[128,128]{1,0:T(8,128)(2,1)S(1)}, bf16[128,128]{1,0:T(8,128)(2,1)S(1)}, u32[]{:S(2)}, u32[]{:S(2)}) collective-permute-start(bf16[128,128]{1,0:T(8,128)(2,1)S(1)} %get-tuple-element.20), channel_id=1, source_target_pairs={{0,1},{1,2},{2,3},{3,0},{4,5},{5,6},{6,7},{7,4},{8,9},{9,10},{10,1... | collective-permute-start | bytes 98312 | tf_op jit(solution)/shard_map/ppermute | solution.py:236
  108.8 1.9 %collective-permute-start.7 = (bf16[128,128]{1,0:T(8,128)(2,1)S(1)}, bf16[128,128]{1,0:T(8,128)(2,1)S(1)}, u32[]{:S(2)}, u32[]{:S(2)}) collective-permute-start(bf16[128,128]{1,0:T(8,128)(2,1)S(1)} %get-tuple-element.20), channel_id=1, source_target_pairs={{0,3},{1,0},{2,1},{3,2},{4,7},{5,4},{6,5},{7,6},{8,11},{9,8},{10,9... | collective-permute-start | bytes 98312 | tf_op jit(solution)/shard_map/ppermute | solution.py:236
  110.8 0.1 copy.24
  110.9 0.6 add_maximum_fusion.first_ref
  111.5 14.1 %collective-permute-done.5 = bf16[128,128]{1,0:T(8,128)(2,1)S(1)} collective-permute-done((bf16[128,128]{1,0:T(8,128)(2,1)S(1)}, bf16[128,128]{1,0:T(8,128)(2,1)S(1)}, u32[]{:S(2)}, u32[]{:S(2)}) %collective-permute-start.5) | collective-permute-done | bytes 32800 | tf_op jit(solution)/shard_map/ppermute | solution.py:236
  125.7 1.2 convolution_convert_fusion.5
  126.9 1.2 convolution_convert_fusion.6
  128.2 0.1 broadcast_select_fusion
  128.3 2.1 %collective-permute-start.8 = (bf16[8,4,128,128]{3,2,1,0:T(8,128)(2,1)S(1)}, bf16[8,4,128,128]{3,2,1,0:T(8,128)(2,1)S(1)}, u32[]{:S(2)}, u32[]{:S(2)}) collective-permute-start(bf16[8,4,128,128]{3,2,1,0:T(8,128)(2,1)S(1)} %broadcast_select_fusion), channel_id=1, source_target_pairs={{0,4},{4,0},{1,5},{5,1},{2,6},{6,2},{3,7},{7,3},{8,12},{12,8},{9,1... | collective-permute-start | bytes 3145736 | tf_op jit(solution)/shard_map/ppermute | solution.py:240
  130.4 0.5 convolution_convert_fusion.7
  130.9 0.5 convolution_convert_fusion.4
  131.4 0.4 copy-done.7
  131.9 0.9 pad_maximum_fusion.1.normed_ref
  132.8 4.1 %queries.1.queries_ref = bf16[128,512]{1,0:T(8,128)(2,1)} custom-call(bf16[128,2560]{1,0:T(8,128)(2,1)} %pad_maximum_fusion.1.normed_ref, f32[128,128]{1,0:T(8,128)} %get-tuple-element.45.cosine_ref, f32[128,128]{1,0:T(8,128)} %get-tuple-element.21.sine_ref, bf16[8,640,512]{2,1,0:T(8,128)(2,1)} %bitcast.45), custom_call_target="tpu_custom_call" | custom-call | tf_op jit(solution)/shard_map/queries/pallas_call | solution.py:255
  136.9 3.3 %near.1 = (f32[128,512]{1,0:T(8,128)}, f32[4,128,128]{2,1,0:T(8,128)}) custom-call(bf16[128,512]{1,0:T(8,128)(2,1)} %queries.1.queries_ref, bf16[8,4,128,128]{3,2,1,0:T(8,128)(2,1)} %bitcast.48, bf16[4,128,128]{2,1,0:T(8,128)(2,1)} %copy-done.2, s32[1,1152]{1,0:T(1,128)} %bitcast.59, s32[128,1]{1,0:T(8,128)} %iota_add_fusion.token_ref, ...), custom_call_target="tpu_custom_call" | custom-call | tf_op jit(solution)/shard_map/near/pallas_call | solution.py:266
  140.2 1.0 copy-done.3
  141.2 5.0 %attend.1 = bf16[4,128,640]{2,1,0:T(8,128)(2,1)} custom-call(bf16[128,512]{1,0:T(8,128)(2,1)} %queries.1.queries_ref, bf16[8,4,128,128]{3,2,1,0:T(8,128)(2,1)} %copy-done.3, s32[1,1024]{1,0:T(1,128)} %bitcast.60, s32[128,1]{1,0:T(8,128)} %iota_add_fusion.token_ref, s32[128,1]{1,0:T(8,128)} %add_maximum_fusion.first_ref, ...), custom_call_target="tpu_custom_call" | custom-call | tf_op jit(solution)/shard_map/attend/pallas_call | solution.py:276
  146.2 5.8 %all-to-all-start.3 = ((bf16[4,128,640]{2,1,0:T(8,128)(2,1)}), bf16[4,128,640]{2,1,0:T(8,128)(2,1)S(1)}, u32[]{:S(2)}, u32[]{:S(2)}) async-start(bf16[4,128,640]{2,1,0:T(8,128)(2,1)} %attend.1), calls=%async_computation.3 | async-start | bytes 1310720 | tf_op jit(solution)/shard_map/all_to_all | solution.py:285
  152.0 0.7 pad_maximum_fusion.5
  152.6 15.2 %all-to-all-done.3 = bf16[4,128,640]{2,1,0:T(8,128)(2,1)S(1)} async-done(((bf16[4,128,640]{2,1,0:T(8,128)(2,1)}), bf16[4,128,640]{2,1,0:T(8,128)(2,1)S(1)}, u32[]{:S(2)}, u32[]{:S(2)}) %all-to-all-start.3) | async-done | bytes 655392 | tf_op jit(solution)/shard_map/all_to_all | solution.py:285
  167.8 0.5 fusion.33
  168.3 0.5 convolution_add_fusion.2
  168.8 0.5 convolution_add_fusion.1
  169.3 1.1 fusion.32
  (65 shorter events, 1.1 us)
Async XLA Ops:
  7.2 19.0 %copy-start.6 = (bf16[128,640]{1,0:T(8,128)(2,1)S(1)}, bf16[128,640]{1,0:T(8,128)(2,1)}, u32[]{:S(2)}) copy-start(bf16[128,640]{1,0:T(8,128)(2,1)} %param.6) | copy-start | bytes 491524
  7.2 29.0 %copy-start.9 = (bf16[2560]{0:T(1024)(128)(2,1)S(1)}, bf16[2560]{0:T(1024)(128)(2,1)}, u32[]{:S(2)}) copy-start(bf16[2560]{0:T(1024)(128)(2,1)} %param.8) | copy-start | bytes 15364
  10.4 36.3 %all-to-all-start = ((bf16[16,48,512]{2,1,0:T(8,128)(2,1)}), bf16[16,48,512]{2,1,0:T(8,128)(2,1)S(1)}, u32[]{:S(2)}, u32[]{:S(2)}) async-start(bf16[16,48,512]{2,1,0:T(8,128)(2,1)} %broadcast_in_dim.55), calls=%async_computation | async-start | bytes 1572864 | tf_op jit(solution)/shard_map/all_to_all | solution.py:36
  26.1 106.7 %all-gather.3.cloned.1.call-start = ((), (), s32[]{:S(2)}) async-start(), calls=%async_computation.4 | async-start | bytes 5898240 | tf_op jit(solution)/shard_map/all_gather | solution.py:201
  26.2 22.0 %collective-permute-start = (bf16[128,640]{1,0:T(8,128)(2,1)S(1)}, bf16[128,640]{1,0:T(8,128)(2,1)S(1)}, u32[]{:S(2)}, u32[]{:S(2)}) collective-permute-start(bf16[128,640]{1,0:T(8,128)(2,1)S(1)} %copy-done.6), channel_id=1, source_target_pairs={{0,1},{1,2},{2,3},{3,0},{4,5},{5,6},{6,7},{7,4},{8,9},{9,10},{10,1... | collective-permute-start | bytes 491528 | tf_op jit(solution)/shard_map/ppermute | solution.py:190
  31.0 27.6 %collective-permute-start.1 = (bf16[128,640]{1,0:T(8,128)(2,1)S(1)}, bf16[128,640]{1,0:T(8,128)(2,1)S(1)}, u32[]{:S(2)}, u32[]{:S(2)}) collective-permute-start(bf16[128,640]{1,0:T(8,128)(2,1)S(1)} %copy-done.6), channel_id=1, source_target_pairs={{0,2},{1,3},{2,0},{3,1},{4,6},{5,7},{6,4},{7,5},{8,10},{9,11},{10,... | collective-permute-start | bytes 491528 | tf_op jit(solution)/shard_map/ppermute | solution.py:190
  33.0 25.7 %collective-permute-start.2 = (bf16[128,640]{1,0:T(8,128)(2,1)S(1)}, bf16[128,640]{1,0:T(8,128)(2,1)S(1)}, u32[]{:S(2)}, u32[]{:S(2)}) collective-permute-start(bf16[128,640]{1,0:T(8,128)(2,1)S(1)} %copy-done.6), channel_id=1, source_target_pairs={{0,3},{1,0},{2,1},{3,2},{4,7},{5,4},{6,5},{7,6},{8,11},{9,8},{10,9... | collective-permute-start | bytes 491528 | tf_op jit(solution)/shard_map/ppermute | solution.py:190
  47.1 0.8 copy-start.1
  59.9 15.3 %all-to-all-start.1 = ((bf16[4,16,24,128]{3,2,1,0:T(8,128)(2,1)}), bf16[4,16,24,128]{3,2,1,0:T(8,128)(2,1)S(1)}, u32[]{:S(2)}, u32[]{:S(2)}) async-start(bf16[4,16,24,128]{3,2,1,0:T(8,128)(2,1)} %broadcast_in_dim.57), calls=%async_computation.1 | async-start | bytes 786432 | tf_op jit(solution)/shard_map/all_to_all | solution.py:36
  64.4 62.5 %copy-start.4 = (bf16[128,2560]{1,0:T(8,128)(2,1)}, bf16[128,2560]{1,0:T(8,128)(2,1)S(1)}, u32[]{:S(2)}) copy-start(bf16[128,2560]{1,0:T(8,128)(2,1)S(1)} %fusion.30) | copy-start | bytes 1966084
  67.7 11.6 %copy-start.10 = (s32[128]{0:T(128)S(1)}, s32[128]{0:T(128)}, u32[]{:S(2)}) copy-start(s32[128]{0:T(128)} %param.7) | copy-start | bytes 1540
  75.2 3.7 %collective-permute-start.3 = (bf16[4,16,24,128]{3,2,1,0:T(8,128)(2,1)S(1)}, bf16[4,16,24,128]{3,2,1,0:T(8,128)(2,1)S(1)}, u32[]{:S(2)}, u32[]{:S(2)}) collective-permute-start(bf16[4,16,24,128]{3,2,1,0:T(8,128)(2,1)S(1)} %all-to-all-done.1), channel_id=1, source_target_pairs={{0,4},{4,0},{1,5},{5,1},{2,6},{6,2},{3,7},{7,3},{8,12},{12,8},{9,1... | collective-permute-start | bytes 1179656 | tf_op jit(solution)/shard_map/ppermute | solution.py:196
  80.8 9.7 %collective-permute-start.4 = (bf16[128,128]{1,0:T(8,128)(2,1)S(1)}, bf16[128,128]{1,0:T(8,128)(2,1)S(1)}, u32[]{:S(2)}, u32[]{:S(2)}) collective-permute-start(bf16[128,128]{1,0:T(8,128)(2,1)S(1)} %get-tuple-element.20), channel_id=1, source_target_pairs={{0,64},{4,68},{8,72},{12,76},{16,80},{20,84},{24,88},{28,92},{32,9... | collective-permute-start | bytes 98312 | tf_op jit(solution)/shard_map/ppermute | solution.py:231
  91.9 36.3 %all-to-all-start.2 = ((bf16[32,128,128]{2,1,0:T(8,128)(2,1)}), bf16[32,128,128]{2,1,0:T(8,128)(2,1)S(1)}, u32[]{:S(2)}, u32[]{:S(2)}) async-start(bf16[32,128,128]{2,1,0:T(8,128)(2,1)} %bitcast.5), calls=%async_computation.2 | async-start | bytes 2097152 | tf_op jit(solution)/shard_map/all_to_all | solution.py:235
  102.1 23.6 %collective-permute-start.5 = (bf16[128,128]{1,0:T(8,128)(2,1)S(1)}, bf16[128,128]{1,0:T(8,128)(2,1)S(1)}, u32[]{:S(2)}, u32[]{:S(2)}) collective-permute-start(bf16[128,128]{1,0:T(8,128)(2,1)S(1)} %get-tuple-element.20), channel_id=1, source_target_pairs={{0,2},{1,3},{2,0},{3,1},{4,6},{5,7},{6,4},{7,5},{8,10},{9,11},{10,... | collective-permute-start | bytes 98312 | tf_op jit(solution)/shard_map/ppermute | solution.py:236
  104.6 21.1 %collective-permute-start.6 = (bf16[128,128]{1,0:T(8,128)(2,1)S(1)}, bf16[128,128]{1,0:T(8,128)(2,1)S(1)}, u32[]{:S(2)}, u32[]{:S(2)}) collective-permute-start(bf16[128,128]{1,0:T(8,128)(2,1)S(1)} %get-tuple-element.20), channel_id=1, source_target_pairs={{0,1},{1,2},{2,3},{3,0},{4,5},{5,6},{6,7},{7,4},{8,9},{9,10},{10,1... | collective-permute-start | bytes 98312 | tf_op jit(solution)/shard_map/ppermute | solution.py:236
  108.8 16.8 %collective-permute-start.7 = (bf16[128,128]{1,0:T(8,128)(2,1)S(1)}, bf16[128,128]{1,0:T(8,128)(2,1)S(1)}, u32[]{:S(2)}, u32[]{:S(2)}) collective-permute-start(bf16[128,128]{1,0:T(8,128)(2,1)S(1)} %get-tuple-element.20), channel_id=1, source_target_pairs={{0,3},{1,0},{2,1},{3,2},{4,7},{5,4},{6,5},{7,6},{8,11},{9,8},{10,9... | collective-permute-start | bytes 98312 | tf_op jit(solution)/shard_map/ppermute | solution.py:236
  125.7 2.4 %copy-start.2 = (bf16[4,128,128]{2,1,0:T(8,128)(2,1)}, bf16[4,128,128]{2,1,0:T(8,128)(2,1)S(1)}, u32[]{:S(2)}) copy-start(bf16[4,128,128]{2,1,0:T(8,128)(2,1)S(1)} %pad_maximum_fusion.4.own_ref) | copy-start | bytes 393220
  128.2 2.7 %copy-start = (bf16[32,128,128]{2,1,0:T(8,128)(2,1)}, bf16[32,128,128]{2,1,0:T(8,128)(2,1)S(1)}, u32[]{:S(2)}) copy-start(bf16[32,128,128]{2,1,0:T(8,128)(2,1)S(1)} %all-to-all-done.2) | copy-start | bytes 3145732
  128.2 2.2 %copy-start.5 = (bf16[128,2560]{1,0:T(8,128)(2,1)S(1)}, bf16[128,2560]{1,0:T(8,128)(2,1)}, u32[]{:S(2)}) copy-start(bf16[128,2560]{1,0:T(8,128)(2,1)} %copy-done.4) | copy-start | bytes 1966084
  128.3 11.9 %collective-permute-start.8 = (bf16[8,4,128,128]{3,2,1,0:T(8,128)(2,1)S(1)}, bf16[8,4,128,128]{3,2,1,0:T(8,128)(2,1)S(1)}, u32[]{:S(2)}, u32[]{:S(2)}) collective-permute-start(bf16[8,4,128,128]{3,2,1,0:T(8,128)(2,1)S(1)} %broadcast_select_fusion), channel_id=1, source_target_pairs={{0,4},{4,0},{1,5},{5,1},{2,6},{6,2},{3,7},{7,3},{8,12},{12,8},{9,1... | collective-permute-start | bytes 3145736 | tf_op jit(solution)/shard_map/ppermute | solution.py:240
  130.9 0.9 copy-start.7
  130.9 1.0 copy-start.8
  140.2 1.0 copy-start.3
  146.2 21.7 %all-to-all-start.3 = ((bf16[4,128,640]{2,1,0:T(8,128)(2,1)}), bf16[4,128,640]{2,1,0:T(8,128)(2,1)S(1)}, u32[]{:S(2)}, u32[]{:S(2)}) async-start(bf16[4,128,640]{2,1,0:T(8,128)(2,1)} %attend.1), calls=%async_computation.3 | async-start | bytes 1310720 | tf_op jit(solution)/shard_map/all_to_all | solution.py:285
Sparse Core Ops, SparseCore 0:
  48.1 46.9 all-gather.2

commit v11 on v8

--- a/solution.py
+++ b/solution.py
@@ -68,6 +68,10 @@
         ],
         axis=1,
     )
+
+
+def on_core(value):
+    return pltpu.with_memory_space_constraint(value, pltpu.VMEM)
 
 
 def fetch(qo_ref, at, weights_ref, sems):
@@ -222,7 +226,7 @@
         out_specs=vmem,
         scratch_shapes=scratch,
         name="queries",
-    )(reordered, cosine, sine, qo_all)
+    )(*(on_core(a) for a in (reordered, cosine, sine)), qo_all)
     reach_back = jnp.maximum(own_start, token_index - (WINDOW - 1))
     partial = pl.pallas_call(
         attend_kernel,
@@ -231,7 +235,10 @@
         out_specs=vmem,
         scratch_shapes=scratch,
         name="attend",
-    )(queries, mine, partner, own_kv, keys_at, token_index[:, None], reach_back[:, None], qo_all)
+    )(
+        *(on_core(a) for a in (queries, mine, partner, own_kv, keys_at, token_index[:, None], reach_back[:, None])),
+        qo_all,
+    )
 
     received = lax.all_to_all(partial, "tp", 0, 0, tiled=True)
     summed = jnp.zeros((tok, shard), jnp.float32)

time: 183 us -> 181 us (0.989)
  waiting for transfers between devices: 78.4 us -> 81.1 us
  transfers between devices with their start and end apart: 13 -> 13, of which waited for: 6 -> 6; matrix products, arithmetic and copies ran while one was open for 10% -> 9% of each run, Pallas kernels for 2% -> 2%
where the time goes in v11:
time: 181 us; the launch traced here: 180 us
  waiting for transfers between devices  81.1 us (45%)
  starting transfers between devices  55 us (30%)
  between operations  14.6 us (8%)
  matrix products  9.41 us (5%)
  Pallas kernels  8.23 us (5%)
  other arithmetic  6.96 us (4%)
  local copies, waits for them, and re-layouts  5.09 us (3%)
    all_to_all x2, waiting for transfers between devices, spread(): return lax.all_to_all(copies, axes, 0, 0, tiled=True)  40.5 us
    all_to_all x2, starting transfers between devices, spread(): return lax.all_to_all(copies, axes, 0, 0, tiled=True)  18.7 us
    all_to_all x1, waiting for transfers between devices, per_device(): received = lax.all_to_all(partial, 'tp', 0, 0, tiled=True)  17.5 us
    ppermute x3, waiting for transfers between devices, per_device(): lax.ppermute(kv_share, 'tp', [(i, (i + k) % nx) for i in range(nx)])  13.2 us
    ppermute x3, starting transfers between devices, per_device(): lax.ppermute(tokens, 'tp', [(i, (i + k) % nx) for i in range(nx)])  12.3 us
    ppermute x3, starting transfers between devices, per_device(): lax.ppermute(kv_share, 'tp', [(i, (i + k) % nx) for i in range(nx)])  12.2 us
    ppermute x1, waiting for transfers between devices, per_device(): lax.ppermute(kv_share, SEQ, [(i, i + block) for i in range(devices - bloc...  8.75 us
    dot_general x8, matrix products, turned(): jnp.dot(values[:, g:g + per], hot, preferred_element_type=jnp.float32)  6.52 us
  transfers between devices with their start and end apart: 13, of which 6 were waited for; matrix products, arithmetic and copies ran while one was open for 9% of the time, Pallas kernels for 2%

profile of v11, /device:TPU:2, one launch (start us, length us, event | category | flops | bytes accessed | tf_op | source)
XLA Modules:
  0.0 180.4 jit_solution(10425045441703068134)
XLA Ops:
  7.2 4.6 %collective-permute-start = (bf16[128,640]{1,0:T(8,128)(2,1)}, bf16[128,640]{1,0:T(8,128)(2,1)S(1)}, u32[]{:S(2)}, u32[]{:S(2)}) collective-permute-start(bf16[128,640]{1,0:T(8,128)(2,1)} %param.6), channel_id=1, source_target_pairs={{0,2},{1,3},{2,0},{3,1},{4,6},{5,7},{6,4},{7,5},{8,10},{9,11},{10,... | collective-permute-start | bytes 491528 | tf_op jit(solution)/shard_map/ppermute | solution.py:167
  11.8 3.5 %collective-permute-start.1 = (bf16[128,640]{1,0:T(8,128)(2,1)}, bf16[128,640]{1,0:T(8,128)(2,1)S(1)}, u32[]{:S(2)}, u32[]{:S(2)}) collective-permute-start(bf16[128,640]{1,0:T(8,128)(2,1)} %param.6), channel_id=1, source_target_pairs={{0,1},{1,2},{2,3},{3,0},{4,5},{5,6},{6,7},{7,4},{8,9},{9,10},{10,1... | collective-permute-start | bytes 491528 | tf_op jit(solution)/shard_map/ppermute | solution.py:167
  15.3 4.2 %collective-permute-start.2 = (bf16[128,640]{1,0:T(8,128)(2,1)}, bf16[128,640]{1,0:T(8,128)(2,1)S(1)}, u32[]{:S(2)}, u32[]{:S(2)}) collective-permute-start(bf16[128,640]{1,0:T(8,128)(2,1)} %param.6), channel_id=1, source_target_pairs={{0,3},{1,0},{2,1},{3,2},{4,7},{5,4},{6,5},{7,6},{8,11},{9,8},{10,9... | collective-permute-start | bytes 491528 | tf_op jit(solution)/shard_map/ppermute | solution.py:167
  19.5 0.7 convert_bitcast_fusion
  20.1 0.7 select_select_fusion.8
  20.9 0.8 maximum_maximum_fusion
  21.7 1.0 broadcast_in_dim.56
  22.7 13.9 %all-to-all-start = ((bf16[16,48,512]{2,1,0:T(8,128)(2,1)}), bf16[16,48,512]{2,1,0:T(8,128)(2,1)S(1)}, u32[]{:S(2)}, u32[]{:S(2)}) async-start(bf16[16,48,512]{2,1,0:T(8,128)(2,1)} %broadcast_in_dim.56), calls=%async_computation | async-start | bytes 1572864 | tf_op jit(solution)/shard_map/all_to_all | solution.py:36
  36.6 0.0 all-gather.3.cloned.1.call-start
  36.7 0.1 pad_add_fusion
  36.8 0.1 add_bitcast_fusion
  37.0 0.1 select_select_fusion.3
  37.2 0.2 fusion.28
  37.4 22.9 %all-to-all-done = bf16[16,48,512]{2,1,0:T(8,128)(2,1)S(1)} async-done(((bf16[16,48,512]{2,1,0:T(8,128)(2,1)}), bf16[16,48,512]{2,1,0:T(8,128)(2,1)S(1)}, u32[]{:S(2)}, u32[]{:S(2)}) %all-to-all-start) | async-done | bytes 786464 | tf_op jit(solution)/shard_map/all_to_all | solution.py:36
  60.3 0.1 fusion.79
  60.5 0.1 reshape.112
  60.5 0.1 reshape.111
  60.6 0.9 pad_maximum_fusion.3
  61.5 0.2 fusion.30
  61.8 0.8 convolution_convert_fusion
  62.6 0.8 convolution_convert_fusion.1
  63.4 0.8 convolution_convert_fusion.2
  64.2 1.0 broadcast_in_dim.57
  65.2 4.8 %all-to-all-start.1 = ((bf16[8,16,24,128]{3,2,1,0:T(8,128)(2,1)}), bf16[8,16,24,128]{3,2,1,0:T(8,128)(2,1)S(1)}, u32[]{:S(2)}, u32[]{:S(2)}) async-start(bf16[8,16,24,128]{3,2,1,0:T(8,128)(2,1)} %broadcast_in_dim.57), calls=%async_computation.1 | async-start | bytes 1572864 | tf_op jit(solution)/shard_map/all_to_all | solution.py:36
  70.0 0.8 convolution_convert_fusion.3
  70.8 0.1 pad_maximum_fusion
  70.9 17.5 %all-to-all-done.1 = bf16[8,16,24,128]{3,2,1,0:T(8,128)(2,1)S(1)} async-done(((bf16[8,16,24,128]{3,2,1,0:T(8,128)(2,1)}), bf16[8,16,24,128]{3,2,1,0:T(8,128)(2,1)S(1)}, u32[]{:S(2)}, u32[]{:S(2)}) %all-to-all-start.1) | async-done | bytes 786464 | tf_op jit(solution)/shard_map/all_to_all | solution.py:36
  88.5 0.1 slice_convert_fusion
  88.6 0.3 convert_reduce_fusion
  88.9 0.1 select_reduce_fusion
  89.0 0.4 fusion.83
  89.4 0.1 fusion.81
  89.4 0.3 fusion.45
  89.8 0.1 fusion.44
  89.9 1.9 %collective-permute-start.3 = (bf16[128,128]{1,0:T(8,128)(2,1)S(1)}, bf16[128,128]{1,0:T(8,128)(2,1)S(1)}, u32[]{:S(2)}, u32[]{:S(2)}) collective-permute-start(bf16[128,128]{1,0:T(8,128)(2,1)S(1)} %get-tuple-element.8), channel_id=1, source_target_pairs={{0,64},{4,68},{8,72},{12,76},{16,80},{20,84},{24,88},{28,92},{32,9... | collective-permute-start | bytes 98312 | tf_op jit(solution)/shard_map/ppermute | solution.py:200
  91.8 8.8 %collective-permute-done.3 = bf16[128,128]{1,0:T(8,128)(2,1)S(1)} collective-permute-done((bf16[128,128]{1,0:T(8,128)(2,1)S(1)}, bf16[128,128]{1,0:T(8,128)(2,1)S(1)}, u32[]{:S(2)}, u32[]{:S(2)}) %collective-permute-start.3) | collective-permute-done | bytes 32800 | tf_op jit(solution)/shard_map/ppermute | solution.py:200
  100.6 0.1 broadcast_select_fusion.1
  100.7 1.2 broadcast_in_dim.68
  101.9 4.4 %all-to-all-start.2 = ((bf16[32,128,128]{2,1,0:T(8,128)(2,1)}), bf16[32,128,128]{2,1,0:T(8,128)(2,1)S(1)}, u32[]{:S(2)}, u32[]{:S(2)}) async-start(bf16[32,128,128]{2,1,0:T(8,128)(2,1)} %bitcast.4), calls=%async_computation.2 | async-start | bytes 2097152 | tf_op jit(solution)/shard_map/all_to_all | solution.py:204
  106.4 4.6 %collective-permute-start.4 = (bf16[128,128]{1,0:T(8,128)(2,1)S(1)}, bf16[128,128]{1,0:T(8,128)(2,1)S(1)}, u32[]{:S(2)}, u32[]{:S(2)}) collective-permute-start(bf16[128,128]{1,0:T(8,128)(2,1)S(1)} %get-tuple-element.8), channel_id=1, source_target_pairs={{0,2},{1,3},{2,0},{3,1},{4,6},{5,7},{6,4},{7,5},{8,10},{9,11},{10,... | collective-permute-start | bytes 98312 | tf_op jit(solution)/shard_map/ppermute | solution.py:205
  111.0 3.4 %collective-permute-start.5 = (bf16[128,128]{1,0:T(8,128)(2,1)S(1)}, bf16[128,128]{1,0:T(8,128)(2,1)S(1)}, u32[]{:S(2)}, u32[]{:S(2)}) collective-permute-start(bf16[128,128]{1,0:T(8,128)(2,1)S(1)} %get-tuple-element.8), channel_id=1, source_target_pairs={{0,1},{1,2},{2,3},{3,0},{4,5},{5,6},{6,7},{7,4},{8,9},{9,10},{10,1... | collective-permute-start | bytes 98312 | tf_op jit(solution)/shard_map/ppermute | solution.py:205
  114.4 4.3 %collective-permute-start.6 = (bf16[128,128]{1,0:T(8,128)(2,1)S(1)}, bf16[128,128]{1,0:T(8,128)(2,1)S(1)}, u32[]{:S(2)}, u32[]{:S(2)}) collective-permute-start(bf16[128,128]{1,0:T(8,128)(2,1)S(1)} %get-tuple-element.8), channel_id=1, source_target_pairs={{0,3},{1,0},{2,1},{3,2},{4,7},{5,4},{6,5},{7,6},{8,11},{9,8},{10,9... | collective-permute-start | bytes 98312 | tf_op jit(solution)/shard_map/ppermute | solution.py:205
  118.6 0.1 copy.28
  118.8 13.2 %collective-permute-done.4 = bf16[128,128]{1,0:T(8,128)(2,1)S(1)} collective-permute-done((bf16[128,128]{1,0:T(8,128)(2,1)S(1)}, bf16[128,128]{1,0:T(8,128)(2,1)S(1)}, u32[]{:S(2)}, u32[]{:S(2)}) %collective-permute-start.4) | collective-permute-done | bytes 32800 | tf_op jit(solution)/shard_map/ppermute | solution.py:205
  132.0 1.2 convolution_convert_fusion.4
  133.2 1.2 convolution_convert_fusion.5
  134.4 1.1 all-to-all-done.2
  135.5 1.1 broadcast_select_fusion
  136.6 1.9 %collective-permute-start.7 = (bf16[8,4,128,128]{3,2,1,0:T(8,128)(2,1)}, bf16[8,4,128,128]{3,2,1,0:T(8,128)(2,1)S(1)}, u32[]{:S(2)}, u32[]{:S(2)}) collective-permute-start(bf16[8,4,128,128]{3,2,1,0:T(8,128)(2,1)} %broadcast_select_fusion), channel_id=1, source_target_pairs={{0,4},{4,0},{1,5},{5,1},{2,6},{6,2},{3,7},{7,3},{8,12},{12,8},{9,1... | collective-permute-start | bytes 3145736 | tf_op jit(solution)/shard_map/ppermute | solution.py:209
  138.5 0.5 convolution_convert_fusion.6
  139.0 0.5 convolution_convert_fusion.7
  139.5 0.4 copy-done.2
  139.9 0.1 copy-done.3
  140.1 0.0 all-gather.3.cloned.1.call-done
  140.1 3.0 %queries.1.queries_ref = bf16[128,512]{1,0:T(8,128)(2,1)} custom-call(bf16[128,2560]{1,0:T(8,128)(2,1)S(1)} %pad_maximum_fusion.2.normed_ref, f32[128,128]{1,0:T(8,128)S(1)} %get-tuple-element.23.cosine_ref, f32[128,128]{1,0:T(8,128)S(1)} %get-tuple-element.9.sine_ref, bf16[8,640,512]{2,1,0:T(8,128)(2,1)} %bitcast.37), custom_call_target="tpu_custom_call" | custom-call | tf_op jit(solution)/shard_map/queries/pallas_call | solution.py:222
  143.1 0.9 copy-done
  144.0 5.2 %attend.1 = bf16[4,128,640]{2,1,0:T(8,128)(2,1)} custom-call(bf16[128,512]{1,0:T(8,128)(2,1)S(1)} %copy-done, bf16[8,4,128,128]{3,2,1,0:T(8,128)(2,1)S(1)} %bitcast.35, bf16[8,4,128,128]{3,2,1,0:T(8,128)(2,1)S(1)} %collective-permute-done.7.partner_ref, bf16[4,128,128]{2,1,0:T(8,128)(2,1)S(1)} %pad_maximum_fusion.4.own_ref, s32[1,2176]{1,0:T(1,128)S(1)} %bitcast.36, ...), custom_call_target="tpu_custom_call" | custom-call | tf_op jit(solution)/shard_map/attend/pallas_call | solution.py:231
  149.3 3.5 %all-to-all-start.3 = ((bf16[4,128,640]{2,1,0:T(8,128)(2,1)}), bf16[4,128,640]{2,1,0:T(8,128)(2,1)S(1)}, u32[]{:S(2)}, u32[]{:S(2)}) async-start(bf16[4,128,640]{2,1,0:T(8,128)(2,1)} %attend.1), calls=%async_computation.3 | async-start | bytes 1310720 | tf_op jit(solution)/shard_map/all_to_all | solution.py:243
  152.8 0.7 pad_maximum_fusion.5
  153.4 17.5 %all-to-all-done.3 = bf16[4,128,640]{2,1,0:T(8,128)(2,1)S(1)} async-done(((bf16[4,128,640]{2,1,0:T(8,128)(2,1)}), bf16[4,128,640]{2,1,0:T(8,128)(2,1)S(1)}, u32[]{:S(2)}, u32[]{:S(2)}) %all-to-all-start.3) | async-done | bytes 655392 | tf_op jit(solution)/shard_map/all_to_all | solution.py:243
  171.0 0.5 fusion.33
  171.4 0.5 convolution_add_fusion.2
  171.9 0.5 convolution_add_fusion.1
  172.4 1.1 fusion.32
  (40 shorter events, 0.4 us)
Async XLA Ops:
  7.2 29.9 %copy-start.1 = (bf16[128,640]{1,0:T(8,128)(2,1)S(1)}, bf16[128,640]{1,0:T(8,128)(2,1)}, u32[]{:S(2)}) copy-start(bf16[128,640]{1,0:T(8,128)(2,1)} %param.6) | copy-start | bytes 491524
  7.2 29.8 %copy-start.4 = (bf16[2560]{0:T(1024)(128)(2,1)S(1)}, bf16[2560]{0:T(1024)(128)(2,1)}, u32[]{:S(2)}) copy-start(bf16[2560]{0:T(1024)(128)(2,1)} %param.8) | copy-start | bytes 15364
  7.2 29.8 %collective-permute-start = (bf16[128,640]{1,0:T(8,128)(2,1)}, bf16[128,640]{1,0:T(8,128)(2,1)S(1)}, u32[]{:S(2)}, u32[]{:S(2)}) collective-permute-start(bf16[128,640]{1,0:T(8,128)(2,1)} %param.6), channel_id=1, source_target_pairs={{0,2},{1,3},{2,0},{3,1},{4,6},{5,7},{6,4},{7,5},{8,10},{9,11},{10,... | collective-permute-start | bytes 491528 | tf_op jit(solution)/shard_map/ppermute | solution.py:167
  11.8 25.2 %collective-permute-start.1 = (bf16[128,640]{1,0:T(8,128)(2,1)}, bf16[128,640]{1,0:T(8,128)(2,1)S(1)}, u32[]{:S(2)}, u32[]{:S(2)}) collective-permute-start(bf16[128,640]{1,0:T(8,128)(2,1)} %param.6), channel_id=1, source_target_pairs={{0,1},{1,2},{2,3},{3,0},{4,5},{5,6},{6,7},{7,4},{8,9},{9,10},{10,1... | collective-permute-start | bytes 491528 | tf_op jit(solution)/shard_map/ppermute | solution.py:167
  15.3 21.7 %collective-permute-start.2 = (bf16[128,640]{1,0:T(8,128)(2,1)}, bf16[128,640]{1,0:T(8,128)(2,1)S(1)}, u32[]{:S(2)}, u32[]{:S(2)}) collective-permute-start(bf16[128,640]{1,0:T(8,128)(2,1)} %param.6), channel_id=1, source_target_pairs={{0,3},{1,0},{2,1},{3,2},{4,7},{5,4},{6,5},{7,6},{8,11},{9,8},{10,9... | collective-permute-start | bytes 491528 | tf_op jit(solution)/shard_map/ppermute | solution.py:167
  22.7 37.6 %all-to-all-start = ((bf16[16,48,512]{2,1,0:T(8,128)(2,1)}), bf16[16,48,512]{2,1,0:T(8,128)(2,1)S(1)}, u32[]{:S(2)}, u32[]{:S(2)}) async-start(bf16[16,48,512]{2,1,0:T(8,128)(2,1)} %broadcast_in_dim.56), calls=%async_computation | async-start | bytes 1572864 | tf_op jit(solution)/shard_map/all_to_all | solution.py:36
  36.6 103.5 %all-gather.3.cloned.1.call-start = ((), (), s32[]{:S(2)}) async-start(), calls=%async_computation.4 | async-start | bytes 5898240 | tf_op jit(solution)/shard_map/all_gather | solution.py:177
  65.2 23.2 %all-to-all-start.1 = ((bf16[8,16,24,128]{3,2,1,0:T(8,128)(2,1)}), bf16[8,16,24,128]{3,2,1,0:T(8,128)(2,1)S(1)}, u32[]{:S(2)}, u32[]{:S(2)}) async-start(bf16[8,16,24,128]{3,2,1,0:T(8,128)(2,1)} %broadcast_in_dim.57), calls=%async_computation.1 | async-start | bytes 1572864 | tf_op jit(solution)/shard_map/all_to_all | solution.py:36
  70.8 18.1 %copy-start.5 = (s32[128]{0:T(128)S(1)}, s32[128]{0:T(128)}, u32[]{:S(2)}) copy-start(s32[128]{0:T(128)} %param.7) | copy-start | bytes 1540
  89.9 10.7 %collective-permute-start.3 = (bf16[128,128]{1,0:T(8,128)(2,1)S(1)}, bf16[128,128]{1,0:T(8,128)(2,1)S(1)}, u32[]{:S(2)}, u32[]{:S(2)}) collective-permute-start(bf16[128,128]{1,0:T(8,128)(2,1)S(1)} %get-tuple-element.8), channel_id=1, source_target_pairs={{0,64},{4,68},{8,72},{12,76},{16,80},{20,84},{24,88},{28,92},{32,9... | collective-permute-start | bytes 98312 | tf_op jit(solution)/shard_map/ppermute | solution.py:200
  101.9 33.5 %all-to-all-start.2 = ((bf16[32,128,128]{2,1,0:T(8,128)(2,1)}), bf16[32,128,128]{2,1,0:T(8,128)(2,1)S(1)}, u32[]{:S(2)}, u32[]{:S(2)}) async-start(bf16[32,128,128]{2,1,0:T(8,128)(2,1)} %bitcast.4), calls=%async_computation.2 | async-start | bytes 2097152 | tf_op jit(solution)/shard_map/all_to_all | solution.py:204
  106.4 25.6 %collective-permute-start.4 = (bf16[128,128]{1,0:T(8,128)(2,1)S(1)}, bf16[128,128]{1,0:T(8,128)(2,1)S(1)}, u32[]{:S(2)}, u32[]{:S(2)}) collective-permute-start(bf16[128,128]{1,0:T(8,128)(2,1)S(1)} %get-tuple-element.8), channel_id=1, source_target_pairs={{0,2},{1,3},{2,0},{3,1},{4,6},{5,7},{6,4},{7,5},{8,10},{9,11},{10,... | collective-permute-start | bytes 98312 | tf_op jit(solution)/shard_map/ppermute | solution.py:205
  111.0 21.0 %collective-permute-start.5 = (bf16[128,128]{1,0:T(8,128)(2,1)S(1)}, bf16[128,128]{1,0:T(8,128)(2,1)S(1)}, u32[]{:S(2)}, u32[]{:S(2)}) collective-permute-start(bf16[128,128]{1,0:T(8,128)(2,1)S(1)} %get-tuple-element.8), channel_id=1, source_target_pairs={{0,1},{1,2},{2,3},{3,0},{4,5},{5,6},{6,7},{7,4},{8,9},{9,10},{10,1... | collective-permute-start | bytes 98312 | tf_op jit(solution)/shard_map/ppermute | solution.py:205
  114.4 17.6 %collective-permute-start.6 = (bf16[128,128]{1,0:T(8,128)(2,1)S(1)}, bf16[128,128]{1,0:T(8,128)(2,1)S(1)}, u32[]{:S(2)}, u32[]{:S(2)}) collective-permute-start(bf16[128,128]{1,0:T(8,128)(2,1)S(1)} %get-tuple-element.8), channel_id=1, source_target_pairs={{0,3},{1,0},{2,1},{3,2},{4,7},{5,4},{6,5},{7,6},{8,11},{9,8},{10,9... | collective-permute-start | bytes 98312 | tf_op jit(solution)/shard_map/ppermute | solution.py:205
  136.6 6.5 %collective-permute-start.7 = (bf16[8,4,128,128]{3,2,1,0:T(8,128)(2,1)}, bf16[8,4,128,128]{3,2,1,0:T(8,128)(2,1)S(1)}, u32[]{:S(2)}, u32[]{:S(2)}) collective-permute-start(bf16[8,4,128,128]{3,2,1,0:T(8,128)(2,1)} %broadcast_select_fusion), channel_id=1, source_target_pairs={{0,4},{4,0},{1,5},{5,1},{2,6},{6,2},{3,7},{7,3},{8,12},{12,8},{9,1... | collective-permute-start | bytes 3145736 | tf_op jit(solution)/shard_map/ppermute | solution.py:209
  139.0 0.9 copy-start.2
  139.0 1.0 copy-start.3
  143.1 0.9 copy-start
  149.3 21.7 %all-to-all-start.3 = ((bf16[4,128,640]{2,1,0:T(8,128)(2,1)}), bf16[4,128,640]{2,1,0:T(8,128)(2,1)S(1)}, u32[]{:S(2)}, u32[]{:S(2)}) async-start(bf16[4,128,640]{2,1,0:T(8,128)(2,1)} %attend.1), calls=%async_computation.3 | async-start | bytes 1310720 | tf_op jit(solution)/shard_map/all_to_all | solution.py:243
Sparse Core Ops, SparseCore 0:
  61.7 42.0 all-gather.2
